TPU v7x, 32 devices: a whole 2x2x4 slice. The times are simulated.
32 devices in a mesh: shard: 4 (over y, x), ctx: 4 (over z), tensor: 2 (over core).
Axes of the slice: x: 2, y: 2, z: 4, core: 2. Of those that a mesh axis runs over, the one named last changes fastest.
Arguments:
- streams: bfloat16 [2048, 4, 2048], P(('shard', 'ctx')), may hold values from -6 to 6
- lengths: int32 [4, 4], P('shard'), may hold values from 1 to 384, 512 in all within a row
- destination: int32 [2048], P(('shard', 'ctx')), may hold values from 0 to 2047, as said below
- w_query: bfloat16 [2048, 2048], P('shard', 'tensor'), may hold values from -0.125 to 0.125
- w_key: bfloat16 [2048, 2048], P('shard', 'tensor'), may hold values from -0.125 to 0.125
- w_value: bfloat16 [2048, 2048], P('shard', 'tensor'), may hold values from -0.125 to 0.125
- w_output: bfloat16 [2048, 2048], P('tensor', 'shard'), may hold values from -1.5 to 1.5
- w_gate: bfloat16 [2048, 8192], P('shard', 'tensor'), may hold values from -0.125 to 0.125
- w_up: bfloat16 [2048, 8192], P('shard', 'tensor'), may hold values from -0.125 to 0.125
- w_down: bfloat16 [8192, 2048], P('tensor', 'shard'), may hold values from -0.0625 to 0.0625
- mix_weight: float32 [2, 2048, 6], replicated, may hold values from -0.125 to 0.125
- mix_static: float32 [2, 4, 6], replicated, may hold values from -3 to 3
- cotangent: bfloat16 [2048, 4, 2048], P(('shard', 'ctx')), may hold values from -6 to 6
Outputs:
- streams_out: bfloat16 [2048, 4, 2048], P(('shard', 'ctx'))
- grad_streams: bfloat16 [2048, 4, 2048], P(('shard', 'ctx'))
- grad_query: float32 [2048, 2048], P(('shard', 'ctx'), 'tensor')
- grad_key: float32 [2048, 2048], P(('shard', 'ctx'), 'tensor')
- grad_value: float32 [2048, 2048], P(('shard', 'ctx'), 'tensor')
- grad_output: float32 [2048, 2048], P('tensor', ('shard', 'ctx'))
- grad_gate: float32 [2048, 8192], P(('shard', 'ctx'), 'tensor')
- grad_up: float32 [2048, 8192], P(('shard', 'ctx'), 'tensor')
- grad_down: float32 [8192, 2048], P('tensor', ('shard', 'ctx'))
- grad_mix_weight: float32 [2, 2048, 6], replicated
- grad_mix_static: float32 [2, 4, 6], replicated
Inputs may be any that keep to these rules, and one draw needn't show every extreme that they name: `lengths`: each row sums to 512 and its largest entry is 384. `destination`: A permutation that keeps every group of 512 consecutive indices within itself; the 128 tokens of each aligned block of 128 indices send exactly 32 tokens to each aligned block of 128 slots of their group, as 32 consecutive tokens to 32 consecutive slots in the same order.
All inputs are finite; a program needn't handle non-finite values.
Results may differ from a plain program's by a relative error of at most 0.02.
The roundings to bfloat16 on the way count: a program that leaves them out, or rounds other values in their place, can miss the bound.
Values may be sent and summed in bfloat16 or wider, within the bound.
A program may use at most 384 MiB of HBM per device.

v0:
```python
import jax
import jax.numpy as jnp
from jax import lax
from jax.sharding import PartitionSpec as P

HD = 128


PRECISE = lax.Precision.HIGHEST
EPSILON = 1e-05
FLOOR_SCORE = -1e30


def for_sending(array):
    return jax.tree.map(lambda a: a.astype(jnp.bfloat16) if a.dtype == jnp.float32 else a, array)


def norm_rows(value):
    centred = value - jnp.mean(value, -1, keepdims=True)
    scaled = lax.rsqrt(jnp.mean(centred * centred, -1, keepdims=True) + EPSILON)
    return (centred * scaled, scaled)


def norm_back(normed, scaled, grad):
    return scaled * (
        grad
        - jnp.mean(grad, -1, keepdims=True)
        - normed * jnp.mean(grad * normed, -1, keepdims=True)
    )


def angles(positions, head_size):
    indices = jnp.arange(head_size // 2, dtype=jnp.float32)
    frequency = 10000.0 ** (-(2.0 * indices / head_size))
    turned = positions.astype(jnp.float32)[:, None] * frequency[None, :]
    return (jnp.cos(turned)[:, None, :], jnp.sin(turned)[:, None, :])


def rotate(value, cosine, sine):
    half = value.shape[-1] // 2
    first = value[..., :half]
    second = value[..., half:]
    return jnp.concatenate([first * cosine - second * sine, second * cosine + first * sine], -1)


def contract_rows(left, right):
    return lax.dot_general(
        left, right, (((0,), (0,)), ((), ())), preferred_element_type=jnp.float32
    )


def contract_cols(left, right):
    return lax.dot_general(
        left, right, (((1,), (1,)), ((), ())), preferred_element_type=jnp.float32
    )


def mixing(current, weight, static):
    normed, scaled = norm_rows(current)
    active = jnp.tanh(jnp.einsum("tsd,dk->tsk", normed, weight, precision=PRECISE))
    table = active + static
    branch_in = jnp.einsum("ts,tsd->td", table[..., 0], current, precision=PRECISE)
    return (branch_in, table, active, normed, scaled)


def combine(current, branch_out, table):
    total = current.shape[1]
    beta = table[..., total + 1]
    return beta[..., None] * branch_out[:, None, :] + jnp.einsum(
        "tij,tid->tjd", table[..., 1 : total + 1], current, precision=PRECISE
    )


def combine_back(current, branch_out, table, grad_top):
    total = current.shape[1]
    grad_branch = jnp.einsum("ts,tsd->td", table[..., total + 1], grad_top, precision=PRECISE)
    grad_beta = jnp.einsum("tsd,td->ts", grad_top, branch_out, precision=PRECISE)
    grad_mixer = jnp.einsum("tid,tjd->tij", current, grad_top, precision=PRECISE)
    grad_current = jnp.einsum(
        "tij,tjd->tid", table[..., 1 : total + 1], grad_top, precision=PRECISE
    )
    return (grad_branch, grad_beta, grad_mixer, grad_current)


def mixing_back(
    current, table, active, normed, scaled, weight, grad_in, grad_beta, grad_mixer, grad_current
):
    grad_alpha = jnp.einsum("td,tsd->ts", grad_in, current, precision=PRECISE)
    grad_table = jnp.concatenate([grad_alpha[..., None], grad_mixer, grad_beta[..., None]], -1)
    grad_inner = grad_table * (1.0 - active * active)
    grad_weight = jnp.einsum("tsd,tsk->dk", normed, grad_inner, precision=PRECISE)
    grad_normed = jnp.einsum("tsk,dk->tsd", grad_inner, weight, precision=PRECISE)
    grad_current = (
        grad_current
        + table[..., 0][..., None] * grad_in[:, None, :]
        + norm_back(normed, scaled, grad_normed)
    )
    return (grad_current, grad_weight, jnp.sum(grad_table, 0))


def key_block(keys, values, key_info, index, block, heads):
    start = index * block
    key_rows = lax.dynamic_slice_in_dim(keys, start, block, 0).reshape(block, heads, -1)
    value_rows = lax.dynamic_slice_in_dim(values, start, block, 0).reshape(block, heads, -1)
    info_rows = lax.dynamic_slice_in_dim(key_info, start, block, 0)
    return (key_rows, value_rows, info_rows)


def block_scores(queries, key_rows, info_rows, query_seg, query_pos):
    scores = jnp.einsum(
        "qhd,khd->hqk", queries, key_rows, preferred_element_type=jnp.float32
    ) * queries.shape[2] ** (-0.5)
    allowed = (query_seg[:, None] == info_rows[None, :, 0]) & (
        info_rows[None, :, 1] <= query_pos[:, None]
    )
    return (scores, allowed[None])


def shards(
    streams,
    lengths,
    destination,
    w_query,
    w_key,
    w_value,
    w_output,
    w_gate,
    w_up,
    w_down,
    mix_weight,
    mix_static,
    cotangent,
):
    rows_here, stream_total, model_width = streams.shape
    owners = lax.axis_size("ctx")
    run_rows = rows_here // owners
    group_rows = rows_here * owners
    placed = lax.axis_index("ctx") * rows_here + jnp.arange(rows_here, dtype=jnp.int32)
    ends = jnp.cumsum(lengths[0])
    starts = ends - lengths[0]
    segment = jnp.sum((placed[:, None] >= ends[None, :]).astype(jnp.int32), axis=1)
    begin = jnp.max(jnp.where(starts[None, :] <= placed[:, None], starts[None, :], 0), axis=1)
    local_dest = destination - lax.axis_index("shard") * group_rows
    sort_order = jnp.argsort(local_dest)
    inverse = jnp.argsort(sort_order)
    sent_info = jnp.stack([local_dest % rows_here, segment, placed - begin], axis=1)[sort_order]
    arrived, arrived_info = (
        lax.all_to_all(
            streams[sort_order].reshape(owners, run_rows, stream_total, model_width),
            "ctx",
            split_axis=0,
            concat_axis=0,
            tiled=True,
        ),
        lax.all_to_all(
            sent_info.reshape(owners, run_rows, 3), "ctx", split_axis=0, concat_axis=0, tiled=True
        ),
    )
    current = arrived.reshape(rows_here, stream_total, model_width).astype(jnp.float32)
    arrived_info = arrived_info.reshape(rows_here, 3)
    query_seg = arrived_info[:, 1]
    query_pos = arrived_info[:, 2]
    grad_top = cotangent[arrived_info[:, 0]].astype(jnp.float32)
    query_full, key_full, value_full, output_full, gate_full, up_full, down_full = (
        lax.all_gather(w_query, "shard", axis=0, tiled=True),
        lax.all_gather(w_key, "shard", axis=0, tiled=True),
        lax.all_gather(w_value, "shard", axis=0, tiled=True),
        lax.all_gather(w_output, "shard", axis=1, tiled=True),
        lax.all_gather(w_gate, "shard", axis=0, tiled=True),
        lax.all_gather(w_up, "shard", axis=0, tiled=True),
        lax.all_gather(w_down, "shard", axis=1, tiled=True),
    )
    heads = query_full.shape[1] // HD
    block = min(512, group_rows)
    blocks = group_rows // block
    scale = HD ** (-0.5)
    branch_in, table_one, active_one, normed_one, scaled_one = mixing(
        current, mix_weight[0], mix_static[0]
    )
    attn_normed, attn_scaled = norm_rows(branch_in)
    attn_input = attn_normed.astype(jnp.bfloat16)
    cosine, sine = angles(query_pos, HD)
    queries = rotate(
        jnp.dot(attn_input, query_full, preferred_element_type=jnp.float32).reshape(
            rows_here, heads, HD
        ),
        cosine,
        sine,
    ).astype(jnp.bfloat16)
    key_local = rotate(
        jnp.dot(attn_input, key_full, preferred_element_type=jnp.float32).reshape(
            rows_here, heads, HD
        ),
        cosine,
        sine,
    ).astype(jnp.bfloat16)
    value_local = jnp.dot(attn_input, value_full, preferred_element_type=jnp.float32).astype(
        jnp.bfloat16
    )
    keys, values, key_info = (
        lax.all_gather(key_local.reshape(rows_here, heads * HD), "ctx", axis=0, tiled=True),
        lax.all_gather(value_local, "ctx", axis=0, tiled=True),
        lax.all_gather(
            for_sending(jnp.stack([query_seg, query_pos], axis=1)), "ctx", axis=0, tiled=True
        ),
    )

    def stats_step(carry, index):
        top, total = carry
        key_rows, value_rows, info_rows = key_block(keys, values, key_info, index, block, heads)
        scores, allowed = block_scores(queries, key_rows, info_rows, query_seg, query_pos)
        new_top = jnp.maximum(top, jnp.max(jnp.where(allowed, scores, FLOOR_SCORE), -1))
        total = total * jnp.exp(top - new_top) + jnp.sum(
            jnp.where(allowed, jnp.exp(scores - new_top[..., None]), 0.0), -1
        )
        return ((new_top, total), None)

    start_top = jnp.full((heads, rows_here), FLOOR_SCORE, jnp.float32)
    (top, total), unused = lax.scan(
        stats_step, (start_top, jnp.zeros((heads, rows_here), jnp.float32)), jnp.arange(blocks)
    )
    log_total = top + jnp.log(total)

    def probs_of(index):
        key_rows, value_rows, info_rows = key_block(keys, values, key_info, index, block, heads)
        scores, allowed = block_scores(queries, key_rows, info_rows, query_seg, query_pos)
        return (
            jnp.where(allowed, jnp.exp(scores - log_total[..., None]), 0.0),
            key_rows,
            value_rows,
        )

    def out_step(accum, index):
        probs, key_rows, value_rows = probs_of(index)
        return (
            accum
            + jnp.einsum(
                "hqk,khd->qhd",
                probs.astype(jnp.bfloat16),
                value_rows,
                preferred_element_type=jnp.float32,
            ),
            None,
        )

    attended, unused = lax.scan(
        out_step, jnp.zeros((rows_here, heads, HD), jnp.float32), jnp.arange(blocks)
    )
    attended = attended.reshape(rows_here, heads * HD).astype(jnp.bfloat16)
    attn_out = lax.psum(
        jnp.dot(attended, output_full, preferred_element_type=jnp.float32), "tensor"
    )
    middle = combine(current, attn_out, table_one)
    branch_two, table_two, active_two, normed_two, scaled_two = mixing(
        middle, mix_weight[1], mix_static[1]
    )
    ffn_normed, ffn_scaled = norm_rows(branch_two)
    ffn_input = ffn_normed.astype(jnp.bfloat16)
    gate = jnp.dot(ffn_input, gate_full, preferred_element_type=jnp.float32)
    upward = jnp.dot(ffn_input, up_full, preferred_element_type=jnp.float32)
    hidden = (jax.nn.silu(gate) * upward).astype(jnp.bfloat16)
    ffn_out = lax.psum(
        jnp.dot(hidden, down_full, preferred_element_type=jnp.float32).astype(jnp.bfloat16),
        "tensor",
    ).astype(jnp.float32)
    final = combine(middle, ffn_out, table_two).astype(jnp.bfloat16)
    returned = lax.all_to_all(
        final.reshape(owners, run_rows, stream_total, model_width),
        "ctx",
        split_axis=0,
        concat_axis=0,
        tiled=True,
    )
    streams_out = returned.reshape(rows_here, stream_total, model_width)[inverse]
    query_full, key_full, value_full, output_full, gate_full, up_full, down_full = (
        lax.all_gather(w_query, "shard", axis=0, tiled=True),
        lax.all_gather(w_key, "shard", axis=0, tiled=True),
        lax.all_gather(w_value, "shard", axis=0, tiled=True),
        lax.all_gather(w_output, "shard", axis=1, tiled=True),
        lax.all_gather(w_gate, "shard", axis=0, tiled=True),
        lax.all_gather(w_up, "shard", axis=0, tiled=True),
        lax.all_gather(w_down, "shard", axis=1, tiled=True),
    )
    grad_branch, grad_beta, grad_mixer, grad_middle = combine_back(
        middle, ffn_out, table_two, grad_top
    )
    grad_ffn_out = grad_branch.astype(jnp.bfloat16)
    grad_down = contract_rows(hidden, grad_ffn_out)
    grad_hidden = contract_cols(grad_ffn_out, down_full)
    sigma = jax.nn.sigmoid(gate)
    grad_gate_in = (grad_hidden * upward * sigma * (1.0 + gate * (1.0 - sigma))).astype(
        jnp.bfloat16
    )
    grad_up_in = (grad_hidden * gate * sigma).astype(jnp.bfloat16)
    grad_gate = contract_rows(ffn_input, grad_gate_in)
    grad_up = contract_rows(ffn_input, grad_up_in)
    grad_ffn_input = lax.psum(
        (contract_cols(grad_gate_in, gate_full) + contract_cols(grad_up_in, up_full)).astype(
            jnp.bfloat16
        ),
        "tensor",
    ).astype(jnp.float32)
    grad_gate, grad_up, grad_down = (
        lax.psum_scatter(grad_gate, ("shard", "ctx"), scatter_dimension=0, tiled=True),
        lax.psum_scatter(grad_up, ("shard", "ctx"), scatter_dimension=0, tiled=True),
        lax.psum_scatter(grad_down, ("shard", "ctx"), scatter_dimension=1, tiled=True),
    )
    grad_branch_two = norm_back(ffn_normed, ffn_scaled, grad_ffn_input)
    grad_middle, grad_weight_two, grad_static_two = mixing_back(
        middle,
        table_two,
        active_two,
        normed_two,
        scaled_two,
        mix_weight[1],
        grad_branch_two,
        grad_beta,
        grad_mixer,
        grad_middle,
    )
    grad_branch, grad_beta, grad_mixer, grad_current = combine_back(
        current, attn_out, table_one, grad_middle
    )
    grad_attn_out = grad_branch.astype(jnp.bfloat16)
    grad_output = contract_rows(attended, grad_attn_out)
    grad_attended = (
        contract_cols(grad_attn_out, output_full).astype(jnp.bfloat16).reshape(rows_here, heads, HD)
    )

    def delta_step(delta, index):
        probs, key_rows, value_rows = probs_of(index)
        grad_probs = jnp.einsum(
            "qhd,khd->hqk", grad_attended, value_rows, preferred_element_type=jnp.float32
        )
        return (delta + jnp.sum(probs * grad_probs, -1), None)

    delta, unused = lax.scan(
        delta_step, jnp.zeros((heads, rows_here), jnp.float32), jnp.arange(blocks)
    )

    def grad_step(grad_query_acc, index):
        probs, key_rows, value_rows = probs_of(index)
        grad_probs = jnp.einsum(
            "qhd,khd->hqk", grad_attended, value_rows, preferred_element_type=jnp.float32
        )
        grad_scores = (probs * (grad_probs - delta[..., None])).astype(jnp.bfloat16)
        grad_query_acc = grad_query_acc + jnp.einsum(
            "hqk,khd->qhd", grad_scores, key_rows, preferred_element_type=jnp.float32
        )
        grad_key_rows = (
            jnp.einsum("hqk,qhd->khd", grad_scores, queries, preferred_element_type=jnp.float32)
            * scale
        )
        grad_value_rows = jnp.einsum(
            "hqk,qhd->khd",
            probs.astype(jnp.bfloat16),
            grad_attended,
            preferred_element_type=jnp.float32,
        )
        return (grad_query_acc, (grad_key_rows, grad_value_rows))

    grad_query_rot, key_value_terms = lax.scan(
        grad_step, jnp.zeros((rows_here, heads, HD), jnp.float32), jnp.arange(blocks)
    )
    grad_query_rot = grad_query_rot * scale
    grad_key_rot, grad_value_vec = (
        lax.psum_scatter(
            key_value_terms[0].reshape(group_rows, heads * HD).astype(jnp.bfloat16),
            "ctx",
            scatter_dimension=0,
            tiled=True,
        ).astype(jnp.float32),
        lax.psum_scatter(
            key_value_terms[1].reshape(group_rows, heads * HD).astype(jnp.bfloat16),
            "ctx",
            scatter_dimension=0,
            tiled=True,
        ).astype(jnp.float32),
    )
    grad_query_lin = (
        rotate(grad_query_rot, cosine, -sine).reshape(rows_here, heads * HD).astype(jnp.bfloat16)
    )
    grad_key_lin = (
        rotate(grad_key_rot.reshape(rows_here, heads, HD), cosine, -sine)
        .reshape(rows_here, heads * HD)
        .astype(jnp.bfloat16)
    )
    grad_value_lin = grad_value_vec.astype(jnp.bfloat16)
    grad_query = contract_rows(attn_input, grad_query_lin)
    grad_key = contract_rows(attn_input, grad_key_lin)
    grad_value = contract_rows(attn_input, grad_value_lin)
    grad_attn_input = lax.psum(
        (
            contract_cols(grad_query_lin, query_full)
            + contract_cols(grad_key_lin, key_full)
            + contract_cols(grad_value_lin, value_full)
        ).astype(jnp.bfloat16),
        "tensor",
    ).astype(jnp.float32)
    grad_query, grad_key, grad_value, grad_output = (
        lax.psum_scatter(grad_query, ("shard", "ctx"), scatter_dimension=0, tiled=True),
        lax.psum_scatter(grad_key, ("shard", "ctx"), scatter_dimension=0, tiled=True),
        lax.psum_scatter(grad_value, ("shard", "ctx"), scatter_dimension=0, tiled=True),
        lax.psum_scatter(grad_output, ("shard", "ctx"), scatter_dimension=1, tiled=True),
    )
    grad_branch_one = norm_back(attn_normed, attn_scaled, grad_attn_input)
    grad_current, grad_weight_one, grad_static_one = mixing_back(
        current,
        table_one,
        active_one,
        normed_one,
        scaled_one,
        mix_weight[0],
        grad_branch_one,
        grad_beta,
        grad_mixer,
        grad_current,
    )
    grad_mix_weight, grad_mix_static = lax.psum(
        (
            jnp.stack([grad_weight_one, grad_weight_two]),
            jnp.stack([grad_static_one, grad_static_two]),
        ),
        ("shard", "ctx"),
    )
    grad_back = lax.all_to_all(
        grad_current.astype(jnp.bfloat16).reshape(owners, run_rows, stream_total, model_width),
        "ctx",
        split_axis=0,
        concat_axis=0,
        tiled=True,
    )
    grad_streams = grad_back.reshape(rows_here, stream_total, model_width)[inverse]
    return (
        streams_out,
        grad_streams,
        grad_query,
        grad_key,
        grad_value,
        grad_output,
        grad_gate,
        grad_up,
        grad_down,
        grad_mix_weight,
        grad_mix_static,
    )


def solution(mesh):
    return jax.shard_map(
        shards,
        mesh=mesh,
        in_specs=(
            P(("shard", "ctx"), None, None),
            P("shard", None),
            P(("shard", "ctx")),
            P("shard", "tensor"),
            P("shard", "tensor"),
            P("shard", "tensor"),
            P("tensor", "shard"),
            P("shard", "tensor"),
            P("shard", "tensor"),
            P("tensor", "shard"),
            P(),
            P(),
            P(("shard", "ctx"), None, None),
        ),
        out_specs=(
            P(("shard", "ctx"), None, None),
            P(("shard", "ctx"), None, None),
            P(("shard", "ctx"), "tensor"),
            P(("shard", "ctx"), "tensor"),
            P(("shard", "ctx"), "tensor"),
            P("tensor", ("shard", "ctx")),
            P(("shard", "ctx"), "tensor"),
            P(("shard", "ctx"), "tensor"),
            P("tensor", ("shard", "ctx")),
            P(),
            P(),
        ),
        check_vma=False,
    )
```

profile of v0, /device:TPU:8, one launch (start us, length us, event | category | flops | bytes accessed | tf_op | source)
XLA Modules:
  0.0 4023.1 jit_solution(15721581580882088486)
XLA Ops:
  33.8 40.0 all-to-all-done
  92.4 26.0 all-gather.16.cloned.1.call-done
  125.0 48.0 %all-gather.10.cloned.1.call-done = bf16[2048,1024]{1,0:T(8,128)(2,1)} async-done(((bf16[512,1024]{1,0:T(8,128)(2,1)}), bf16[2048,1024]{1,0:T(8,128)(2,1)}) %all-gather.10.cloned.1.call-update) | async-done | bytes 4194320 | tf_op jit(solution)/shard_map/all_gather | solution.py:167
  186.2 20.0 all-gather.18.cloned.1.call-done
  210.7 22.7 all-gather.12.cloned.1.call-done
  236.1 51.1 %all-gather.20.cloned.1.call-done = bf16[1024,2048]{1,0:T(8,128)(2,1)} async-done(((bf16[1024,512]{1,0:T(8,128)(2,1)}), bf16[1024,2048]{1,0:T(8,128)(2,1)}) %all-gather.20.cloned.1.call-update) | async-done | bytes 4194320 | tf_op jit(solution)/shard_map/all_gather | solution.py:168
  300.7 10.5 all-reduce.6.cloned.1.call-done
  346.7 124.9 %all-gather.24.cloned.1.call-done = bf16[2048,4096]{1,0:T(8,128)(2,1)} async-done(((bf16[512,4096]{1,0:T(8,128)(2,1)}), bf16[2048,4096]{1,0:T(8,128)(2,1)}) %all-gather.24.cloned.1.call-update) | async-done | bytes 16777232 | tf_op jit(solution)/shard_map/all_gather | solution.py:170
  481.3 149.7 %all-gather.22.cloned.1.call-done = bf16[2048,4096]{1,0:T(8,128)(2,1)} async-done(((bf16[512,4096]{1,0:T(8,128)(2,1)}), bf16[2048,4096]{1,0:T(8,128)(2,1)}) %all-gather.22.cloned.1.call-update) | async-done | bytes 16777232 | tf_op jit(solution)/shard_map/all_gather | solution.py:169
  640.7 149.4 %all-gather.26.cloned.1.call-done = bf16[4096,2048]{1,0:T(8,128)(2,1)} async-done(((bf16[4096,512]{1,0:T(8,128)(2,1)}), bf16[4096,2048]{1,0:T(8,128)(2,1)}) %all-gather.26.cloned.1.call-update) | async-done | bytes 16777232 | tf_op jit(solution)/shard_map/all_gather | solution.py:171
  790.1 14.9 multiply_convert_fusion.2
  805.1 13.1 fusion.92
  827.1 13.1 fusion.9
  841.0 11.7 fusion.93
  863.6 18.7 fusion.33
  936.1 11.9 fusion.96
  965.1 18.3 reduce-scatter.30.cloned.1.call-done
  988.2 16.1 fusion.31
  1067.0 13.3 fusion.80
  1081.6 13.3 fusion.82
  1096.4 13.3 fusion.45
  1111.3 12.9 add_convert_fusion.1
  1131.8 14.7 add_convert_fusion
  1146.5 31.1 all-to-all-done.2
  1188.2 124.0 %psum.47 = f32[2,4,6]{2,1,0:T(4,128)} all-reduce(f32[2,4,6]{2,1,0:T(4,128)S(1)} %pad_maximum_fusion.9), channel_id=1, replica_groups=mesh['shard'=4,'ctx'=4,'tensor'=2] {'shard','ctx'}, use_global_device_ids=true, to_apply=%region_40.41 | all-reduce | flops 48 | bytes 384 | tf_op jit(solution)/shard_map/psum | solution.py:419
  1324.3 73.4 %reduce-scatter.20.cloned.1.call-done = f32[1024,128]{1,0:T(8,128)} async-done(((f32[1024,2048]{1,0:T(8,128)}), f32[1024,128]{1,0:T(8,128)}) %reduce-scatter.20.cloned.1.call-update) | async-done | bytes 524304 | tf_op jit(solution)/shard_map/reduce_scatter | solution.py:404
  1397.7 179.5 %reduce-scatter.18.cloned.1.call-done = f32[128,1024]{1,0:T(8,128)} async-done(((f32[2048,1024]{1,0:T(8,128)}), f32[128,1024]{1,0:T(8,128)}) %reduce-scatter.18.cloned.1.call-update) | async-done | bytes 524304 | tf_op jit(solution)/shard_map/reduce_scatter | solution.py:403
  1577.2 182.7 %reduce-scatter.16.cloned.1.call-done = f32[128,1024]{1,0:T(8,128)} async-done(((f32[2048,1024]{1,0:T(8,128)}), f32[128,1024]{1,0:T(8,128)}) %reduce-scatter.16.cloned.1.call-update) | async-done | bytes 524304 | tf_op jit(solution)/shard_map/reduce_scatter | solution.py:402
  1759.9 182.8 %reduce-scatter.14.cloned.1.call-done = f32[128,1024]{1,0:T(8,128)} async-done(((f32[2048,1024]{1,0:T(8,128)}), f32[128,1024]{1,0:T(8,128)}) %reduce-scatter.14.cloned.1.call-update) | async-done | bytes 524304 | tf_op jit(solution)/shard_map/reduce_scatter | solution.py:401
  1942.7 689.8 %reduce-scatter.24.cloned.1.call-done = f32[128,4096]{1,0:T(8,128)} async-done(((f32[2048,4096]{1,0:T(8,128)}), f32[128,4096]{1,0:T(8,128)}) %reduce-scatter.24.cloned.1.call-update) | async-done | bytes 2097168 | tf_op jit(solution)/shard_map/reduce_scatter | solution.py:305
  2632.6 691.7 %reduce-scatter.22.cloned.1.call-done = f32[128,4096]{1,0:T(8,128)} async-done(((f32[2048,4096]{1,0:T(8,128)}), f32[128,4096]{1,0:T(8,128)}) %reduce-scatter.22.cloned.1.call-update) | async-done | bytes 2097168 | tf_op jit(solution)/shard_map/reduce_scatter | solution.py:304
  3324.3 691.7 %reduce-scatter.26.cloned.1.call-done = f32[4096,128]{1,0:T(8,128)} async-done(((f32[4096,2048]{1,0:T(8,128)}), f32[4096,128]{1,0:T(8,128)}) %reduce-scatter.26.cloned.1.call-update) | async-done | bytes 2097168 | tf_op jit(solution)/shard_map/reduce_scatter | solution.py:306
  (393 shorter events, 332.8 us)
Async XLA Ops:
  7.2 82.1 %all-gather.14.cloned.1.call-start = ((), (), s32[]{:S(2)}) async-start(), calls=%async_computation.15 | async-start | bytes 5242880 | tf_op jit(solution)/shard_map/all_gather | solution.py:165
  7.9 110.5 %all-gather.16.cloned.1.call-start = ((), (), s32[]{:S(2)}) async-start(), calls=%async_computation.16 | async-start | bytes 5242880 | tf_op jit(solution)/shard_map/all_gather | solution.py:166
  15.5 9.5 all-to-all-start.1
  25.0 48.8 %all-to-all-start = ((bf16[4,32,4,2048]{3,2,1,0:T(4,128)(2,1)}), bf16[4,32,4,2048]{3,2,1,0:T(4,128)(2,1)S(1)}, u32[]{:S(2)}, u32[]{:S(2)}) async-start(bf16[4,32,4,2048]{3,2,1,0:T(4,128)(2,1)} %bitcast.238), calls=%async_computation | async-start | bytes 4194304 | tf_op jit(solution)/shard_map/all_to_all | solution.py:148
  30.0 143.0 %all-gather.10.cloned.1.call-start = ((), (), s32[]{:S(2)}) async-start(), calls=%async_computation.13 | async-start | bytes 5242880 | tf_op jit(solution)/shard_map/all_gather | solution.py:167
  30.7 175.5 %all-gather.18.cloned.1.call-start = ((), (), s32[]{:S(2)}) async-start(), calls=%async_computation.17 | async-start | bytes 1310720 | tf_op jit(solution)/shard_map/all_gather | solution.py:201
  73.8 237.4 %copy-start.5 = (bf16[4,32,4,2048]{3,2,1,0:T(4,128)(2,1)}, bf16[4,32,4,2048]{3,2,1,0:T(4,128)(2,1)S(1)}, u32[]{:S(2)}) copy-start(bf16[4,32,4,2048]{3,2,1,0:T(4,128)(2,1)S(1)} %all-to-all-done) | copy-start | bytes 6291460
  125.0 108.5 %all-gather.12.cloned.1.call-start = ((), (), s32[]{:S(2)}) async-start(), calls=%async_computation.14 | async-start | bytes 1310720 | tf_op jit(solution)/shard_map/all_gather | solution.py:202
  176.6 110.6 %all-gather.20.cloned.1.call-start = ((), (), s32[]{:S(2)}) async-start(), calls=%async_computation.18 | async-start | bytes 5242880 | tf_op jit(solution)/shard_map/all_gather | solution.py:168
  177.2 134.0 %all-reduce.6.cloned.1.call-start = ((), (), s32[]{:S(2)}) async-start(), calls=%async_computation.19 | async-start | bytes 2097152 | tf_op jit(solution)/shard_map/psum | solution.py:250
  236.1 55.8 %copy-start.23 = (bf16[8,128,128]{2,1,0:T(8,128)(2,1)}, bf16[8,128,128]{2,1,0:T(8,128)(2,1)S(1)}, u32[]{:S(2)}) copy-start(bf16[8,128,128]{2,1,0:T(8,128)(2,1)S(1)} %convolution_convert_fusion.2) | copy-start | bytes 786436
  291.2 180.4 %all-gather.24.cloned.1.call-start = ((), (), s32[]{:S(2)}) async-start(), calls=%async_computation.21 | async-start | bytes 20971520 | tf_op jit(solution)/shard_map/all_gather | solution.py:170
  291.9 339.1 %all-gather.22.cloned.1.call-start = ((), (), s32[]{:S(2)}) async-start(), calls=%async_computation.20 | async-start | bytes 20971520 | tf_op jit(solution)/shard_map/all_gather | solution.py:169
  292.7 497.5 %all-gather.26.cloned.1.call-start = ((), (), s32[]{:S(2)}) async-start(), calls=%async_computation.22 | async-start | bytes 20971520 | tf_op jit(solution)/shard_map/all_gather | solution.py:171
  293.3 567.0 %all-reduce.12.cloned.1.call-start = ((), (), s32[]{:S(2)}) async-start(), calls=%async_computation.34 | async-start | bytes 2097152 | tf_op jit(solution)/shard_map/psum | solution.py:262
  329.4 559.9 %copy-start.44 = (f32[128,4,6]{0,2,1:T(8,128)}, f32[128,4,6]{0,2,1:T(8,128)S(1)}, u32[]{:S(2)}) copy-start(f32[128,4,6]{0,2,1:T(8,128)S(1)} %get-tuple-element.258) | copy-start | bytes 36868
  340.1 521.9 %copy-start.53 = (f32[128]{0:T(128)}, f32[128]{0:T(128)S(1)}, u32[]{:S(2)}) copy-start(f32[128]{0:T(128)S(1)} %broadcast_multiply_fusion.10) | copy-start | bytes 1540
  340.5 521.5 %copy-start.55 = (f32[128]{0:T(128)}, f32[128]{0:T(128)S(1)}, u32[]{:S(2)}) copy-start(f32[128]{0:T(128)S(1)} %add_rsqrt_fusion.2) | copy-start | bytes 1540
  840.2 114.3 %reduce-scatter.28.cloned.1.call-start = ((), (), s32[]{:S(2)}) async-start(), calls=%async_computation.32 | async-start | bytes 1310720
  928.4 54.9 %reduce-scatter.30.cloned.1.call-start = ((), (), s32[]{:S(2)}) async-start(), calls=%async_computation.33 | async-start | bytes 1310720
  933.9 79.3 %all-reduce.8.cloned.1.call-start = ((), (), s32[]{:S(2)}) async-start(), calls=%async_computation.23 | async-start | bytes 1048576 | tf_op jit(solution)/shard_map/psum | solution.py:392
  988.0 324.3 %all-reduce.10.cloned.1.call-start = ((), (), s32[]{:S(2)}) async-start(), calls=%async_computation.31 | async-start | bytes 262144 | tf_op jit(solution)/shard_map/psum | solution.py:419
  1046.4 351.3 %reduce-scatter.20.cloned.1.call-start = ((), (), s32[]{:S(2)}) async-start(), calls=%async_computation.27 | async-start | bytes 8912896 | tf_op jit(solution)/shard_map/reduce_scatter | solution.py:404
  1051.1 526.1 %reduce-scatter.18.cloned.1.call-start = ((), (), s32[]{:S(2)}) async-start(), calls=%async_computation.26 | async-start | bytes 8912896 | tf_op jit(solution)/shard_map/reduce_scatter | solution.py:403
  1056.5 703.4 %reduce-scatter.16.cloned.1.call-start = ((), (), s32[]{:S(2)}) async-start(), calls=%async_computation.25 | async-start | bytes 8912896 | tf_op jit(solution)/shard_map/reduce_scatter | solution.py:402
  1061.2 881.5 %reduce-scatter.14.cloned.1.call-start = ((), (), s32[]{:S(2)}) async-start(), calls=%async_computation.24 | async-start | bytes 8912896 | tf_op jit(solution)/shard_map/reduce_scatter | solution.py:401
  1065.8 1566.7 %reduce-scatter.24.cloned.1.call-start = ((), (), s32[]{:S(2)}) async-start(), calls=%async_computation.29 | async-start | bytes 35651584 | tf_op jit(solution)/shard_map/reduce_scatter | solution.py:305
  1080.4 2243.9 %reduce-scatter.22.cloned.1.call-start = ((), (), s32[]{:S(2)}) async-start(), calls=%async_computation.28 | async-start | bytes 35651584 | tf_op jit(solution)/shard_map/reduce_scatter | solution.py:304
  1094.9 2921.1 %reduce-scatter.26.cloned.1.call-start = ((), (), s32[]{:S(2)}) async-start(), calls=%async_computation.30 | async-start | bytes 35651584 | tf_op jit(solution)/shard_map/reduce_scatter | solution.py:306
  1124.2 53.5 %all-to-all-start.2 = ((bf16[4,32,4,2048]{3,2,1,0:T(4,128)(2,1)}), bf16[4,32,4,2048]{3,2,1,0:T(4,128)(2,1)}, u32[]{:S(2)}, u32[]{:S(2)}) async-start(bf16[4,32,4,2048]{3,2,1,0:T(4,128)(2,1)} %bitcast.239), calls=%async_computation.2 | async-start | bytes 4194304 | tf_op jit(solution)/shard_map/all_to_all | solution.py:267
  1177.6 141.6 %all-to-all-start.3 = ((bf16[4,32,4,2048]{3,2,1,0:T(4,128)(2,1)}), bf16[4,32,4,2048]{3,2,1,0:T(4,128)(2,1)}, u32[]{:S(2)}, u32[]{:S(2)}) async-start(bf16[4,32,4,2048]{3,2,1,0:T(4,128)(2,1)} %bitcast.253), calls=%async_computation.3 | async-start | bytes 4194304 | tf_op jit(solution)/shard_map/all_to_all | solution.py:426
  1313.9 2702.1 %copy-start.1 = (bf16[128,4,2048]{2,1,0:T(4,128)(2,1)S(1)}, bf16[128,4,2048]{2,1,0:T(4,128)(2,1)}, u32[]{:S(2)}) copy-start(bf16[128,4,2048]{2,1,0:T(4,128)(2,1)} %param.13) | copy-start | bytes 6291460
  (87 other events, 1017.0 us)
Sparse Core Ops, SparseCore 0:
  9.9 53.9 all-gather.13
  65.7 52.6 all-gather.15
  120.3 52.6 all-gather.9
  175.0 31.2 all-gather.17
  208.3 25.1 all-gather.11
  235.1 52.0 all-gather.19
  291.3 19.8 all-reduce.5
  313.2 158.3 all-gather.23
  473.6 157.4 all-gather.21
  632.8 157.2 all-gather.25
  840.3 19.9 all-reduce.11
  928.5 25.9 reduce-scatter.27
  957.5 25.7 reduce-scatter.29
  988.1 19.7 all-reduce.7
  1046.5 109.0 all-reduce.9
  1158.5 239.1 reduce-scatter.19
  1400.5 176.6 reduce-scatter.17
  1580.1 179.7 reduce-scatter.15
  1762.9 179.7 reduce-scatter.13
  1945.6 686.8 reduce-scatter.23
  2635.6 688.6 reduce-scatter.21
  3327.4 688.6 reduce-scatter.25
where the time goes:
time: 4030 us; the launch traced here: 4020 us
  waiting for transfers between devices  3400 us (84%)
  matrix products  344 us (9%)
  blocking collectives  132 us (3%)
  local copies, waits for them, and re-layouts  60.2 us (1%)
  other arithmetic  42 us (1%)
    reduce_scatter x1, waiting for transfers between devices, shards(): lax.psum_scatter(grad_gate, ('shard', 'ctx'), scatter_dimension=0, tiled=...  692 us
    reduce_scatter x1, waiting for transfers between devices, shards(): lax.psum_scatter(grad_down, ('shard', 'ctx'), scatter_dimension=1, tiled=...  692 us
    reduce_scatter x1, waiting for transfers between devices, shards(): lax.psum_scatter(grad_up, ('shard', 'ctx'), scatter_dimension=0, tiled=True)  690 us
    reduce_scatter x1, waiting for transfers between devices, shards(): lax.psum_scatter(grad_query, ('shard', 'ctx'), scatter_dimension=0, tiled...  183 us
    reduce_scatter x1, waiting for transfers between devices, shards(): lax.psum_scatter(grad_key, ('shard', 'ctx'), scatter_dimension=0, tiled=T...  183 us
    reduce_scatter x1, waiting for transfers between devices, shards(): lax.psum_scatter(grad_value, ('shard', 'ctx'), scatter_dimension=0, tiled...  180 us
    all_gather x1, waiting for transfers between devices, shards(): lax.all_gather(w_gate, 'shard', axis=0, tiled=True)  150 us
    all_gather x1, waiting for transfers between devices, shards(): lax.all_gather(w_down, 'shard', axis=1, tiled=True)  149 us
  transfers between devices with their start and end apart: 26, of which 22 were waited for; matrix products, arithmetic and copies ran while one was open for 7% of the time, Pallas kernels for 0%

commit v1 on v0

v1 whole, which is shorter than its diff:
```python
import jax
import jax.numpy as jnp
from jax import lax
from jax.sharding import PartitionSpec as P

HD = 128


PRECISE = lax.Precision.HIGHEST
EPSILON = 1e-05
FLOOR_SCORE = -1e30
TEAM = ("ctx", "tensor")


def norm_rows(value):
    centred = value - jnp.mean(value, -1, keepdims=True)
    scaled = lax.rsqrt(jnp.mean(centred * centred, -1, keepdims=True) + EPSILON)
    return (centred * scaled, scaled)


def norm_back(normed, scaled, grad):
    return scaled * (
        grad
        - jnp.mean(grad, -1, keepdims=True)
        - normed * jnp.mean(grad * normed, -1, keepdims=True)
    )


def angles(positions, head_size):
    indices = jnp.arange(head_size // 2, dtype=jnp.float32)
    frequency = 10000.0 ** (-(2.0 * indices / head_size))
    turned = positions.astype(jnp.float32)[:, None] * frequency[None, :]
    return (jnp.cos(turned)[:, None, :], jnp.sin(turned)[:, None, :])


def rotate(value, cosine, sine):
    half = value.shape[-1] // 2
    first = value[..., :half]
    second = value[..., half:]
    return jnp.concatenate([first * cosine - second * sine, second * cosine + first * sine], -1)


def dot(left, right):
    return jnp.dot(left, right, preferred_element_type=jnp.float32)


def contract_rows(left, right):
    return lax.dot_general(
        left, right, (((0,), (0,)), ((), ())), preferred_element_type=jnp.float32
    )


def contract_cols(left, right):
    return lax.dot_general(
        left, right, (((1,), (1,)), ((), ())), preferred_element_type=jnp.float32
    )


def mixing(current, weight, static):
    normed, scaled = norm_rows(current)
    active = jnp.tanh(jnp.einsum("tsd,dk->tsk", normed, weight, precision=PRECISE))
    table = active + static
    total = current.shape[1]
    branch_in = sum(table[:, i, 0][:, None] * current[:, i] for i in range(total))
    return (branch_in, table, active, normed, scaled)


def combine(current, branch_out, table):
    total = current.shape[1]
    return jnp.stack(
        [
            table[:, j, total + 1][:, None] * branch_out
            + sum(table[:, i, 1 + j][:, None] * current[:, i] for i in range(total))
            for j in range(total)
        ],
        1,
    )


def combine_back(current, table, grad_top):
    total = current.shape[1]
    grad_mixer = jnp.stack(
        [jnp.sum(current * grad_top[:, j][:, None], -1) for j in range(total)], -1
    )
    grad_current = jnp.stack(
        [
            sum(table[:, i, 1 + j][:, None] * grad_top[:, j] for j in range(total))
            for i in range(total)
        ],
        1,
    )
    return (grad_mixer, grad_current)


def branch_grad(table, grad_top):
    total = grad_top.shape[1]
    return sum(table[:, j, total + 1][:, None] * grad_top[:, j] for j in range(total))


def mixing_back(
    current, table, active, normed, scaled, weight, grad_in, grad_beta, grad_mixer, grad_current
):
    grad_alpha = jnp.sum(grad_in[:, None] * current, -1)
    grad_table = jnp.concatenate([grad_alpha[..., None], grad_mixer, grad_beta[..., None]], -1)
    grad_inner = grad_table * (1.0 - active * active)
    grad_weight = jnp.einsum("tsd,tsk->dk", normed, grad_inner, precision=PRECISE)
    grad_normed = jnp.einsum("tsk,dk->tsd", grad_inner, weight, precision=PRECISE)
    grad_current = (
        grad_current
        + table[..., 0][..., None] * grad_in[:, None, :]
        + norm_back(normed, scaled, grad_normed)
    )
    return (grad_current, grad_weight, jnp.sum(grad_table, 0))


def team_gather(value):
    return lax.all_gather(value, TEAM, axis=0, tiled=True)


def team_sum(value, kind=jnp.bfloat16):
    return lax.psum_scatter(
        value.astype(kind), TEAM, scatter_dimension=0, tiled=True
    ).astype(jnp.float32)


def shards(
    streams,
    lengths,
    destination,
    w_query,
    w_key,
    w_value,
    w_output,
    w_gate,
    w_up,
    w_down,
    mix_weight,
    mix_static,
    cotangent,
):
    rows_here, stream_total, width = streams.shape
    owners = lax.axis_size("ctx")
    cores = lax.axis_size("tensor")
    here = lax.axis_index("ctx")
    core = lax.axis_index("tensor")
    run_rows = rows_here // owners
    part = run_rows // cores
    mine = rows_here // cores
    group_rows = rows_here * owners
    head_cols = w_query.shape[1] // owners
    heads = head_cols // HD
    units = w_gate.shape[1] // owners
    scale = HD ** (-0.5)

    def columns(weight, count):
        return lax.dynamic_slice_in_dim(weight, here * count, count, 1)

    def rows(weight, count):
        return lax.dynamic_slice_in_dim(weight, here * count, count, 0)

    qkv = jnp.concatenate([columns(w, head_cols) for w in (w_query, w_key, w_value)], 1)
    qkv = lax.all_gather(qkv, "shard", axis=0, tiled=True)
    out_w = lax.all_gather(rows(w_output, head_cols), "shard", axis=0)
    out_w = out_w.transpose(1, 0, 2).reshape(head_cols, width)
    gate_up = jnp.concatenate([columns(w, units) for w in (w_gate, w_up)], 1)
    gate_up = lax.all_gather(gate_up, "shard", axis=0, tiled=True)
    down = lax.all_gather(rows(w_down, units), "shard", axis=0)
    down = down.transpose(1, 0, 2).reshape(units, width)

    order = jnp.arange(group_rows, dtype=jnp.int32)
    within = order % mine
    placed = (
        order // rows_here * rows_here
        + within // part * run_rows
        + order % rows_here // mine * part
        + within % part
    )
    spans = lengths[0]
    count = jnp.arange(spans.shape[0], dtype=jnp.int32)
    ends = jnp.sum(jnp.where(count[None, :] <= count[:, None], spans[None, :], 0), 1)
    starts = ends - spans
    segment = jnp.sum((placed[:, None] >= ends[None, :]).astype(jnp.int32), axis=1)
    begin = jnp.max(jnp.where(starts[None, :] <= placed[:, None], starts[None, :], 0), axis=1)
    position = placed - begin

    local_dest = destination - lax.axis_index("shard") * group_rows
    heads_of_runs = local_dest.reshape(owners, run_rows)[:, 0]
    every = lax.all_gather(heads_of_runs, "ctx", axis=0)
    sent = jnp.sum(jnp.where(every // rows_here == here, every % rows_here, 0), 1) + core * part
    packed = jnp.concatenate(
        [lax.dynamic_slice_in_dim(cotangent, sent[c], part, 0) for c in range(owners)], 0
    )
    arrived = lax.all_to_all(packed, "ctx", split_axis=0, concat_axis=0, tiled=True)
    came_from = heads_of_runs // rows_here * part
    grad_top = jnp.concatenate(
        [lax.dynamic_slice_in_dim(arrived, came_from[r], part, 0) for r in range(owners)], 0
    ).astype(jnp.float32)

    def own_rows(value):
        split = value.reshape(owners, cores, part, stream_total, width)
        return lax.dynamic_index_in_dim(split, core, 1, keepdims=False).reshape(
            mine, stream_total, width
        )

    current = own_rows(streams).astype(jnp.float32)
    branch_in, table_one, active_one, normed_one, scaled_one = mixing(
        current, mix_weight[0], mix_static[0]
    )
    attn_normed, attn_scaled = norm_rows(branch_in)
    attn_input = team_gather(attn_normed.astype(jnp.bfloat16))
    cosine, sine = angles(position, HD)
    lin = dot(attn_input, qkv).reshape(group_rows, 3, heads, HD)
    queries = rotate(lin[:, 0], cosine, sine).astype(jnp.bfloat16)
    keys = rotate(lin[:, 1], cosine, sine).astype(jnp.bfloat16)
    values = lin[:, 2].astype(jnp.bfloat16)
    allowed = (segment[:, None] == segment[None, :]) & (position[None, :] <= position[:, None])
    scores = jnp.einsum("qhd,khd->hqk", queries, keys, preferred_element_type=jnp.float32) * scale
    scores = jnp.where(allowed[None], scores, FLOOR_SCORE)
    top = jnp.max(scores, -1, keepdims=True)
    probs = jnp.where(allowed[None], jnp.exp(scores - top), 0.0)
    probs = probs / jnp.sum(probs, -1, keepdims=True)
    probs_low = probs.astype(jnp.bfloat16)
    attended = jnp.einsum("hqk,khd->qhd", probs_low, values, preferred_element_type=jnp.float32)
    attended = attended.reshape(group_rows, head_cols).astype(jnp.bfloat16)
    attn_out = team_sum(dot(attended, out_w), jnp.float32)

    middle = combine(current, attn_out, table_one)
    branch_two, table_two, active_two, normed_two, scaled_two = mixing(
        middle, mix_weight[1], mix_static[1]
    )
    ffn_normed, ffn_scaled = norm_rows(branch_two)
    ffn_input = team_gather(ffn_normed.astype(jnp.bfloat16))
    grad_ffn_out = team_gather(branch_grad(table_two, grad_top).astype(jnp.bfloat16))
    both = dot(ffn_input, gate_up)
    gate, upward = both[:, :units], both[:, units:]
    sigma = jax.nn.sigmoid(gate)
    hidden = (gate * sigma * upward).astype(jnp.bfloat16)
    ffn_out = team_sum(dot(hidden, down))
    grad_hidden = contract_cols(grad_ffn_out, down)
    grad_both = jnp.concatenate(
        [
            (grad_hidden * upward * sigma * (1.0 + gate * (1.0 - sigma))).astype(jnp.bfloat16),
            (grad_hidden * gate * sigma).astype(jnp.bfloat16),
        ],
        1,
    )
    grad_ffn_input = team_sum(contract_cols(grad_both, gate_up))

    def to_owner_rows(partial):
        summed = lax.psum_scatter(
            partial.astype(jnp.bfloat16), "shard", scatter_dimension=0, tiled=True
        )
        moved = lax.all_to_all(summed, "ctx", split_axis=0, concat_axis=0, tiled=True)
        return moved.reshape(owners, summed.shape[0] // owners, summed.shape[1])

    def row_parts(moved, amount):
        split = moved.reshape(owners, moved.shape[1], amount, moved.shape[2] // amount)
        return [
            split[:, :, i].transpose(1, 0, 2).reshape(moved.shape[1], -1).astype(jnp.float32)
            for i in range(amount)
        ]

    def to_owner_columns(left, right):
        shard_total = lax.axis_size("shard")
        partial = jnp.einsum(
            "th,tsd->shd",
            left,
            right.reshape(group_rows, shard_total, -1),
            preferred_element_type=jnp.float32,
        )
        summed = lax.psum_scatter(
            partial.astype(jnp.bfloat16), "shard", scatter_dimension=0, tiled=False
        )
        split = summed.reshape(left.shape[1], owners, -1).transpose(1, 0, 2)
        moved = lax.all_to_all(split, "ctx", split_axis=0, concat_axis=0, tiled=True)
        return moved.reshape(owners * left.shape[1], -1).astype(jnp.float32)

    grad_down = to_owner_columns(hidden, grad_ffn_out)
    grad_gate, grad_up = row_parts(to_owner_rows(contract_rows(ffn_input, grad_both)), 2)

    grad_beta = jnp.sum(grad_top * ffn_out[:, None], -1)
    grad_mixer, grad_middle = combine_back(middle, table_two, grad_top)
    grad_branch_two = norm_back(ffn_normed, ffn_scaled, grad_ffn_input)
    grad_middle, grad_weight_two, grad_static_two = mixing_back(
        middle,
        table_two,
        active_two,
        normed_two,
        scaled_two,
        mix_weight[1],
        grad_branch_two,
        grad_beta,
        grad_mixer,
        grad_middle,
    )
    grad_attn_out = team_gather(branch_grad(table_one, grad_middle).astype(jnp.bfloat16))
    final = combine(middle, ffn_out, table_two).astype(jnp.bfloat16)

    grad_attended = (
        contract_cols(grad_attn_out, out_w).astype(jnp.bfloat16).reshape(group_rows, heads, HD)
    )
    grad_probs = jnp.einsum(
        "qhd,khd->hqk", grad_attended, values, preferred_element_type=jnp.float32
    )
    delta = jnp.sum(probs * grad_probs, -1, keepdims=True)
    grad_scores = (probs * (grad_probs - delta)).astype(jnp.bfloat16)
    grad_query_rot = (
        jnp.einsum("hqk,khd->qhd", grad_scores, keys, preferred_element_type=jnp.float32) * scale
    )
    grad_key_rot = (
        jnp.einsum("hqk,qhd->khd", grad_scores, queries, preferred_element_type=jnp.float32)
        * scale
    )
    grad_value_vec = jnp.einsum(
        "hqk,qhd->khd", probs_low, grad_attended, preferred_element_type=jnp.float32
    )
    grad_lin = jnp.concatenate(
        [
            rotate(grad_query_rot, cosine, -sine).reshape(group_rows, head_cols),
            rotate(grad_key_rot, cosine, -sine).reshape(group_rows, head_cols),
            grad_value_vec.reshape(group_rows, head_cols),
        ],
        1,
    ).astype(jnp.bfloat16)
    grad_attn_input = team_sum(contract_cols(grad_lin, qkv))
    grad_output = to_owner_columns(attended, grad_attn_out)
    grad_query, grad_key, grad_value = row_parts(
        to_owner_rows(contract_rows(attn_input, grad_lin)), 3
    )

    grad_beta = jnp.sum(grad_middle * attn_out[:, None], -1)
    grad_mixer, grad_current = combine_back(current, table_one, grad_middle)
    grad_branch_one = norm_back(attn_normed, attn_scaled, grad_attn_input)
    grad_current, grad_weight_one, grad_static_one = mixing_back(
        current,
        table_one,
        active_one,
        normed_one,
        scaled_one,
        mix_weight[0],
        grad_branch_one,
        grad_beta,
        grad_mixer,
        grad_current,
    )
    grad_mix_weight, grad_mix_static = lax.psum(
        (
            jnp.stack([grad_weight_one, grad_weight_two]),
            jnp.stack([grad_static_one, grad_static_two]),
        ),
        ("shard", "ctx", "tensor"),
    )

    def all_rows(value):
        value = value.astype(jnp.bfloat16).reshape(owners, part, stream_total, width)
        full = lax.all_gather(value, "tensor", axis=1)
        return full.reshape(rows_here, stream_total, width)

    return (
        all_rows(final),
        all_rows(grad_current),
        grad_query,
        grad_key,
        grad_value,
        grad_output,
        grad_gate,
        grad_up,
        grad_down,
        grad_mix_weight,
        grad_mix_static,
    )


def solution(mesh):
    return jax.shard_map(
        shards,
        mesh=mesh,
        in_specs=(
            P(("shard", "ctx"), None, None),
            P("shard", None),
            P(("shard", "ctx")),
            P("shard", "tensor"),
            P("shard", "tensor"),
            P("shard", "tensor"),
            P("tensor", "shard"),
            P("shard", "tensor"),
            P("shard", "tensor"),
            P("tensor", "shard"),
            P(),
            P(),
            P(("shard", "ctx"), None, None),
        ),
        out_specs=(
            P(("shard", "ctx"), None, None),
            P(("shard", "ctx"), None, None),
            P(("shard", "ctx"), "tensor"),
            P(("shard", "ctx"), "tensor"),
            P(("shard", "ctx"), "tensor"),
            P("tensor", ("shard", "ctx")),
            P(("shard", "ctx"), "tensor"),
            P(("shard", "ctx"), "tensor"),
            P("tensor", ("shard", "ctx")),
            P(),
            P(),
        ),
        check_vma=False,
    )
```

time: 4030 us -> 1030 us (0.26)
  waiting for transfers between devices: 3400 us -> 646 us
  matrix products: 344 us -> 96.6 us
  blocking collectives: 132 us -> 58.7 us
    reduce_scatter x7 -> x6, waiting for transfers between devices: 2690 us -> 200 us  [the longest x2 105 us: to_owner_rows(): lax.psum_scatter(partial.astype(jnp.bfloat16), 'shard', scatter_dimension...]
    all_gather x9 -> x10, waiting for transfers between devices: 592 us -> 289 us  [the longest x4 101 us: team_gather(): return lax.all_gather(value, TEAM, axis=0, tiled=True)]
    dot_general x27 -> x11, matrix products: 202 us -> 40.7 us  [the longest x4 25 us: dot(): return jnp.dot(left, right, preferred_element_type=jnp.float32)]
    psum x1, waiting for transfers between devices: 0.01 us -> 82.3 us  [shards(): lax.psum((jnp.stack([grad_weight_one, grad_weight_two]), jnp.stack([grad_...]
    psum x1, blocking collectives: 124 us -> 50 us  [shards(): lax.psum((jnp.stack([grad_weight_one, grad_weight_two]), jnp.stack([grad_...]
    dot_general x7 -> x2, matrix products: 58.2 us -> 15.3 us  [contract_rows(): lax.dot_general(left, right, (((0,), (0,)), ((), ())), preferred_element_...]
  transfers between devices with their start and end apart: 26 -> 24, of which waited for: 22 -> 21; matrix products, arithmetic and copies ran while one was open for 7% -> 17% of each run, Pallas kernels for 0% -> 0%
where the time goes in v1:
time: 1030 us; the launch traced here: 1020 us
  waiting for transfers between devices  646 us (63%)
  matrix products  96.6 us (9%)
  local copies, waits for them, and re-layouts  92.6 us (9%)
  other arithmetic  65.3 us (6%)
  blocking collectives  58.7 us (6%)
  between operations  32.3 us (3%)
  starting transfers between devices  28.3 us (3%)
    reduce_scatter x2, waiting for transfers between devices, to_owner_rows(): lax.psum_scatter(partial.astype(jnp.bfloat16), 'shard', scatter_dimension...  105 us
    all_gather x4, waiting for transfers between devices, team_gather(): return lax.all_gather(value, TEAM, axis=0, tiled=True)  101 us
    reduce_scatter x4, waiting for transfers between devices, team_sum(): lax.psum_scatter(value.astype(kind), TEAM, scatter_dimension=0, tiled=True)  95.7 us
    all_gather x1, waiting for transfers between devices, shards(): gate_up = lax.all_gather(gate_up, 'shard', axis=0, tiled=True)  83.6 us
    psum x1, waiting for transfers between devices, shards(): lax.psum((jnp.stack([grad_weight_one, grad_weight_two]), jnp.stack([grad_...  82.3 us
    psum x1, blocking collectives, shards(): lax.psum((jnp.stack([grad_weight_one, grad_weight_two]), jnp.stack([grad_...  50 us
    all_gather x1, waiting for transfers between devices, shards(): qkv = lax.all_gather(qkv, 'shard', axis=0, tiled=True)  45.9 us
    all_gather x1, waiting for transfers between devices, shards(): down = lax.all_gather(rows(w_down, units), 'shard', axis=0)  42.6 us
  transfers between devices with their start and end apart: 24, of which 21 were waited for; matrix products, arithmetic and copies ran while one was open for 17% of the time, Pallas kernels for 0%

profile of v1, /device:TPU:8, one launch (start us, length us, event | category | flops | bytes accessed | tf_op | source)
XLA Modules:
  0.0 1020.1 jit_solution(14557247119277641216)
XLA Ops:
  24.1 8.7 all-reduce
  40.5 29.0 %all-gather.14.cloned.1.call-done = bf16[512,2048]{1,0:T(8,128)(2,1)} async-done(((bf16[64,2048]{1,0:T(8,128)(2,1)}), bf16[512,2048]{1,0:T(8,128)(2,1)}) %all-gather.14.cloned.1.call-update) | async-done | bytes 2097168 | tf_op jit(solution)/shard_map/all_gather | solution.py:117
  69.6 45.9 %all-gather.16.cloned.1.call-done = bf16[2048,768]{1,0:T(8,128)(2,1)} async-done(((bf16[512,768]{1,0:T(8,128)(2,1)}), bf16[2048,768]{1,0:T(8,128)(2,1)}) %all-gather.16.cloned.1.call-update) | async-done | bytes 3145744 | tf_op jit(solution)/shard_map/all_gather | solution.py:162
  115.5 5.4 fusion.111
  160.6 5.1 all-to-all-start
  175.1 30.0 %all-to-all-done = bf16[64,4,2048]{2,1,0:T(4,128)(2,1)} async-done(((bf16[64,4,2048]{2,1,0:T(4,128)(2,1)}), bf16[64,4,2048]{2,1,0:T(4,128)(2,1)}, u32[]{:S(2)}, u32[]{:S(2)}) %all-to-all-start) | async-done | bytes 1048608 | tf_op jit(solution)/shard_map/all_to_all | solution.py:193
  226.5 42.6 %all-gather.32.cloned.1.call-done = bf16[4096,512]{1,0:T(8,128)(2,1)} async-done(((bf16[1024,512]{1,0:T(8,128)(2,1)}), bf16[4096,512]{1,0:T(8,128)(2,1)}) %all-gather.32.cloned.1.call-update) | async-done | bytes 4194320 | tf_op jit(solution)/shard_map/all_gather | solution.py:167
  269.1 6.3 copy.225
  275.4 83.6 %all-gather.20.cloned.1.call-done = bf16[2048,2048]{1,0:T(8,128)(2,1)} async-done(((bf16[512,2048]{1,0:T(8,128)(2,1)}), bf16[2048,2048]{1,0:T(8,128)(2,1)}) %all-gather.20.cloned.1.call-update) | async-done | bytes 8388624 | tf_op jit(solution)/shard_map/all_gather | solution.py:166
  359.0 30.7 %all-gather.18.cloned.1.call-done = bf16[512,2048]{1,0:T(8,128)(2,1)} async-done(((bf16[64,2048]{1,0:T(8,128)(2,1)}), bf16[512,2048]{1,0:T(8,128)(2,1)}) %all-gather.18.cloned.1.call-update) | async-done | bytes 2097168 | tf_op jit(solution)/shard_map/all_gather | solution.py:117
  389.7 10.5 %fusion.113 = f32[512,2048]{1,0:T(8,128)} fusion(bf16[512,2048]{1,0:T(8,128)(2,1)} %all-gather.18.cloned.1.call-done, bf16[2048,2048]{1,0:T(8,128)(2,1)} %all-gather.20.cloned.1.call-done), kind=kOutput, calls=%fused_computation.353 | convolution fusion | flops 4294967296 | bytes 14680064 | tf_op jit(solution)/shard_map/dot_general | solution.py:44
  400.2 19.7 %all-gather.24.cloned.1.call-done = bf16[512,2048]{1,0:T(8,128)(2,1)} async-done(((bf16[64,2048]{1,0:T(8,128)(2,1)}), bf16[512,2048]{1,0:T(8,128)(2,1)}) %all-gather.24.cloned.1.call-update) | async-done | bytes 2097168 | tf_op jit(solution)/shard_map/all_gather | solution.py:117
  419.9 8.2 multiply_convert_fusion.2
  429.4 5.7 convolution_convert_fusion.4
  435.3 6.2 convolution_convert_fusion.2
  447.1 20.0 %reduce-scatter.17.cloned.1.call-done = bf16[64,2048]{1,0:T(8,128)(2,1)} async-done(((bf16[512,2048]{1,0:T(8,128)(2,1)}), bf16[64,2048]{1,0:T(8,128)(2,1)}) %reduce-scatter.17.cloned.1.call-update) | async-done | bytes 262160 | tf_op jit(solution)/shard_map/reduce_scatter | solution.py:121
  468.5 35.7 %reduce-scatter.15.cloned.1.call-done = bf16[64,2048]{1,0:T(8,128)(2,1)} async-done(((bf16[512,2048]{1,0:T(8,128)(2,1)}), bf16[64,2048]{1,0:T(8,128)(2,1)}) %reduce-scatter.15.cloned.1.call-update) | async-done | bytes 262160 | tf_op jit(solution)/shard_map/reduce_scatter | solution.py:121
  521.7 6.2 convert_bitcast_fusion
  528.2 21.2 %all-gather.26.cloned.1.call-done = bf16[512,2048]{1,0:T(8,128)(2,1)} async-done(((bf16[64,2048]{1,0:T(8,128)(2,1)}), bf16[512,2048]{1,0:T(8,128)(2,1)}) %all-gather.26.cloned.1.call-update) | async-done | bytes 2097168 | tf_op jit(solution)/shard_map/all_gather | solution.py:117
  573.6 5.3 convolution_convert_fusion.1
  579.2 10.0 convolution_convert_fusion
  597.0 7.4 reduce-scatter.27.cloned.1.call-done
  604.4 5.2 all-to-all-start.4
  617.6 38.4 %reduce-scatter.19.cloned.1.call-done = bf16[64,2048]{1,0:T(8,128)(2,1)} async-done(((bf16[512,2048]{1,0:T(8,128)(2,1)}), bf16[64,2048]{1,0:T(8,128)(2,1)}) %reduce-scatter.19.cloned.1.call-update) | async-done | bytes 262160 | tf_op jit(solution)/shard_map/reduce_scatter | solution.py:121
  657.4 30.1 %reduce-scatter.25.cloned.1.call-done = bf16[1,256,512]{1,2,0:T(8,128)(2,1)} async-done(((bf16[4,256,512]{1,2,0:T(8,128)(2,1)}), bf16[1,256,512]{1,2,0:T(8,128)(2,1)}) %reduce-scatter.25.cloned.1.call-update) | async-done | bytes 262160
  694.9 39.5 %reduce-scatter.21.cloned.1.call-done = bf16[512,768]{1,0:T(8,128)(2,1)} async-done(((bf16[2048,768]{1,0:T(8,128)(2,1)}), bf16[512,768]{1,0:T(8,128)(2,1)}) %reduce-scatter.21.cloned.1.call-update) | async-done | bytes 786448 | tf_op jit(solution)/shard_map/reduce_scatter | solution.py:250
  752.0 6.6 all-to-all-done.1
  758.6 65.1 %reduce-scatter.23.cloned.1.call-done = bf16[512,2048]{1,0:T(8,128)(2,1)} async-done(((bf16[2048,2048]{1,0:T(8,128)(2,1)}), bf16[512,2048]{1,0:T(8,128)(2,1)}) %reduce-scatter.23.cloned.1.call-update) | async-done | bytes 2097168 | tf_op jit(solution)/shard_map/reduce_scatter | solution.py:250
  823.7 5.3 all-to-all-start.3
  844.9 50.0 %psum.15 = f32[2,4,6]{2,1,0:T(4,128)} all-reduce(f32[2,4,6]{2,1,0:T(4,128)S(1)} %pad_maximum_fusion.16), channel_id=1, replica_groups=mesh['shard'=4,'ctx'=4,'tensor'=2] {'shard','ctx','tensor'}, use_global_device_ids=true, to_apply=%region_46.47 | all-reduce | flops 48 | bytes 384 | tf_op jit(solution)/shard_map/psum | solution.py:346
  895.0 82.3 %all-reduce.5.cloned.1.call-done = f32[2,2048,6]{1,2,0:T(8,128)} async-done(((f32[2,2048,6]{1,2,0:T(8,128)}), f32[2,2048,6]{1,2,0:T(8,128)}) %all-reduce.5.cloned.1.call-update) | async-done | bytes 98320 | tf_op jit(solution)/shard_map/psum | solution.py:346
  978.8 10.5 %all-gather.28.cloned.1.call-done = bf16[4,2,16,4,2048]{4,2,3,0,1:T(8,128)(2,1)} async-done(((bf16[4,1,16,4,2048]{4,2,3,0,1:T(8,128)(2,1)}), bf16[4,2,16,4,2048]{4,2,3,0,1:T(8,128)(2,1)}) %all-gather.28.cloned.1.call-update) | async-done | bytes 2097168 | tf_op jit(solution)/shard_map/all_gather | solution.py:356
  (473 shorter events, 211.3 us)
Async XLA Ops:
  7.2 31.1 %all-gather.30.cloned.1.call-start = ((), (), s32[]{:S(2)}) async-start(), calls=%async_computation.28 | async-start | bytes 1310720 | tf_op jit(solution)/shard_map/all_gather | solution.py:163
  9.1 60.5 %all-gather.14.cloned.1.call-start = ((), (), s32[]{:S(2)}) async-start(), calls=%async_computation.13 | async-start | bytes 2359296 | tf_op jit(solution)/shard_map/all_gather | solution.py:117
  17.3 195.2 %copy-start.68 = (f32[64]{0:T(128)}, f32[64]{0:T(128)S(1)}, u32[]{:S(2)}) copy-start(f32[64]{0:T(128)S(1)} %get-tuple-element.203) | copy-start | bytes 772
  19.3 96.2 %all-gather.16.cloned.1.call-start = ((), (), s32[]{:S(2)}) async-start(), calls=%async_computation.14 | async-start | bytes 3932160 | tf_op jit(solution)/shard_map/all_gather | solution.py:162
  22.4 190.2 %reduce-scatter.13.cloned.1.call-start = ((), (), s32[]{:S(2)}) async-start(), calls=%async_computation.15 | async-start | bytes 4718592 | tf_op jit(solution)/shard_map/reduce_scatter | solution.py:121
  143.2 125.9 %all-gather.32.cloned.1.call-start = ((), (), s32[]{:S(2)}) async-start(), calls=%async_computation.29 | async-start | bytes 5242880 | tf_op jit(solution)/shard_map/all_gather | solution.py:167
  145.5 213.5 %all-gather.20.cloned.1.call-start = ((), (), s32[]{:S(2)}) async-start(), calls=%async_computation.17 | async-start | bytes 10485760 | tf_op jit(solution)/shard_map/all_gather | solution.py:166
  160.6 44.4 %all-to-all-start = ((bf16[64,4,2048]{2,1,0:T(4,128)(2,1)}), bf16[64,4,2048]{2,1,0:T(4,128)(2,1)}, u32[]{:S(2)}, u32[]{:S(2)}) async-start(bf16[64,4,2048]{2,1,0:T(4,128)(2,1)} %pad_maximum_fusion.6), calls=%async_computation.2 | async-start | bytes 2097152 | tf_op jit(solution)/shard_map/all_to_all | solution.py:193
  165.8 223.9 %all-gather.18.cloned.1.call-start = ((), (), s32[]{:S(2)}) async-start(), calls=%async_computation.16 | async-start | bytes 2359296 | tf_op jit(solution)/shard_map/all_gather | solution.py:117
  175.0 39.2 %copy-start.72 = (f32[64]{0:T(128)}, f32[64]{0:T(128)S(1)}, u32[]{:S(2)}) copy-start(f32[64]{0:T(128)S(1)} %get-tuple-element.190) | copy-start | bytes 772
  175.1 39.2 %copy-start.73 = (f32[64]{0:T(128)}, f32[64]{0:T(128)S(1)}, u32[]{:S(2)}) copy-start(f32[64]{0:T(128)S(1)} %get-tuple-element.193) | copy-start | bytes 772
  175.1 39.2 %copy-start.74 = (f32[64]{0:T(128)}, f32[64]{0:T(128)S(1)}, u32[]{:S(2)}) copy-start(f32[64]{0:T(128)S(1)} %get-tuple-element.195) | copy-start | bytes 772
  175.1 39.2 %copy-start.75 = (f32[64]{0:T(128)}, f32[64]{0:T(128)S(1)}, u32[]{:S(2)}) copy-start(f32[64]{0:T(128)S(1)} %get-tuple-element.198) | copy-start | bytes 772
  219.9 222.4 %copy-start.77 = (f32[64]{0:T(128)}, f32[64]{0:T(128)S(1)}, u32[]{:S(2)}) copy-start(f32[64]{0:T(128)S(1)} %get-tuple-element.179) | copy-start | bytes 772
  221.9 198.0 %all-gather.24.cloned.1.call-start = ((), (), s32[]{:S(2)}) async-start(), calls=%async_computation.20 | async-start | bytes 2359296 | tf_op jit(solution)/shard_map/all_gather | solution.py:117
  222.7 223.0 %copy-start.79 = (f32[64]{0:T(128)}, f32[64]{0:T(128)S(1)}, u32[]{:S(2)}) copy-start(f32[64]{0:T(128)S(1)} %get-tuple-element.166) | copy-start | bytes 772
  225.9 241.2 %reduce-scatter.17.cloned.1.call-start = ((), (), s32[]{:S(2)}) async-start(), calls=%async_computation.21 | async-start | bytes 2359296 | tf_op jit(solution)/shard_map/reduce_scatter | solution.py:121
  435.2 69.0 %reduce-scatter.15.cloned.1.call-start = ((), (), s32[]{:S(2)}) async-start(), calls=%async_computation.18 | async-start | bytes 2359296 | tf_op jit(solution)/shard_map/reduce_scatter | solution.py:121
  441.5 107.9 %all-gather.26.cloned.1.call-start = ((), (), s32[]{:S(2)}) async-start(), calls=%async_computation.22 | async-start | bytes 2359296 | tf_op jit(solution)/shard_map/all_gather | solution.py:117
  517.7 86.7 %reduce-scatter.27.cloned.1.call-start = ((), (), s32[]{:S(2)}) async-start(), calls=%async_computation.31 | async-start | bytes 5242880
  528.0 128.0 %reduce-scatter.19.cloned.1.call-start = ((), (), s32[]{:S(2)}) async-start(), calls=%async_computation.23 | async-start | bytes 2359296 | tf_op jit(solution)/shard_map/reduce_scatter | solution.py:121
  566.1 121.5 %reduce-scatter.25.cloned.1.call-start = ((), (), s32[]{:S(2)}) async-start(), calls=%async_computation.30 | async-start | bytes 1310720
  573.5 160.8 %reduce-scatter.21.cloned.1.call-start = ((), (), s32[]{:S(2)}) async-start(), calls=%async_computation.25 | async-start | bytes 3932160 | tf_op jit(solution)/shard_map/reduce_scatter | solution.py:250
  578.9 244.8 %reduce-scatter.23.cloned.1.call-start = ((), (), s32[]{:S(2)}) async-start(), calls=%async_computation.26 | async-start | bytes 10485760 | tf_op jit(solution)/shard_map/reduce_scatter | solution.py:250
  604.4 83.1 %all-to-all-start.4 = ((bf16[4,1024,128]{1,2,0:T(8,128)(2,1)}), bf16[4,1024,128]{1,2,0:T(8,128)(2,1)}, u32[]{:S(2)}, u32[]{:S(2)}) async-start(bf16[4,1024,128]{1,2,0:T(8,128)(2,1)} %bitcast.467), calls=%async_computation.10 | async-start | bytes 2097152 | tf_op jit(solution)/shard_map/all_to_all | solution.py:275
  609.7 226.9 %all-gather.22.cloned.1.call-start = ((), (), s32[]{:S(2)}) async-start(), calls=%async_computation.19 | async-start | bytes 3145728 | tf_op jit(solution)/shard_map/all_gather | solution.py:356
  615.5 40.4 %copy-start.67 = (f32[64]{0:T(128)S(1)}, f32[64]{0:T(128)}, u32[]{:S(2)}) copy-start(f32[64]{0:T(128)} %copy-done.66) | copy-start | bytes 772
  687.5 49.1 %all-to-all-start.2 = ((bf16[4,256,128]{1,2,0:T(8,128)(2,1)}), bf16[4,256,128]{1,2,0:T(8,128)(2,1)S(1)}, u32[]{:S(2)}, u32[]{:S(2)}) async-start(bf16[4,256,128]{1,2,0:T(8,128)(2,1)} %bitcast.475), calls=%async_computation.7 | async-start | bytes 524288 | tf_op jit(solution)/shard_map/all_to_all | solution.py:275
  736.6 22.0 %all-to-all-start.1 = ((bf16[4,128,768]{1,2,0:T(8,128)(2,1)}), bf16[4,128,768]{1,2,0:T(8,128)(2,1)}, u32[]{:S(2)}, u32[]{:S(2)}) async-start(bf16[4,128,768]{1,2,0:T(8,128)(2,1)} %copy.248), calls=%async_computation.6 | async-start | bytes 1572864 | tf_op jit(solution)/shard_map/all_to_all | solution.py:253
  741.8 235.5 %all-reduce.5.cloned.1.call-start = ((), (), s32[]{:S(2)}) async-start(), calls=%async_computation.27 | async-start | bytes 262144 | tf_op jit(solution)/shard_map/psum | solution.py:346
  823.7 174.7 %all-to-all-start.3 = ((bf16[4,128,2048]{2,1,0:T(8,128)(2,1)}), bf16[4,128,2048]{2,1,0:T(8,128)(2,1)}, u32[]{:S(2)}, u32[]{:S(2)}) async-start(bf16[4,128,2048]{2,1,0:T(8,128)(2,1)} %bitcast.454), calls=%async_computation.9 | async-start | bytes 4194304 | tf_op jit(solution)/shard_map/all_to_all | solution.py:253
  829.0 160.4 %all-gather.28.cloned.1.call-start = ((), (), s32[]{:S(2)}) async-start(), calls=%async_computation.24 | async-start | bytes 3145728 | tf_op jit(solution)/shard_map/all_gather | solution.py:356
  (127 other events, 604.6 us)
Sparse Core Ops, SparseCore 0:
  10.4 27.7 all-gather.29
  40.4 29.0 all-gather.13
  72.0 43.4 all-gather.15
  143.3 69.2 reduce-scatter.12
  214.8 54.1 all-gather.31
  271.3 87.6 all-gather.19
  360.6 29.0 all-gather.17
  391.3 28.5 all-gather.23
  435.3 31.7 reduce-scatter.16
  469.8 34.3 reduce-scatter.14
  517.8 31.5 all-gather.25
  552.2 52.1 reduce-scatter.26
  607.4 48.4 reduce-scatter.18
  659.5 27.9 reduce-scatter.24
  690.4 43.9 reduce-scatter.20
  737.3 86.3 reduce-scatter.22
  825.7 10.8 all-gather.21
  843.5 133.7 all-reduce.4
  979.4 9.9 all-gather.27

commit v2 on v1

--- a/solution.py
+++ b/solution.py
@@ -1,6 +1,10 @@
+import functools
+
 import jax
 import jax.numpy as jnp
 from jax import lax
+from jax.experimental import pallas as pl
+from jax.experimental.pallas import tpu as pltpu
 from jax.sharding import PartitionSpec as P
 
 HD = 128
@@ -113,14 +117,478 @@
     return (grad_current, grad_weight, jnp.sum(grad_table, 0))
 
 
-def team_gather(value):
-    return lax.all_gather(value, TEAM, axis=0, tiled=True)
-
-
-def team_sum(value, kind=jnp.bfloat16):
-    return lax.psum_scatter(
-        value.astype(kind), TEAM, scatter_dimension=0, tiled=True
-    ).astype(jnp.float32)
+def greet(partners):
+    barrier = pltpu.get_barrier_semaphore()
+    for partner in partners:
+        pl.semaphore_signal(
+            barrier, inc=1, device_id=partner, device_id_type=pl.DeviceIdType.MESH
+        )
+    pl.semaphore_wait(barrier, len(partners))
+
+
+def send(source, target, sent, received, device):
+    pltpu.make_async_remote_copy(
+        src_ref=source,
+        dst_ref=target,
+        send_sem=sent,
+        recv_sem=received,
+        device_id=device,
+        device_id_type=pl.DeviceIdType.MESH,
+    ).start()
+
+
+def landed(block, semaphore):
+    pltpu.make_async_copy(block, block, semaphore).wait()
+
+
+def ring(owners, cores):
+    here = lax.axis_index("ctx")
+    core = lax.axis_index("tensor")
+    right, left = lax.rem(here + 1, owners), lax.rem(here + owners - 1, owners)
+    return here, core, cores - 1 - core, right, left
+
+
+def gather_first(values, outs, sems, owners, cores):
+    local, sent_right, sent_left, sent_pair, came, came_pair = sems
+    here, core, pair, right, left = ring(owners, cores)
+    for i, (value, out) in enumerate(zip(values, outs)):
+        target = out.at[here, core]
+
+        @pl.when(here < owners - 1)
+        def _():
+            send(value, target, sent_right.at[i, here], came.at[i, here], {"ctx": right})
+
+        @pl.when(here > 0)
+        def _():
+            send(value, target, sent_left.at[i, here], came.at[i, here], {"ctx": left})
+
+        send(value, target, sent_pair.at[i, here], came_pair.at[i, here], {"tensor": pair})
+        pltpu.make_async_copy(value, target, local.at[i]).start()
+
+
+def gather_rest(values, outs, sems, owners, cores):
+    local, sent_right, sent_left, sent_pair, came, came_pair = sems
+    here, core, pair, right, left = ring(owners, cores)
+
+    def arrive(i, out, block, onward, sent, device):
+        held = out.at[block, core]
+        landed(held, came.at[i, block])
+
+        @pl.when(onward)
+        def _():
+            send(held, held, sent.at[i, block], came.at[i, block], device)
+
+        send(held, held, sent_pair.at[i, block], came_pair.at[i, block], {"tensor": pair})
+
+    for step in range(1, owners):
+        for i, out in enumerate(outs):
+
+            @pl.when(here >= step)
+            def _():
+                arrive(i, out, here - step, here < owners - 1, sent_right, {"ctx": right})
+
+            @pl.when(here + step < owners)
+            def _():
+                arrive(i, out, here + step, here > 0, sent_left, {"ctx": left})
+
+    for i, (value, out) in enumerate(zip(values, outs)):
+        pltpu.make_async_copy(value, out.at[here, core], local.at[i]).wait()
+        for block in range(owners):
+            landed(out.at[block, pair], came_pair.at[i, block])
+            landed(out.at[block, core], sent_pair.at[i, block])
+
+            @pl.when((here < owners - 1) & (block <= here))
+            def _():
+                landed(out.at[block, core], sent_right.at[i, block])
+
+            @pl.when((here > 0) & (block >= here))
+            def _():
+                landed(out.at[block, core], sent_left.at[i, block])
+
+
+def gather_sems(amount, owners):
+    return [pltpu.SemaphoreType.DMA((amount,))] + [
+        pltpu.SemaphoreType.DMA((amount, owners)) for _ in range(5)
+    ]
+
+
+def line_partners(owners, cores):
+    here, core, pair, right, left = ring(owners, cores)
+    return [{"ctx": right}, {"ctx": left}, {"tensor": pair}]
+
+
+def gather_kernel(amount, owners, cores, *refs):
+    values, outs, sems = refs[:amount], refs[amount : 2 * amount], refs[2 * amount :]
+    greet(line_partners(owners, cores))
+    gather_first(values, outs, sems, owners, cores)
+    gather_rest(values, outs, sems, owners, cores)
+
+
+ANY = pl.BlockSpec(memory_space=pl.ANY)
+INSIDE = pl.BlockSpec(memory_space=pltpu.VMEM)
+
+
+def params(collective_id):
+    return pltpu.CompilerParams(
+        collective_id=collective_id, has_side_effects=True, vmem_limit_bytes=48 << 20
+    )
+
+
+def cost(micros):
+    return pl.CostEstimate(flops=0, transcendentals=0, bytes_accessed=int(micros * 3.0e6))
+
+
+def team_gather(collective_id, *values):
+    owners, cores = lax.axis_size("ctx"), lax.axis_size("tensor")
+    amount = len(values)
+    outs = pl.pallas_call(
+        functools.partial(gather_kernel, amount, owners, cores),
+        out_shape=[jax.ShapeDtypeStruct((owners, cores, *v.shape), v.dtype) for v in values],
+        in_specs=[ANY] * amount,
+        out_specs=[ANY] * amount,
+        scratch_shapes=gather_sems(amount, owners),
+        compiler_params=params(collective_id),
+        cost_estimate=cost(20 * amount),
+        name="team_gather",
+    )(*values)
+    return [o.reshape(-1, v.shape[1]) for o, v in zip(outs, values)]
+
+
+def swap_kernel(owners, value, out, sent, came):
+    here = lax.axis_index("ctx")
+    others = [lax.rem(here + step, owners) for step in range(1, owners)]
+    greet([{"ctx": other} for other in others])
+    out[here] = value[...]
+    for other in others:
+        send(value, out.at[here], sent.at[other], came.at[here], {"ctx": other})
+    for other in others:
+        landed(out.at[other], came.at[other])
+        landed(value, sent.at[other])
+
+
+def team_swap(collective_id, value):
+    owners = lax.axis_size("ctx")
+    return pl.pallas_call(
+        functools.partial(swap_kernel, owners),
+        out_shape=jax.ShapeDtypeStruct((owners, *value.shape), value.dtype),
+        in_specs=[INSIDE],
+        out_specs=INSIDE,
+        scratch_shapes=[pltpu.SemaphoreType.DMA((owners,))] * 2,
+        compiler_params=params(collective_id),
+        cost_estimate=cost(3),
+        name="team_swap",
+    )(value)
+
+
+def plane(index, shards_in):
+    across_x = index + 1 - 2 * lax.rem(index, 2)
+    return across_x, lax.rem(index + 2, shards_in), lax.rem(across_x + 2, shards_in)
+
+
+def open_kernel(shards_in, owners, cores, *refs):
+    value, w_query, w_key, w_value, w_output, out, qkv, out_w = refs[:8]
+    own_sem, sent_w, came_w, passed_w = refs[8:12]
+    sems = refs[12:]
+    index = lax.axis_index("shard")
+    here = lax.axis_index("ctx")
+    depth = w_query.shape[0]
+    count = w_query.shape[1] // owners
+    columns = pl.ds(pl.multiple_of(here * count, count), count)
+    sources = [w.at[:, columns] for w in (w_query, w_key, w_value)] + [w_output.at[columns, :]]
+
+    def target(weight, block):
+        if weight == 3:
+            wide = w_output.shape[1]
+            return out_w.at[:, pl.ds(pl.multiple_of(block * wide, wide), wide)]
+        rows = pl.ds(pl.multiple_of(block * depth, depth), depth)
+        return qkv.at[rows, pl.ds(weight * count, count)]
+
+    others = [lax.rem(index + step, shards_in) for step in range(1, shards_in)]
+    greet([{"shard": other} for other in others] + line_partners(owners, cores))
+    square = shards_in == 4
+    near = plane(index, shards_in)[:2] if square else others
+    for weight in range(4):
+        for other in near:
+            send(
+                sources[weight],
+                target(weight, index),
+                sent_w.at[weight, other],
+                came_w.at[weight, index],
+                {"shard": other},
+            )
+    gather_first([value], [out], sems, owners, cores)
+    for weight in range(4):
+        pltpu.make_async_copy(
+            sources[weight], target(weight, index), own_sem.at[weight]
+        ).start()
+    if square:
+        across_x, across_y, far = plane(index, shards_in)
+        for weight, source, device in (
+            (0, across_x, across_y),
+            (2, across_y, across_x),
+            (1, across_x, across_y),
+            (3, across_y, across_x),
+        ):
+            held = target(weight, source)
+            landed(held, came_w.at[weight, source])
+            send(
+                held, held, passed_w.at[weight], came_w.at[weight, source], {"shard": device}
+            )
+    gather_rest([value], [out], sems, owners, cores)
+    for weight in range(4):
+        pltpu.make_async_copy(
+            sources[weight], target(weight, index), own_sem.at[weight]
+        ).wait()
+        for other in near:
+            landed(sources[weight], sent_w.at[weight, other])
+    if square:
+        for weight, source in ((0, across_y), (2, across_x), (1, across_y), (3, across_x)):
+            landed(target(weight, source), came_w.at[weight, source])
+        for weight in range(4):
+            landed(target(weight, far), came_w.at[weight, far])
+            landed(sources[weight], passed_w.at[weight])
+    else:
+        for weight in range(4):
+            for other in others:
+                landed(target(weight, other), came_w.at[weight, other])
+
+
+def open_team(collective_id, value, weights):
+    shards_in, owners, cores = [lax.axis_size(a) for a in ("shard", "ctx", "tensor")]
+    depth = weights[0].shape[0]
+    count = weights[0].shape[1] // owners
+    out, qkv, out_w = pl.pallas_call(
+        functools.partial(open_kernel, shards_in, owners, cores),
+        out_shape=[
+            jax.ShapeDtypeStruct((owners, cores, *value.shape), value.dtype),
+            jax.ShapeDtypeStruct((shards_in * depth, 3 * count), value.dtype),
+            jax.ShapeDtypeStruct((count, shards_in * weights[3].shape[1]), value.dtype),
+        ],
+        in_specs=[ANY] * 5,
+        out_specs=[ANY] * 3,
+        scratch_shapes=[
+            pltpu.SemaphoreType.DMA((4,)),
+            pltpu.SemaphoreType.DMA((4, shards_in)),
+            pltpu.SemaphoreType.DMA((4, shards_in)),
+            pltpu.SemaphoreType.DMA((4,)),
+        ]
+        + gather_sems(1, owners),
+        compiler_params=params(collective_id),
+        cost_estimate=cost(40),
+        name="open_team",
+    )(value, *weights)
+    return out.reshape(-1, value.shape[1]), qkv, out_w
+
+
+def scatter_kernel(amount, owners, cores, *refs):
+    parts, outs = refs[:amount], refs[amount : 2 * amount]
+    pairs, halves, from_left, from_right = [
+        refs[k * amount : (k + 1) * amount] for k in range(2, 6)
+    ]
+    total, sent_pair, came_pair, sent, came_left, came_right = refs[6 * amount :]
+    here, core, pair, right, left = ring(owners, cores)
+    greet(line_partners(owners, cores))
+    order = [k // 2 if k % 2 else owners - 1 - k // 2 for k in range(owners)]
+    for i in range(amount):
+        for block in order:
+            send(
+                parts[i].at[block, pair],
+                pairs[i].at[block],
+                sent_pair.at[i, block],
+                came_pair.at[i, block],
+                {"tensor": pair},
+            )
+
+    def add_up(i, block, more, arrived, came):
+        landed(pairs[i].at[block], came_pair.at[i, block])
+        total[...] = parts[i][block, core].astype(jnp.float32) + pairs[i][block].astype(
+            jnp.float32
+        )
+
+        @pl.when(more)
+        def _():
+            landed(arrived[i].at[block], came.at[i, block])
+            total[...] += arrived[i][block].astype(jnp.float32)
+
+    def pass_on(i, block, more, arrived, came, device):
+        add_up(i, block, more, arrived, came)
+        halves[i][block] = total[...].astype(halves[i].dtype)
+        send(
+            halves[i].at[block],
+            arrived[i].at[block],
+            sent.at[i, block],
+            came.at[i, block],
+            {"ctx": device},
+        )
+
+    for step in range(2 * owners - 2):
+        for i in range(amount):
+            rightward = owners - 1 - (step - here)
+            leftward = step - (owners - 1 - here)
+
+            @pl.when((rightward > here) & (step >= here))
+            def _():
+                pass_on(i, rightward, here > 0, from_left, came_left, right)
+
+            @pl.when((leftward >= 0) & (leftward < here))
+            def _():
+                pass_on(i, leftward, here < owners - 1, from_right, came_right, left)
+
+    for i in range(amount):
+        add_up(i, here, here > 0, from_left, came_left)
+
+        @pl.when(here < owners - 1)
+        def _():
+            landed(from_right[i].at[here], came_right.at[i, here])
+            total[...] += from_right[i][here].astype(jnp.float32)
+
+        outs[i][...] = total[...]
+    for i in range(amount):
+        for block in range(owners):
+            landed(pairs[i].at[block], sent_pair.at[i, block])
+
+            @pl.when(block != here)
+            def _():
+                landed(halves[i].at[block], sent.at[i, block])
+
+
+def team_sum(collective_id, *values):
+    owners, cores = lax.axis_size("ctx"), lax.axis_size("tensor")
+    amount = len(values)
+    width = values[0].shape[1]
+    mine = values[0].shape[0] // (owners * cores)
+    blocks = [pltpu.VMEM((owners, mine, width), v.dtype) for v in values]
+    return pl.pallas_call(
+        functools.partial(scatter_kernel, amount, owners, cores),
+        out_shape=[jax.ShapeDtypeStruct((mine, width), jnp.float32)] * amount,
+        in_specs=[INSIDE] * amount,
+        out_specs=[INSIDE] * amount,
+        scratch_shapes=blocks * 4
+        + [pltpu.VMEM((mine, width), jnp.float32)]
+        + [pltpu.SemaphoreType.DMA((amount, owners)) for _ in range(5)],
+        compiler_params=params(collective_id),
+        cost_estimate=cost(20 * amount),
+        name="team_sum",
+    )(*[v.reshape(owners, cores, mine, width) for v in values])
+
+
+def close_kernel(amount, shards_in, owners, cores, *refs):
+    values, mixed = refs[:amount], refs[amount]
+    outs, summed = refs[amount + 1 : 2 * amount + 1], refs[2 * amount + 1]
+    pairs, half, quarters, blocks, local, sent, came = refs[2 * amount + 2 : 2 * amount + 9]
+    sent_c, came_c, sent_s, came_s, sent_b, came_b = refs[2 * amount + 9 :]
+    here, core, pair, right, left = ring(owners, cores)
+    index = lax.axis_index("shard")
+    around = [lax.rem(here + step, owners) for step in range(1, owners)]
+    others = [lax.rem(index + step, shards_in) for step in range(1, shards_in)]
+    greet(
+        [{"tensor": pair}]
+        + [{"ctx": other} for other in around]
+        + [{"shard": other} for other in others]
+    )
+    wide = mixed.shape[1] // cores
+    thin = wide // owners
+    send(
+        mixed.at[:, pl.ds(pl.multiple_of(pair * wide, wide), wide)],
+        pairs,
+        sent.at[amount],
+        came.at[amount],
+        {"tensor": pair},
+    )
+    for i in range(amount):
+        target = outs[i].at[:, core]
+        send(values[i], target, sent.at[i], came.at[i], {"tensor": pair})
+        pltpu.make_async_copy(values[i], target, local.at[i]).start()
+    landed(pairs, came.at[amount])
+    half[...] = mixed[:, pl.ds(pl.multiple_of(core * wide, wide), wide)] + pairs[...]
+    for other in around:
+        send(
+            half.at[:, pl.ds(pl.multiple_of(other * thin, thin), thin)],
+            quarters.at[here],
+            sent_c.at[other],
+            came_c.at[here],
+            {"ctx": other},
+        )
+    total = half[:, pl.ds(pl.multiple_of(here * thin, thin), thin)]
+    for other in around:
+        landed(quarters.at[other], came_c.at[other])
+        total += quarters[other]
+    blocks[index] = total
+    for other in others:
+        send(
+            blocks.at[index], blocks.at[index], sent_s.at[other], came_s.at[index], {"shard": other}
+        )
+    for other in others:
+        landed(blocks.at[other], came_s.at[other])
+    total = blocks[0]
+    for block in range(1, shards_in):
+        total += blocks[block]
+
+    def place(owner, half_of):
+        return summed.at[half_of * owners + owner]
+
+    summed[core * owners + here] = total
+    for other in around:
+        send(place(here, core), place(here, core), sent_b.at[other], came_b.at[here, core], {"ctx": other})
+    send(place(here, core), place(here, core), sent_b.at[here], came_b.at[here, core], {"tensor": pair})
+    for other in around:
+        landed(place(other, core), came_b.at[other, core])
+        send(
+            place(other, core),
+            place(other, core),
+            sent_b.at[owners + other],
+            came_b.at[other, core],
+            {"tensor": pair},
+        )
+    for owner in range(owners):
+        landed(place(owner, pair), came_b.at[owner, pair])
+        landed(place(owner, core), sent_b.at[owner])
+    for other in around:
+        landed(place(other, core), sent_b.at[owners + other])
+        landed(quarters.at[other], sent_c.at[other])
+    for other in others:
+        landed(blocks.at[other], sent_s.at[other])
+    landed(pairs, sent.at[amount])
+    for i in range(amount):
+        target = outs[i].at[:, core]
+        landed(outs[i].at[:, pair], came.at[i])
+        landed(target, sent.at[i])
+        pltpu.make_async_copy(values[i], target, local.at[i]).wait()
+
+
+def close_team(collective_id, mixed, *values):
+    shards_in, owners, cores = [lax.axis_size(a) for a in ("shard", "ctx", "tensor")]
+    amount = len(values)
+    height, width = mixed.shape
+    thin = width // (cores * owners)
+    out = pl.pallas_call(
+        functools.partial(close_kernel, amount, shards_in, owners, cores),
+        out_shape=[
+            jax.ShapeDtypeStruct((v.shape[0], cores, *v.shape[1:]), v.dtype) for v in values
+        ]
+        + [jax.ShapeDtypeStruct((cores * owners, height, thin), jnp.float32)],
+        in_specs=[ANY] * amount + [INSIDE],
+        out_specs=[ANY] * amount + [INSIDE],
+        scratch_shapes=[
+            pltpu.VMEM((height, width // cores), jnp.float32),
+            pltpu.VMEM((height, width // cores), jnp.float32),
+            pltpu.VMEM((owners, height, thin), jnp.float32),
+            pltpu.VMEM((shards_in, height, thin), jnp.float32),
+            pltpu.SemaphoreType.DMA((amount,)),
+            pltpu.SemaphoreType.DMA((amount + 1,)),
+            pltpu.SemaphoreType.DMA((amount + 1,)),
+            pltpu.SemaphoreType.DMA((owners,)),
+            pltpu.SemaphoreType.DMA((owners,)),
+            pltpu.SemaphoreType.DMA((shards_in,)),
+            pltpu.SemaphoreType.DMA((shards_in,)),
+            pltpu.SemaphoreType.DMA((2 * owners,)),
+            pltpu.SemaphoreType.DMA((owners, cores)),
+        ],
+        compiler_params=params(collective_id),
+        cost_estimate=cost(10),
+        name="close_team",
+    )(*values, mixed)
+    return out[-1].transpose(1, 0, 2).reshape(height, width), *out[:-1]
 
 
 def shards(
@@ -158,14 +626,7 @@
     def rows(weight, count):
         return lax.dynamic_slice_in_dim(weight, here * count, count, 0)
 
-    qkv = jnp.concatenate([columns(w, head_cols) for w in (w_query, w_key, w_value)], 1)
-    qkv = lax.all_gather(qkv, "shard", axis=0, tiled=True)
-    out_w = lax.all_gather(rows(w_output, head_cols), "shard", axis=0)
-    out_w = out_w.transpose(1, 0, 2).reshape(head_cols, width)
-    gate_up = jnp.concatenate([columns(w, units) for w in (w_gate, w_up)], 1)
-    gate_up = lax.all_gather(gate_up, "shard", axis=0, tiled=True)
-    down = lax.all_gather(rows(w_down, units), "shard", axis=0)
-    down = down.transpose(1, 0, 2).reshape(units, width)
+    down = lax.all_gather(rows(w_down, units).T, "shard", axis=0, tiled=True)
 
     order = jnp.arange(group_rows, dtype=jnp.int32)
     within = order % mine
@@ -185,7 +646,8 @@
 
     local_dest = destination - lax.axis_index("shard") * group_rows
     heads_of_runs = local_dest.reshape(owners, run_rows)[:, 0]
-    every = lax.all_gather(heads_of_runs, "ctx", axis=0)
+    every = team_swap(6, jnp.broadcast_to(jnp.pad(heads_of_runs, (0, 128 - owners)), (8, 128)))
+    every = every[:, 0, :owners]
     sent = jnp.sum(jnp.where(every // rows_here == here, every % rows_here, 0), 1) + core * part
     packed = jnp.concatenate(
         [lax.dynamic_slice_in_dim(cotangent, sent[c], part, 0) for c in range(owners)], 0
@@ -207,7 +669,12 @@
         current, mix_weight[0], mix_static[0]
     )
     attn_normed, attn_scaled = norm_rows(branch_in)
-    attn_input = team_gather(attn_normed.astype(jnp.bfloat16))
+    attn_input, qkv, out_w = open_team(
+        0, attn_normed.astype(jnp.bfloat16), (w_query, w_key, w_value, w_output)
+    )
+    gate_up = jnp.concatenate([columns(w, units) for w in (w_gate, w_up)], 1)
+    attn_input, gate_up = lax.optimization_barrier((attn_input, gate_up))
+    gate_up = lax.all_gather(gate_up, "shard", axis=0, tiled=True)
     cosine, sine = angles(position, HD)
     lin = dot(attn_input, qkv).reshape(group_rows, 3, heads, HD)
     queries = rotate(lin[:, 0], cosine, sine).astype(jnp.bfloat16)
@@ -222,21 +689,22 @@
     probs_low = probs.astype(jnp.bfloat16)
     attended = jnp.einsum("hqk,khd->qhd", probs_low, values, preferred_element_type=jnp.float32)
     attended = attended.reshape(group_rows, head_cols).astype(jnp.bfloat16)
-    attn_out = team_sum(dot(attended, out_w), jnp.float32)
+    [attn_out] = team_sum(1, dot(attended, out_w))
 
     middle = combine(current, attn_out, table_one)
     branch_two, table_two, active_two, normed_two, scaled_two = mixing(
         middle, mix_weight[1], mix_static[1]
     )
     ffn_normed, ffn_scaled = norm_rows(branch_two)
-    ffn_input = team_gather(ffn_normed.astype(jnp.bfloat16))
-    grad_ffn_out = team_gather(branch_grad(table_two, grad_top).astype(jnp.bfloat16))
+    ffn_input, grad_ffn_out = team_gather(
+        2, ffn_normed.astype(jnp.bfloat16), branch_grad(table_two, grad_top).astype(jnp.bfloat16)
+    )
     both = dot(ffn_input, gate_up)
     gate, upward = both[:, :units], both[:, units:]
     sigma = jax.nn.sigmoid(gate)
     hidden = (gate * sigma * upward).astype(jnp.bfloat16)
-    ffn_out = team_sum(dot(hidden, down))
-    grad_hidden = contract_cols(grad_ffn_out, down)
+    ffn_part = contract_cols(hidden, down).astype(jnp.bfloat16)
+    grad_hidden = dot(grad_ffn_out, down)
     grad_both = jnp.concatenate(
         [
             (grad_hidden * upward * sigma * (1.0 + gate * (1.0 - sigma))).astype(jnp.bfloat16),
@@ -244,40 +712,31 @@
         ],
         1,
     )
-    grad_ffn_input = team_sum(contract_cols(grad_both, gate_up))
-
-    def to_owner_rows(partial):
-        summed = lax.psum_scatter(
-            partial.astype(jnp.bfloat16), "shard", scatter_dimension=0, tiled=True
-        )
+    ffn_input_part = contract_cols(grad_both, gate_up).astype(jnp.bfloat16)
+    down_part = contract_rows(grad_ffn_out, hidden).astype(jnp.bfloat16)
+    gate_up_part = contract_rows(ffn_input, grad_both).astype(jnp.bfloat16)
+    ffn_part, ffn_input_part, down_part, gate_up_part = lax.optimization_barrier(
+        (ffn_part, ffn_input_part, down_part, gate_up_part)
+    )
+
+    def shard_sum(partial):
+        return lax.psum_scatter(partial, "shard", scatter_dimension=0, tiled=True)
+
+    def to_owner_rows(summed):
         moved = lax.all_to_all(summed, "ctx", split_axis=0, concat_axis=0, tiled=True)
         return moved.reshape(owners, summed.shape[0] // owners, summed.shape[1])
 
-    def row_parts(moved, amount):
-        split = moved.reshape(owners, moved.shape[1], amount, moved.shape[2] // amount)
-        return [
-            split[:, :, i].transpose(1, 0, 2).reshape(moved.shape[1], -1).astype(jnp.float32)
-            for i in range(amount)
-        ]
-
-    def to_owner_columns(left, right):
-        shard_total = lax.axis_size("shard")
-        partial = jnp.einsum(
-            "th,tsd->shd",
-            left,
-            right.reshape(group_rows, shard_total, -1),
-            preferred_element_type=jnp.float32,
-        )
-        summed = lax.psum_scatter(
-            partial.astype(jnp.bfloat16), "shard", scatter_dimension=0, tiled=False
-        )
-        split = summed.reshape(left.shape[1], owners, -1).transpose(1, 0, 2)
-        moved = lax.all_to_all(split, "ctx", split_axis=0, concat_axis=0, tiled=True)
-        return moved.reshape(owners * left.shape[1], -1).astype(jnp.float32)
-
-    grad_down = to_owner_columns(hidden, grad_ffn_out)
-    grad_gate, grad_up = row_parts(to_owner_rows(contract_rows(ffn_input, grad_both)), 2)
-
+    def row_part(moved, first, count):
+        cut = moved[:, :, first : first + count]
+        return cut.transpose(1, 0, 2).reshape(moved.shape[1], -1).astype(jnp.float32)
+
+    def column_part(moved, first, count):
+        cut = moved[:, :, first : first + count]
+        return cut.transpose(0, 2, 1).reshape(-1, moved.shape[1]).astype(jnp.float32)
+
+    down_sum = shard_sum(down_part)
+    gate_up_sum = shard_sum(gate_up_part)
+    ffn_out, grad_ffn_input = team_sum(3, ffn_part, ffn_input_part)
     grad_beta = jnp.sum(grad_top * ffn_out[:, None], -1)
     grad_mixer, grad_middle = combine_back(middle, table_two, grad_top)
     grad_branch_two = norm_back(ffn_normed, ffn_scaled, grad_ffn_input)
@@ -293,7 +752,10 @@
         grad_mixer,
         grad_middle,
     )
-    grad_attn_out = team_gather(branch_grad(table_one, grad_middle).astype(jnp.bfloat16))
+    grad_attn_low, down_sum = lax.optimization_barrier(
+        (branch_grad(table_one, grad_middle).astype(jnp.bfloat16), down_sum)
+    )
+    [grad_attn_out] = team_gather(4, grad_attn_low)
     final = combine(middle, ffn_out, table_two).astype(jnp.bfloat16)
 
     grad_attended = (
@@ -322,11 +784,23 @@
         ],
         1,
     ).astype(jnp.bfloat16)
-    grad_attn_input = team_sum(contract_cols(grad_lin, qkv))
-    grad_output = to_owner_columns(attended, grad_attn_out)
-    grad_query, grad_key, grad_value = row_parts(
-        to_owner_rows(contract_rows(attn_input, grad_lin)), 3
-    )
+    attn_input_part = contract_cols(grad_lin, qkv).astype(jnp.bfloat16)
+    attn_part = jnp.concatenate(
+        [contract_rows(attn_input, grad_lin), contract_rows(grad_attn_out, attended)], 1
+    ).astype(jnp.bfloat16)
+    attn_input_part, attn_part, gate_up_sum = lax.optimization_barrier(
+        (attn_input_part, attn_part, gate_up_sum)
+    )
+    grad_down = column_part(to_owner_rows(down_sum), 0, units)
+    moved = to_owner_rows(gate_up_sum)
+    grad_gate, grad_up = row_part(moved, 0, units), row_part(moved, units, units)
+    attn_sum = shard_sum(attn_part)
+    [grad_attn_input] = team_sum(5, attn_input_part)
+    moved = to_owner_rows(attn_sum)
+    grad_query, grad_key, grad_value = [
+        row_part(moved, i * head_cols, head_cols) for i in range(3)
+    ]
+    grad_output = column_part(moved, 3 * head_cols, head_cols)
 
     grad_beta = jnp.sum(grad_middle * attn_out[:, None], -1)
     grad_mixer, grad_current = combine_back(current, table_one, grad_middle)
@@ -343,22 +817,27 @@
         grad_mixer,
         grad_current,
     )
-    grad_mix_weight, grad_mix_static = lax.psum(
-        (
-            jnp.stack([grad_weight_one, grad_weight_two]),
-            jnp.stack([grad_static_one, grad_static_two]),
-        ),
-        ("shard", "ctx", "tensor"),
-    )
-
-    def all_rows(value):
-        value = value.astype(jnp.bfloat16).reshape(owners, part, stream_total, width)
-        full = lax.all_gather(value, "tensor", axis=1)
-        return full.reshape(rows_here, stream_total, width)
+    statics = jnp.stack([grad_static_one, grad_static_two])
+    mixed = jnp.concatenate(
+        [
+            grad_weight_one.T,
+            grad_weight_two.T,
+            jnp.pad(statics.reshape(1, -1), ((0, 3), (0, width - statics.size))),
+        ],
+        0,
+    )
+
+    def runs(value):
+        return value.astype(jnp.bfloat16).reshape(owners, part, stream_total, width)
+
+    mixed, streams_out, grad_streams = close_team(7, mixed, runs(final), runs(grad_current))
+    tables = 2 * mix_weight.shape[2]
+    grad_mix_weight = mixed[:tables].reshape(2, -1, width).transpose(0, 2, 1)
+    grad_mix_static = mixed[tables, : statics.size].reshape(statics.shape)
 
     return (
-        all_rows(final),
-        all_rows(grad_current),
+        streams_out.reshape(rows_here, stream_total, width),
+        grad_streams.reshape(rows_here, stream_total, width),
         grad_query,
         grad_key,
         grad_value,

time: 1030 us -> 579 us (0.56)
  waiting for transfers between devices: 646 us -> 62.7 us
  Pallas kernels: 0 us -> 259 us
  blocking collectives: 58.7 us -> 0 us
  local copies, waits for them, and re-layouts: 92.6 us -> 56.9 us
  other arithmetic: 65.3 us -> 47.6 us
  matrix products: 96.6 us -> 86.1 us
    pallas_call x0 -> x8, Pallas kernels: none -> 259 us  [the longest x3 132 us: team_sum(): pl.pallas_call(functools.partial(scatter_kernel, amount, owners, cores),...]
    all_gather x9 -> x1, waiting for transfers between devices: 206 us -> 0.01 us  [shards(): down = lax.all_gather(rows(w_down, units).T, 'shard', axis=0, tiled=True)]
    reduce_scatter x6 -> x3, waiting for transfers between devices: 200 us -> 44.5 us  [shard_sum(): return lax.psum_scatter(partial, 'shard', scatter_dimension=0, tiled=True)]
    all_gather x1, waiting for transfers between devices: 83.6 us -> 0.01 us  [shards(): gate_up = lax.all_gather(gate_up, 'shard', axis=0, tiled=True)]
    psum x1 -> x0, waiting for transfers between devices: 82.3 us -> none  [shards(): lax.psum((jnp.stack([grad_weight_one, grad_weight_two]), jnp.stack([grad_...]
    psum x1 -> x0, blocking collectives: 50 us -> none  [shards(): lax.psum((jnp.stack([grad_weight_one, grad_weight_two]), jnp.stack([grad_...]
    unnamed x21 -> x5, waiting for transfers between devices: 37.8 us -> 0.59 us
    all_to_all x1, waiting for transfers between devices: 30 us -> 0.01 us  [shards(): lax.all_to_all(packed, 'ctx', split_axis=0, concat_axis=0, tiled=True)]
  transfers between devices with their start and end apart: 24 -> 9, of which waited for: 21 -> 2; matrix products, arithmetic and copies ran while one was open for 17% -> 19% of each run, Pallas kernels for 0% -> 39%
where the time goes in v2:
time: 579 us; the launch traced here: 569 us
  Pallas kernels  259 us (45%)
  matrix products  86.1 us (15%)
  waiting for transfers between devices  62.7 us (11%)
  local copies, waits for them, and re-layouts  56.9 us (10%)
  other arithmetic  47.6 us (8%)
  between operations  32.1 us (6%)
  starting transfers between devices  24.2 us (4%)
    pallas_call x3, Pallas kernels, team_sum(): pl.pallas_call(functools.partial(scatter_kernel, amount, owners, cores),...  132 us
    pallas_call x2, Pallas kernels, team_gather(): pl.pallas_call(functools.partial(gather_kernel, amount, owners, cores), o...  55 us
    reduce_scatter x3, waiting for transfers between devices, shard_sum(): return lax.psum_scatter(partial, 'shard', scatter_dimension=0, tiled=True)  44.5 us
    pallas_call x1, Pallas kernels, open_team(): pl.pallas_call(functools.partial(open_kernel, shards_in, owners, cores),...  38.1 us
    unnamed x365, local copies, waits for them, and re-layouts  31.5 us
    pallas_call x1, Pallas kernels, close_team(): pl.pallas_call(functools.partial(close_kernel, amount, shards_in, owners,...  25.5 us
    dot_general x4, matrix products, dot(): return jnp.dot(left, right, preferred_element_type=jnp.float32)  25.4 us
    dot_general x4, matrix products, contract_cols(): lax.dot_general(left, right, (((1,), (1,)), ((), ())), preferred_element_...  22.8 us
  transfers between devices with their start and end apart: 9, of which 2 were waited for; matrix products, arithmetic and copies ran while one was open for 19% of the time, Pallas kernels for 39%

profile of v2, /device:TPU:8, one launch (start us, length us, event | category | flops | bytes accessed | tf_op | source)
XLA Modules:
  0.0 568.6 jit_solution(3022326764864032696)
XLA Ops:
  13.8 2.6 broadcast_add_fusion.1
  22.7 38.1 %open_team.1 = (bf16[4,2,64,2048]{3,2,1,0:T(8,128)(2,1)}, bf16[2048,768]{1,0:T(8,128)(2,1)}, bf16[256,2048]{1,0:T(8,128)(2,1)S(1)}) custom-call(bf16[64,2048]{1,0:T(8,128)(2,1)S(1)} %fusion.34.refs_0_, bf16[512,1024]{1,0:T(8,128)(2,1)S(1)} %copy-done.7, bf16[512,1024]{1,0:T(8,128)(2,1)S(1)} %copy-done.8, bf16[512,1024]{1,0:T(8,128)(2,1)S(1)} %copy-done.9, ...), custom_call_target="tpu_custom_call" | custom-call | bytes 120000000 | tf_op jit(solution)/shard_map/open_team/pallas_call | solution.py:360
  62.7 8.1 %team_swap.1 = s32[4,8,128]{2,1,0:T(8,128)S(1)} custom-call(s32[8,128]{1,0:T(8,128)S(1)} %broadcast_in_dim.61.value), custom_call_target="tpu_custom_call" | custom-call | bytes 9000000 | tf_op jit(solution)/shard_map/team_swap/pallas_call | solution.py:271
  81.7 5.6 all-to-all-start
  89.8 4.3 fusion.101
  102.8 3.1 fusion.17.refs_0_
  113.8 42.5 %team_sum.3 = f32[64,2048]{1,0:T(8,128)S(1)} custom-call(f32[4,2,64,2048]{3,2,1,0:T(8,128)S(1)} %copy-done.2), custom_call_target="tpu_custom_call" | custom-call | bytes 60000000 | tf_op jit(solution)/shard_map/team_sum/pallas_call | solution.py:461
  166.5 3.4 broadcast_add_fusion
  171.9 35.2 %team_gather.2 = (bf16[4,2,64,2048]{3,2,1,0:T(8,128)(2,1)S(1)}, bf16[4,2,64,2048]{3,2,1,0:T(8,128)(2,1)S(1)}) custom-call(bf16[64,2048]{1,0:T(8,128)(2,1)S(1)} %fusion.35.refs_0_, bf16[64,2048]{1,0:T(8,128)(2,1)S(1)} %add_convert_fusion.6.refs_1_), custom_call_target="tpu_custom_call" | custom-call | bytes 120000000 | tf_op jit(solution)/shard_map/team_gather/pallas_call | solution.py:244
  208.5 9.4 %fusion.102 = f32[512,2048]{1,0:T(8,128)} fusion(bf16[512,2048]{1,0:T(8,128)(2,1)S(1)} %bitcast.381, bf16[2048,2048]{1,0:T(8,128)(2,1)} %all-gather.3.cloned.1.call-done), kind=kOutput, calls=%fused_computation.341 | convolution fusion | flops 4294967296 | bytes 14680064 | tf_op jit(solution)/shard_map/dot_general | solution.py:48
  217.9 8.6 %multiply_convert_fusion.2 = (bf16[512,1024]{1,0:T(8,128)(2,1)}, bf16[512,1024]{1,0:T(8,128)(2,1)}, bf16[512,1024]{1,0:T(8,128)(2,1)S(1)}) fusion(f32[512,2048]{1,0:T(8,128)} %fusion.102, bf16[512,2048]{1,0:T(8,128)(2,1)} %bitcast.383, bf16[2048,1024]{0,1:T(8,128)(2,1)} %all-gather.5.cloned.1.call-done), kind=kOutput, calls=%fused_computation.50 | convolution fusion | flops 2155872256 | bytes 13631488 | tf_op jit(solution)/shard_map/dot_general | solution.py:48
  227.5 4.4 convolution_convert_fusion.1
  231.9 8.3 %convolution_convert_fusion = bf16[2048,2048]{1,0:T(8,128)(2,1)} fusion(bf16[512,2048]{1,0:T(8,128)(2,1)S(1)} %bitcast.382, bf16[512,1024]{1,0:T(8,128)(2,1)} %get-tuple-element.114, bf16[512,1024]{1,0:T(8,128)(2,1)} %get-tuple-element.113), kind=kOutput, calls=%fused_computation.1 | convolution fusion | flops 4303355904 | bytes 12582912 | tf_op jit(solution)/shard_map/dot_general | solution.py:52
  240.2 6.3 %convolution_convert_fusion.3 = bf16[512,2048]{1,0:T(8,128)(2,1)} fusion(bf16[512,1024]{1,0:T(8,128)(2,1)} %copy-done.171, bf16[2048,1024]{0,1:T(8,128)(2,1)} %all-gather.5.cloned.1.call-done), kind=kOutput, calls=%fused_computation.12 | convolution fusion | flops 2148532224 | bytes 7340032 | tf_op jit(solution)/shard_map/dot_general | solution.py:58
  246.5 9.3 %convolution_convert_fusion.5 = bf16[512,2048]{1,0:T(8,128)(2,1)} fusion(bf16[2048,2048]{1,0:T(8,128)(2,1)} %all-gather.3.cloned.1.call-done, bf16[512,1024]{1,0:T(8,128)(2,1)S(1)} %copy-done.175, bf16[512,1024]{1,0:T(8,128)(2,1)S(1)} %copy-done.174), kind=kOutput, calls=%fused_computation.14 | convolution fusion | flops 4300210176 | bytes 12582912 | tf_op jit(solution)/shard_map/dot_general | solution.py:58
  261.7 42.5 %team_sum.4 = (f32[64,2048]{1,0:T(8,128)S(1)}, f32[64,2048]{1,0:T(8,128)S(1)}) custom-call(bf16[4,2,64,2048]{3,2,1,0:T(8,128)(2,1)S(1)} %bitcast.377, bf16[4,2,64,2048]{3,2,1,0:T(8,128)(2,1)S(1)} %bitcast.378), custom_call_target="tpu_custom_call" | custom-call | bytes 120000000 | tf_op jit(solution)/shard_map/team_sum/pallas_call | solution.py:461
  313.2 19.8 %team_gather.3 = bf16[4,2,64,2048]{3,2,1,0:T(8,128)(2,1)S(1)} custom-call(bf16[64,2048]{1,0:T(8,128)(2,1)S(1)} %fusion.29.refs_0_), custom_call_target="tpu_custom_call" | custom-call | bytes 60000000 | tf_op jit(solution)/shard_map/team_gather/pallas_call | solution.py:244
  350.6 5.1 convolution_convert_fusion.4
  355.8 44.5 %reduce-scatter.6.cloned.1.call-done = bf16[512,2048]{1,0:T(8,128)(2,1)} async-done(((bf16[2048,2048]{1,0:T(8,128)(2,1)}), bf16[512,2048]{1,0:T(8,128)(2,1)}) %reduce-scatter.6.cloned.1.call-update) | async-done | bytes 2097168 | tf_op jit(solution)/shard_map/reduce_scatter | solution.py:723
  402.1 5.5 all-to-all-start.3
  412.4 17.6 %all-to-all-done.3 = bf16[4,128,1024]{2,1,0:T(8,128)(2,1)} async-done(((bf16[4,128,1024]{2,1,0:T(8,128)(2,1)}), bf16[4,128,1024]{2,1,0:T(8,128)(2,1)}, u32[]{:S(2)}, u32[]{:S(2)}) %all-to-all-start.3) | async-done | bytes 1048608 | tf_op jit(solution)/shard_map/all_to_all | solution.py:726
  430.0 8.0 %all-to-all-start.2 = ((bf16[4,128,2048]{2,1,0:T(8,128)(2,1)}), bf16[4,128,2048]{2,1,0:T(8,128)(2,1)}, u32[]{:S(2)}, u32[]{:S(2)}) async-start(bf16[4,128,2048]{2,1,0:T(8,128)(2,1)} %bitcast.423), calls=%async_computation.5 | async-start | bytes 4194304 | tf_op jit(solution)/shard_map/all_to_all | solution.py:726
  441.8 2.4 pad_maximum_fusion.7.refs_0_
  444.2 2.8 convert_bitcast_fusion
  447.0 3.1 copy.160
  450.1 47.3 %team_sum.5 = f32[64,2048]{1,0:T(8,128)S(1)} custom-call(bf16[4,2,64,2048]{3,2,1,0:T(8,128)(2,1)S(1)} %bitcast.375), custom_call_target="tpu_custom_call" | custom-call | bytes 60000000 | tf_op jit(solution)/shard_map/team_sum/pallas_call | solution.py:461
  500.7 3.4 fusion.87
  506.6 4.7 all-to-all-start.1
  511.3 2.9 fusion.11
  515.1 2.9 convolution_bitcast_fusion.1
  518.0 25.5 %close_team.1 = (bf16[4,2,16,4,2048]{4,3,2,1,0:T(4,128)(2,1)S(1)}, bf16[4,2,16,4,2048]{4,3,2,1,0:T(4,128)(2,1)}, f32[8,16,256]{2,1,0:T(8,128)S(1)}) custom-call(bf16[4,16,4,2048]{3,2,1,0:T(4,128)(2,1)S(1)} %pad_maximum_fusion.7.refs_0_, bf16[4,16,4,2048]{3,2,1,0:T(4,128)(2,1)S(1)} %bitcast.374, f32[16,2048]{1,0:T(8,128)S(1)} %select_maximum_fusion.refs_2_), custom_call_target="tpu_custom_call" | custom-call | bytes 30000000 | tf_op jit(solution)/shard_map/close_team/pallas_call | solution.py:564
  556.4 4.1 copy.222
  (515 shorter events, 105.3 us)
Async XLA Ops:
  7.2 201.3 %all-gather.3.cloned.1.call-start = ((), (), s32[]{:S(2)}) async-start(), calls=%async_computation.7 | async-start | bytes 10485760 | tf_op jit(solution)/shard_map/all_gather | solution.py:677
  16.4 142.7 %copy-start.91 = (f32[64]{0:T(128)}, f32[64]{0:T(128)S(1)}, u32[]{:S(2)}) copy-start(f32[64]{0:T(128)S(1)} %get-tuple-element.213) | copy-start | bytes 772
  81.7 79.7 %all-to-all-start = ((bf16[64,4,2048]{2,1,0:T(4,128)(2,1)}), bf16[64,4,2048]{2,1,0:T(4,128)(2,1)}, u32[]{:S(2)}, u32[]{:S(2)}) async-start(bf16[64,4,2048]{2,1,0:T(4,128)(2,1)} %pad_maximum_fusion.6), calls=%async_computation | async-start | bytes 2097152 | tf_op jit(solution)/shard_map/all_to_all | solution.py:655
  87.3 130.6 %all-gather.5.cloned.1.call-start = ((), (), s32[]{:S(2)}) async-start(), calls=%async_computation.8 | async-start | bytes 5242880 | tf_op jit(solution)/shard_map/all_gather | solution.py:629
  89.5 223.7 %reduce-scatter.4.cloned.1.call-start = ((), (), s32[]{:S(2)}) async-start(), calls=%async_computation.9 | async-start | bytes 5242880 | tf_op jit(solution)/shard_map/reduce_scatter | solution.py:723
  113.8 45.3 %copy-start.16 = (f32[4,1,16,4,2048]{4,2,0,3,1:T(8,128)S(1)}, f32[4,1,16,4,2048]{4,2,0,3,1:T(8,128)}, u32[]{:S(2)}) copy-start(f32[4,1,16,4,2048]{4,2,0,3,1:T(8,128)} %copy-done.15) | copy-start | bytes 6291460
  170.5 133.7 %copy-start.90 = (f32[64]{0:T(128)}, f32[64]{0:T(128)S(1)}, u32[]{:S(2)}) copy-start(f32[64]{0:T(128)S(1)} %add_rsqrt_fusion.2) | copy-start | bytes 772
  255.8 144.5 %reduce-scatter.6.cloned.1.call-start = ((), (), s32[]{:S(2)}) async-start(), calls=%async_computation.10 | async-start | bytes 10485760 | tf_op jit(solution)/shard_map/reduce_scatter | solution.py:723
  256.4 247.7 %reduce-scatter.8.cloned.1.call-start = ((), (), s32[]{:S(2)}) async-start(), calls=%async_computation.11 | async-start | bytes 5242880 | tf_op jit(solution)/shard_map/reduce_scatter | solution.py:723
  261.7 42.5 %copy-start.43 = (f32[64,2048]{1,0:T(8,128)S(1)}, f32[64,2048]{1,0:T(8,128)}, u32[]{:S(2)}) copy-start(f32[64,2048]{1,0:T(8,128)} %copy-done.42) | copy-start | bytes 1572868
  261.7 42.8 %copy-start.50 = (bf16[16,4,2048]{2,0,1:T(8,128)(2,1)S(1)}, bf16[16,4,2048]{2,0,1:T(8,128)(2,1)}, u32[]{:S(2)}) copy-start(bf16[16,4,2048]{2,0,1:T(8,128)(2,1)} %copy-done.49) | copy-start | bytes 786436
  261.7 42.8 %copy-start.52 = (bf16[16,4,2048]{2,0,1:T(8,128)(2,1)S(1)}, bf16[16,4,2048]{2,0,1:T(8,128)(2,1)}, u32[]{:S(2)}) copy-start(bf16[16,4,2048]{2,0,1:T(8,128)(2,1)} %copy-done.51) | copy-start | bytes 786436
  261.7 42.8 %copy-start.54 = (bf16[16,4,2048]{2,0,1:T(8,128)(2,1)S(1)}, bf16[16,4,2048]{2,0,1:T(8,128)(2,1)}, u32[]{:S(2)}) copy-start(bf16[16,4,2048]{2,0,1:T(8,128)(2,1)} %copy-done.53) | copy-start | bytes 786436
  355.8 44.8 %copy-start.23 = (f32[64,4,2048]{2,0,1:T(8,128)S(1)}, f32[64,4,2048]{2,0,1:T(8,128)}, u32[]{:S(2)}) copy-start(f32[64,4,2048]{2,0,1:T(8,128)} %copy-done.22) | copy-start | bytes 6291460
  355.8 44.8 %copy-start.92 = (f32[64]{0:T(128)S(1)}, f32[64]{0:T(128)}, u32[]{:S(2)}) copy-start(f32[64]{0:T(128)} %copy-done.91) | copy-start | bytes 772
  355.8 44.8 %copy-start.94 = (f32[64]{0:T(128)S(1)}, f32[64]{0:T(128)}, u32[]{:S(2)}) copy-start(f32[64]{0:T(128)} %copy-done.93) | copy-start | bytes 772
  355.8 44.8 %copy-start.96 = (f32[64]{0:T(128)S(1)}, f32[64]{0:T(128)}, u32[]{:S(2)}) copy-start(f32[64]{0:T(128)} %copy-done.95) | copy-start | bytes 772
  355.8 44.8 %copy-start.98 = (f32[64]{0:T(128)S(1)}, f32[64]{0:T(128)}, u32[]{:S(2)}) copy-start(f32[64]{0:T(128)} %copy-done.97) | copy-start | bytes 772
  355.8 44.8 %copy-start.100 = (f32[64]{0:T(128)S(1)}, f32[64]{0:T(128)}, u32[]{:S(2)}) copy-start(f32[64]{0:T(128)} %copy-done.99) | copy-start | bytes 772
  355.8 44.8 %copy-start.102 = (f32[64]{0:T(128)S(1)}, f32[64]{0:T(128)}, u32[]{:S(2)}) copy-start(f32[64]{0:T(128)} %copy-done.101) | copy-start | bytes 772
  355.8 44.8 %copy-start.104 = (f32[64]{0:T(128)S(1)}, f32[64]{0:T(128)}, u32[]{:S(2)}) copy-start(f32[64]{0:T(128)} %copy-done.103) | copy-start | bytes 772
  355.8 44.8 %copy-start.106 = (f32[64]{0:T(128)S(1)}, f32[64]{0:T(128)}, u32[]{:S(2)}) copy-start(f32[64]{0:T(128)} %copy-done.105) | copy-start | bytes 772
  402.1 27.9 %all-to-all-start.3 = ((bf16[4,128,1024]{2,1,0:T(8,128)(2,1)}), bf16[4,128,1024]{2,1,0:T(8,128)(2,1)}, u32[]{:S(2)}, u32[]{:S(2)}) async-start(bf16[4,128,1024]{2,1,0:T(8,128)(2,1)} %bitcast.439), calls=%async_computation.6 | async-start | bytes 2097152 | tf_op jit(solution)/shard_map/all_to_all | solution.py:726
  430.0 76.6 %all-to-all-start.2 = ((bf16[4,128,2048]{2,1,0:T(8,128)(2,1)}), bf16[4,128,2048]{2,1,0:T(8,128)(2,1)}, u32[]{:S(2)}, u32[]{:S(2)}) async-start(bf16[4,128,2048]{2,1,0:T(8,128)(2,1)} %bitcast.423), calls=%async_computation.5 | async-start | bytes 4194304 | tf_op jit(solution)/shard_map/all_to_all | solution.py:726
  450.1 47.3 %copy-start.41 = (f32[64,2048]{1,0:T(8,128)S(1)}, f32[64,2048]{1,0:T(8,128)}, u32[]{:S(2)}) copy-start(f32[64,2048]{1,0:T(8,128)} %copy-done.40) | copy-start | bytes 1572868
  450.1 47.3 %copy-start.89 = (f32[64]{0:T(128)S(1)}, f32[64]{0:T(128)}, u32[]{:S(2)}) copy-start(f32[64]{0:T(128)} %copy-done.88) | copy-start | bytes 772
  450.1 47.9 %copy-start.21 = (bf16[4,1,16,4,2048]{4,3,2,1,0:T(4,128)(2,1)S(1)}, bf16[4,1,16,4,2048]{4,3,2,1,0:T(4,128)(2,1)}, u32[]{:S(2)}) copy-start(bf16[4,1,16,4,2048]{4,3,2,1,0:T(4,128)(2,1)} %copy-done.20) | copy-start | bytes 3145732
  450.1 47.9 %copy-start.61 = (f32[64,1,2048]{2,0,1:T(8,128)S(1)}, f32[64,1,2048]{2,0,1:T(8,128)}, u32[]{:S(2)}) copy-start(f32[64,1,2048]{2,0,1:T(8,128)} %get-tuple-element.131) | copy-start | bytes 1572868
  450.1 47.9 %copy-start.64 = (f32[64,1,2048]{2,0,1:T(8,128)S(1)}, f32[64,1,2048]{2,0,1:T(8,128)}, u32[]{:S(2)}) copy-start(f32[64,1,2048]{2,0,1:T(8,128)} %get-tuple-element.126) | copy-start | bytes 1572868
  450.1 47.9 %copy-start.65 = (f32[64,1,2048]{2,0,1:T(8,128)S(1)}, f32[64,1,2048]{2,0,1:T(8,128)}, u32[]{:S(2)}) copy-start(f32[64,1,2048]{2,0,1:T(8,128)} %get-tuple-element.129) | copy-start | bytes 1572868
  450.1 47.9 %copy-start.66 = (f32[64,1,2048]{2,0,1:T(8,128)S(1)}, f32[64,1,2048]{2,0,1:T(8,128)}, u32[]{:S(2)}) copy-start(f32[64,1,2048]{2,0,1:T(8,128)} %get-tuple-element.130) | copy-start | bytes 1572868
  506.6 44.7 %all-to-all-start.1 = ((bf16[4,128,1024]{1,2,0:T(8,128)(2,1)}), bf16[4,128,1024]{1,2,0:T(8,128)(2,1)}, u32[]{:S(2)}, u32[]{:S(2)}) async-start(bf16[4,128,1024]{1,2,0:T(8,128)(2,1)} %copy_bitcast_fusion), calls=%async_computation.4 | async-start | bytes 2097152 | tf_op jit(solution)/shard_map/all_to_all | solution.py:726
  (153 other events, 385.3 us)
Sparse Core Ops, SparseCore 0:
  62.0 89.6 all-gather.2
  153.5 52.5 all-gather.4
  256.0 54.6 reduce-scatter.3
  313.9 86.4 reduce-scatter.5
  403.1 52.6 reduce-scatter.7

commit v3 on v2

v3 whole, which is shorter than its diff:
```python
import functools

import jax
import jax.numpy as jnp
import numpy as np
from jax import lax
from jax.experimental import pallas as pl
from jax.experimental.pallas import tpu as pltpu
from jax.sharding import PartitionSpec as P

HD = 128


PRECISE = lax.Precision.HIGHEST
EPSILON = 1e-05
FLOOR_SCORE = -1e30
BLOCKS = 4


def mean_of(value):
    width = value.shape[-1]
    while value.shape[-1] > 128 and value.shape[-1] % 256 == 0:
        half = value.shape[-1] // 2
        value = value[..., :half] + value[..., half:]
    return jnp.sum(value, -1, keepdims=True) * (1.0 / width)


def norm_rows(value):
    centred = value - mean_of(value)
    scaled = lax.rsqrt(mean_of(centred * centred) + EPSILON)
    return (centred * scaled, scaled)


def norm_back(normed, scaled, grad):
    return scaled * (grad - mean_of(grad) - normed * mean_of(grad * normed))


def angles(positions, head_size):
    indices = np.arange(head_size // 2, dtype=np.float64)
    frequency = (10000.0 ** (-(2.0 * indices / head_size))).astype(np.float32)
    turned = positions.astype(jnp.float32)[:, None] * frequency[None, :]
    return (jnp.cos(turned)[:, None, :], jnp.sin(turned)[:, None, :])


def dot(left, right):
    return jnp.dot(left, right, preferred_element_type=jnp.float32)


def contract_rows(left, right):
    return lax.dot_general(
        left, right, (((0,), (0,)), ((), ())), preferred_element_type=jnp.float32
    )


def contract_cols(left, right):
    return lax.dot_general(
        left, right, (((1,), (1,)), ((), ())), preferred_element_type=jnp.float32
    )


def greet(partners):
    barrier = pltpu.get_barrier_semaphore()
    for partner in partners:
        pl.semaphore_signal(
            barrier, inc=1, device_id=partner, device_id_type=pl.DeviceIdType.MESH
        )
    pl.semaphore_wait(barrier, len(partners))


def send(source, target, sent, received, device):
    pltpu.make_async_remote_copy(
        src_ref=source,
        dst_ref=target,
        send_sem=sent,
        recv_sem=received,
        device_id=device,
        device_id_type=pl.DeviceIdType.MESH,
    ).start()


def landed(block, semaphore):
    pltpu.make_async_copy(block, block, semaphore).wait()


def ring(owners, cores):
    here = lax.axis_index("ctx")
    core = lax.axis_index("tensor")
    right, left = lax.rem(here + 1, owners), lax.rem(here + owners - 1, owners)
    return here, core, cores - 1 - core, right, left


def gather_first(values, outs, sems, owners, cores):
    local, sent_right, sent_left, sent_pair, came, came_pair = sems
    here, core, pair, right, left = ring(owners, cores)
    for i, (value, out) in enumerate(zip(values, outs)):
        target = out.at[here, core]

        @pl.when(here < owners - 1)
        def _():
            send(value, target, sent_right.at[i, here], came.at[i, here], {"ctx": right})

        @pl.when(here > 0)
        def _():
            send(value, target, sent_left.at[i, here], came.at[i, here], {"ctx": left})

        send(value, target, sent_pair.at[i, here], came_pair.at[i, here], {"tensor": pair})
        pltpu.make_async_copy(value, target, local.at[i]).start()


def gather_rest(values, outs, sems, owners, cores):
    local, sent_right, sent_left, sent_pair, came, came_pair = sems
    here, core, pair, right, left = ring(owners, cores)

    def arrive(i, out, block, onward, sent, device):
        held = out.at[block, core]
        landed(held, came.at[i, block])

        @pl.when(onward)
        def _():
            send(held, held, sent.at[i, block], came.at[i, block], device)

        send(held, held, sent_pair.at[i, block], came_pair.at[i, block], {"tensor": pair})

    for step in range(1, owners):
        for i, out in enumerate(outs):

            @pl.when(here >= step)
            def _():
                arrive(i, out, here - step, here < owners - 1, sent_right, {"ctx": right})

            @pl.when(here + step < owners)
            def _():
                arrive(i, out, here + step, here > 0, sent_left, {"ctx": left})

    for i, (value, out) in enumerate(zip(values, outs)):
        pltpu.make_async_copy(value, out.at[here, core], local.at[i]).wait()
        for block in range(owners):
            landed(out.at[block, pair], came_pair.at[i, block])
            landed(out.at[block, core], sent_pair.at[i, block])

            @pl.when((here < owners - 1) & (block <= here))
            def _():
                landed(out.at[block, core], sent_right.at[i, block])

            @pl.when((here > 0) & (block >= here))
            def _():
                landed(out.at[block, core], sent_left.at[i, block])


def gather_sems(amount, owners):
    return [pltpu.SemaphoreType.DMA((amount,))] + [
        pltpu.SemaphoreType.DMA((amount, owners)) for _ in range(5)
    ]


def line_partners(owners, cores):
    here, core, pair, right, left = ring(owners, cores)
    return [{"ctx": right}, {"ctx": left}, {"tensor": pair}]


def gather_kernel(amount, owners, cores, *refs):
    values, outs, sems = refs[:amount], refs[amount : 2 * amount], refs[2 * amount :]
    greet(line_partners(owners, cores))
    gather_first(values, outs, sems, owners, cores)
    gather_rest(values, outs, sems, owners, cores)


ANY = pl.BlockSpec(memory_space=pl.ANY)
FAR = pl.BlockSpec(memory_space=pltpu.HBM)
INSIDE = pl.BlockSpec(memory_space=pltpu.VMEM)


def params(collective_id):
    return pltpu.CompilerParams(
        collective_id=collective_id, has_side_effects=True, vmem_limit_bytes=48 << 20
    )


def cost(micros):
    return pl.CostEstimate(flops=0, transcendentals=0, bytes_accessed=int(micros * 3.0e6))


def team_gather(collective_id, *values):
    owners, cores = lax.axis_size("ctx"), lax.axis_size("tensor")
    amount = len(values)
    outs = pl.pallas_call(
        functools.partial(gather_kernel, amount, owners, cores),
        out_shape=[jax.ShapeDtypeStruct((owners, cores, *v.shape), v.dtype) for v in values],
        in_specs=[ANY] * amount,
        out_specs=[ANY] * amount,
        scratch_shapes=gather_sems(amount, owners),
        compiler_params=params(collective_id),
        cost_estimate=cost(20 * amount),
        name="team_gather",
    )(*values)
    return [o.reshape(-1, v.shape[1]) for o, v in zip(outs, values)]


def plane(index, shards_in):
    across_x = index + 1 - 2 * lax.rem(index, 2)
    return across_x, lax.rem(index + 2, shards_in), lax.rem(across_x + 2, shards_in)


def open_kernel(shards_in, owners, cores, *refs):
    value, w_query, w_key, w_value, w_output, w_gate, w_up, w_down, note = refs[:9]
    out, qkv, out_w, packed, notes = refs[9:14]
    own_sem, sent_w, came_w, passed_w, sent_n, came_n, pack_sem, load_sem = refs[14:22]
    stage, stage_out, stage_pack = refs[22:25]
    sems = refs[25:]
    index = lax.axis_index("shard")
    here = lax.axis_index("ctx")
    depth = w_query.shape[0]
    count = w_query.shape[1] // owners
    columns = pl.ds(pl.multiple_of(here * count, count), count)
    stored = [w.at[:, columns] for w in (w_query, w_key, w_value)] + [w_output.at[columns, :]]
    sources = [stage.at[0], stage.at[1], stage.at[2], stage_out]
    for k, (slow, source) in enumerate(zip(stored, sources)):
        pltpu.make_async_copy(slow, source, load_sem.at[k]).start()

    def target(weight, block):
        if weight == 3:
            wide = w_output.shape[1]
            return out_w.at[:, pl.ds(pl.multiple_of(block * wide, wide), wide)]
        rows = pl.ds(pl.multiple_of(block * depth, depth), depth)
        return qkv.at[rows, pl.ds(weight * count, count)]

    others = [lax.rem(index + step, shards_in) for step in range(1, shards_in)]
    greet(around("shard", shards_in) + around("ctx", owners) + around("tensor", cores))
    units = w_gate.shape[1] // owners
    hidden = pl.ds(pl.multiple_of(here * units, units), units)
    wide_down = w_down.shape[1]
    pieces = [
        (w_gate.at[:, hidden], stage_pack.at[:, pl.ds(0, units)]),
        (w_up.at[:, hidden], stage_pack.at[:, pl.ds(units, units)]),
    ]
    for k in range(units // depth):
        start = pl.multiple_of(here * units + k * depth, depth)
        place = pl.ds(2 * units + k * wide_down, wide_down)
        pieces.append((w_down.at[pl.ds(start, depth), :], stage_pack.at[:, place]))
    for k, (source, place) in enumerate(pieces):
        pltpu.make_async_copy(source, place, pack_sem.at[k]).start()
    notes[here] = note[...]
    fellows = [lax.rem(here + step, owners) for step in range(1, owners)]
    for fellow in fellows:
        send(note, notes.at[here], sent_n.at[fellow], came_n.at[here], {"ctx": fellow})
    square = shards_in == 4
    near = plane(index, shards_in)[:2] if square else others
    for weight in range(4):
        pltpu.make_async_copy(stored[weight], sources[weight], load_sem.at[weight]).wait()
        for other in near:
            send(
                sources[weight],
                target(weight, index),
                sent_w.at[weight, other],
                came_w.at[weight, index],
                {"shard": other},
            )
    gather_first([value], [out], sems, owners, cores)
    for weight in range(4):
        pltpu.make_async_copy(
            sources[weight], target(weight, index), own_sem.at[weight]
        ).start()
    for k, (source, place) in enumerate(pieces):
        pltpu.make_async_copy(source, place, pack_sem.at[k]).wait()
    pltpu.make_async_copy(stage_pack, packed, load_sem.at[4]).start()
    if square:
        across_x, across_y, far = plane(index, shards_in)
        for weight, source, device in (
            (0, across_x, across_y),
            (2, across_y, across_x),
            (1, across_x, across_y),
            (3, across_y, across_x),
        ):
            held = target(weight, source)
            landed(held, came_w.at[weight, source])
            send(
                held, held, passed_w.at[weight], came_w.at[weight, source], {"shard": device}
            )
    gather_rest([value], [out], sems, owners, cores)
    for fellow in fellows:
        landed(notes.at[fellow], came_n.at[fellow])
        landed(note, sent_n.at[fellow])
    pltpu.make_async_copy(stage_pack, packed, load_sem.at[4]).wait()
    for weight in range(4):
        pltpu.make_async_copy(
            sources[weight], target(weight, index), own_sem.at[weight]
        ).wait()
        for other in near:
            landed(sources[weight], sent_w.at[weight, other])
    if square:
        for weight, source in ((0, across_y), (2, across_x), (1, across_y), (3, across_x)):
            landed(target(weight, source), came_w.at[weight, source])
        for weight in range(4):
            landed(target(weight, far), came_w.at[weight, far])
            landed(sources[weight], passed_w.at[weight])
    else:
        for weight in range(4):
            for other in others:
                landed(target(weight, other), came_w.at[weight, other])


def open_team(collective_id, value, weights, note):
    shards_in, owners, cores = [lax.axis_size(a) for a in ("shard", "ctx", "tensor")]
    depth = weights[0].shape[0]
    count = weights[0].shape[1] // owners
    units = weights[4].shape[1] // owners
    pieces = 2 + units // depth
    out, qkv, out_w, packed, notes = pl.pallas_call(
        functools.partial(open_kernel, shards_in, owners, cores),
        out_shape=[
            jax.ShapeDtypeStruct((owners, cores, *value.shape), value.dtype),
            jax.ShapeDtypeStruct((shards_in * depth, 3 * count), value.dtype),
            jax.ShapeDtypeStruct((count, shards_in * weights[3].shape[1]), value.dtype),
            jax.ShapeDtypeStruct((depth, 3 * units), value.dtype),
            jax.ShapeDtypeStruct((owners, *note.shape), note.dtype),
        ],
        in_specs=[ANY] + [FAR] * 7 + [INSIDE],
        out_specs=[ANY] * 3 + [FAR] + [INSIDE],
        scratch_shapes=[
            pltpu.SemaphoreType.DMA((4,)),
            pltpu.SemaphoreType.DMA((4, shards_in)),
            pltpu.SemaphoreType.DMA((4, shards_in)),
            pltpu.SemaphoreType.DMA((4,)),
            pltpu.SemaphoreType.DMA((owners,)),
            pltpu.SemaphoreType.DMA((owners,)),
            pltpu.SemaphoreType.DMA((pieces,)),
            pltpu.SemaphoreType.DMA((5,)),
            pltpu.VMEM((3, depth, count), value.dtype),
            pltpu.VMEM((count, weights[3].shape[1]), value.dtype),
            pltpu.VMEM((depth, 3 * units), value.dtype),
        ]
        + gather_sems(1, owners),
        compiler_params=params(collective_id),
        cost_estimate=cost(40),
        name="open_team",
    )(value, *weights, note)
    return out.reshape(-1, value.shape[1]), qkv, out_w, packed, notes


def scatter_kernel(amount, swapped, owners, cores, *refs):
    parts, refs = refs[:amount], refs[amount:]
    if swapped:
        summed, refs = refs[0], refs[1:]
    outs, refs = refs[:amount], refs[amount:]
    if swapped:
        rows, refs = refs[0], refs[1:]
    pairs, halves, from_left, from_right = [
        refs[k * amount : (k + 1) * amount] for k in range(4)
    ]
    total, sent_pair, came_pair, sent, came_left, came_right = refs[4 * amount : 4 * amount + 6]
    swap = refs[4 * amount + 6 :]
    here, core, pair, right, left = ring(owners, cores)
    if swapped:
        greet(around("ctx", owners) + around("tensor", cores))
    else:
        greet(line_partners(owners, cores))
    order = [k // 2 if k % 2 else owners - 1 - k // 2 for k in range(owners)]
    for i in range(amount):
        for block in order:
            send(
                parts[i].at[block, pair],
                pairs[i].at[block],
                sent_pair.at[i, block],
                came_pair.at[i, block],
                {"tensor": pair},
            )

    if swapped:
        swap_first(summed, rows, *swap, owners)

    def add_up(i, block, more, arrived, came):
        landed(pairs[i].at[block], came_pair.at[i, block])
        total[...] = parts[i][block, core].astype(jnp.float32) + pairs[i][block].astype(
            jnp.float32
        )

        @pl.when(more)
        def _():
            landed(arrived[i].at[block], came.at[i, block])
            total[...] += arrived[i][block].astype(jnp.float32)

    def pass_on(i, block, more, arrived, came, device):
        add_up(i, block, more, arrived, came)
        halves[i][block] = total[...].astype(halves[i].dtype)
        send(
            halves[i].at[block],
            arrived[i].at[block],
            sent.at[i, block],
            came.at[i, block],
            {"ctx": device},
        )

    for step in range(2 * owners - 2):
        for i in range(amount):
            rightward = owners - 1 - (step - here)
            leftward = step - (owners - 1 - here)

            @pl.when((rightward > here) & (step >= here))
            def _():
                pass_on(i, rightward, here > 0, from_left, came_left, right)

            @pl.when((leftward >= 0) & (leftward < here))
            def _():
                pass_on(i, leftward, here < owners - 1, from_right, came_right, left)

    for i in range(amount):
        add_up(i, here, here > 0, from_left, came_left)

        @pl.when(here < owners - 1)
        def _():
            landed(from_right[i].at[here], came_right.at[i, here])
            total[...] += from_right[i][here].astype(jnp.float32)

        outs[i][...] = total[...]
    if swapped:
        swap_rest(summed, rows, *swap, owners, (), 0)
    for i in range(amount):
        for block in range(owners):
            landed(pairs[i].at[block], sent_pair.at[i, block])

            @pl.when(block != here)
            def _():
                landed(halves[i].at[block], sent.at[i, block])


def team_sum(collective_id, *values):
    return team_sum_and_rows(collective_id, None, *values)[0]


def team_sum_and_rows(collective_id, summed, *values):
    owners, cores = lax.axis_size("ctx"), lax.axis_size("tensor")
    amount = len(values)
    width = values[0].shape[1]
    mine = values[0].shape[0] // (owners * cores)
    blocks = [pltpu.VMEM((owners, mine, width), v.dtype) for v in values]
    more = [] if summed is None else [summed]
    out = pl.pallas_call(
        functools.partial(scatter_kernel, amount, bool(more), owners, cores),
        out_shape=[jax.ShapeDtypeStruct((mine, width), jnp.float32)] * amount
        + [jax.ShapeDtypeStruct(held_shape(m, owners), m.dtype) for m in more],
        in_specs=[INSIDE] * amount + [FAR] * len(more),
        out_specs=[INSIDE] * amount + [FAR] * len(more),
        scratch_shapes=blocks * 4
        + [pltpu.VMEM((mine, width), jnp.float32)]
        + [pltpu.SemaphoreType.DMA((amount, owners)) for _ in range(5)]
        + [sem for m in more for sem in swap_sems(owners)],
        compiler_params=params(collective_id),
        cost_estimate=cost(20 * amount),
        name="team_sum",
    )(*[v.reshape(owners, cores, mine, width) for v in values], *more)
    return out[:amount], out[amount:]


def swap_first(summed, held, local, sent, came, owners):
    here = lax.axis_index("ctx")
    count = summed.shape[0] // owners

    def rows(owner):
        return summed.at[pl.ds(pl.multiple_of(owner * count, count), count), :]

    for step in range(1, owners):
        other = lax.rem(here + step, owners)
        send(rows(other), held.at[here], sent.at[other], came.at[here], {"ctx": other})
    pltpu.make_async_copy(rows(here), held.at[here], local).start()


def put_rows(held, source, outs, block, half, halves):
    amount = len(outs)
    units = held.shape[2] // amount
    for j in range(units // block):
        start = pl.multiple_of((source * halves + half) * units + j * block, block)
        for i, out in enumerate(outs):
            first = (j * amount + i) * block
            piece = held[source, :, first : first + block].astype(jnp.float32)
            if i < amount - 1:
                out[:, pl.ds(start, block)] = piece
            else:
                out[pl.ds(start, block), :] = piece.T


def swap_rest(summed, held, local, sent, came, owners, outs, block, half=0, halves=1):
    here = lax.axis_index("ctx")
    count = summed.shape[0] // owners
    own = summed.at[pl.ds(pl.multiple_of(here * count, count), count), :]
    for step in range(owners):
        source = lax.rem(here + owners - step, owners)
        if step == 0:
            pltpu.make_async_copy(own, held.at[here], local).wait()
        else:
            landed(held.at[source], came.at[source])
        if outs:
            put_rows(held, source, outs, block, half, halves)
    for step in range(1, owners):
        other = lax.rem(here + step, owners)
        landed(held.at[other], sent.at[other])


def held_shape(summed, owners):
    return (owners, summed.shape[0] // owners, summed.shape[1])


def swap_sems(owners):
    return [
        pltpu.SemaphoreType.DMA,
        pltpu.SemaphoreType.DMA((owners,)),
        pltpu.SemaphoreType.DMA((owners,)),
    ]


def swap_outs(summed, owners, amount, halves=1):
    count, units = summed.shape[0] // owners, summed.shape[1] // amount * halves
    shapes = [(count, owners * units)] * (amount - 1) + [(owners * units, count)]
    return [jax.ShapeDtypeStruct(shape, jnp.float32) for shape in shapes]


def around(axis, size):
    index = lax.axis_index(axis)
    return [{axis: lax.rem(index + step, size)} for step in range(1, size)]


def swap_kernel_alone(owners, block, amount, *refs):
    summed, outs, scratch = refs[0], refs[1 : 1 + amount], refs[1 + amount :]
    greet(around("ctx", owners))
    swap_first(summed, *scratch, owners)
    swap_rest(summed, *scratch, owners, outs, block)


def team_rows(collective_id, summed, amount, block):
    owners = lax.axis_size("ctx")
    return pl.pallas_call(
        functools.partial(swap_kernel_alone, owners, block, amount),
        out_shape=swap_outs(summed, owners, amount),
        in_specs=[ANY],
        out_specs=[INSIDE] * amount,
        scratch_shapes=[pltpu.VMEM(held_shape(summed, owners), summed.dtype)]
        + swap_sems(owners),
        compiler_params=params(collective_id),
        cost_estimate=cost(20),
        name="team_rows",
    )(summed)


def close_kernel(amount, shards_in, owners, cores, *refs):
    values, mixed, grads, early = refs[:amount], refs[amount], refs[amount + 1], refs[amount + 2]
    refs = refs[amount + 3 :]
    outs, summed, grad_outs = refs[:amount], refs[amount], refs[amount + 1 : amount + 4]
    refs = refs[amount + 4 :]
    pairs, half, quarters, blocks, local, sent, came = refs[:7]
    sent_c, came_c, sent_s, came_s, sent_b, came_b = refs[7:13]
    swap = refs[13:]
    here, core, pair, right, left = ring(owners, cores)
    index = lax.axis_index("shard")
    near = [lax.rem(here + step, owners) for step in range(1, owners)]
    others = [lax.rem(index + step, shards_in) for step in range(1, shards_in)]
    greet([{"tensor": pair}] + around("ctx", owners) + around("shard", shards_in))
    wide = mixed.shape[1] // cores
    thin = wide // owners
    send(
        mixed.at[:, pl.ds(pl.multiple_of(pair * wide, wide), wide)],
        pairs,
        sent.at[amount],
        came.at[amount],
        {"tensor": pair},
    )
    for i in range(amount):
        target = outs[i].at[:, core]
        send(values[i], target, sent.at[i], came.at[i], {"tensor": pair})
        pltpu.make_async_copy(values[i], target, local.at[i]).start()
    landed(pairs, came.at[amount])
    half[...] = mixed[:, pl.ds(pl.multiple_of(core * wide, wide), wide)] + pairs[...]
    for other in near:
        send(
            half.at[:, pl.ds(pl.multiple_of(other * thin, thin), thin)],
            quarters.at[here],
            sent_c.at[other],
            came_c.at[here],
            {"ctx": other},
        )
    total = half[:, pl.ds(pl.multiple_of(here * thin, thin), thin)]
    for other in near:
        landed(quarters.at[other], came_c.at[other])
        total += quarters[other]
    blocks[index] = total
    for other in others:
        send(
            blocks.at[index], blocks.at[index], sent_s.at[other], came_s.at[index], {"shard": other}
        )
    swap_first(grads, *swap, owners)
    for other in others:
        landed(blocks.at[other], came_s.at[other])
    total = blocks[0]
    for block in range(1, shards_in):
        total += blocks[block]

    def place(owner, half_of):
        return summed.at[half_of * owners + owner]

    summed[core * owners + here] = total
    for other in near:
        send(place(here, core), place(here, core), sent_b.at[other], came_b.at[here, core], {"ctx": other})
    send(place(here, core), place(here, core), sent_b.at[here], came_b.at[here, core], {"tensor": pair})
    for other in near:
        landed(place(other, core), came_b.at[other, core])
        send(
            place(other, core),
            place(other, core),
            sent_b.at[owners + other],
            came_b.at[other, core],
            {"tensor": pair},
        )
    for owner in range(owners):
        landed(place(owner, pair), came_b.at[owner, pair])
        landed(place(owner, core), sent_b.at[owner])
    for other in near:
        landed(place(other, core), sent_b.at[owners + other])
        landed(quarters.at[other], sent_c.at[other])
    for other in others:
        landed(blocks.at[other], sent_s.at[other])
    landed(pairs, sent.at[amount])
    block = grads.shape[1] // (3 * BLOCKS // 2)
    for source in range(owners):
        put_rows(early, source, grad_outs, block, 0, 2)
    swap_rest(grads, *swap, owners, grad_outs, block, 1, 2)
    for i in range(amount):
        target = outs[i].at[:, core]
        landed(outs[i].at[:, pair], came.at[i])
        landed(target, sent.at[i])
        pltpu.make_async_copy(values[i], target, local.at[i]).wait()


def close_team(collective_id, early, grads, mixed, *values):
    shards_in, owners, cores = [lax.axis_size(a) for a in ("shard", "ctx", "tensor")]
    amount = len(values)
    height, width = mixed.shape
    thin = width // (cores * owners)
    out = pl.pallas_call(
        functools.partial(close_kernel, amount, shards_in, owners, cores),
        out_shape=[
            jax.ShapeDtypeStruct((v.shape[0], cores, *v.shape[1:]), v.dtype) for v in values
        ]
        + [jax.ShapeDtypeStruct((cores * owners, height, thin), jnp.float32)]
        + swap_outs(grads, owners, 3, 2),
        in_specs=[ANY] * amount + [INSIDE, FAR, INSIDE],
        out_specs=[ANY] * amount + [INSIDE] * 4,
        scratch_shapes=[
            pltpu.VMEM((height, width // cores), jnp.float32),
            pltpu.VMEM((height, width // cores), jnp.float32),
            pltpu.VMEM((owners, height, thin), jnp.float32),
            pltpu.VMEM((shards_in, height, thin), jnp.float32),
            pltpu.SemaphoreType.DMA((amount,)),
            pltpu.SemaphoreType.DMA((amount + 1,)),
            pltpu.SemaphoreType.DMA((amount + 1,)),
            pltpu.SemaphoreType.DMA((owners,)),
            pltpu.SemaphoreType.DMA((owners,)),
            pltpu.SemaphoreType.DMA((shards_in,)),
            pltpu.SemaphoreType.DMA((shards_in,)),
            pltpu.SemaphoreType.DMA((2 * owners,)),
            pltpu.SemaphoreType.DMA((owners, cores)),
        ]
        + [pltpu.VMEM(held_shape(grads, owners), grads.dtype)]
        + swap_sems(owners),
        compiler_params=params(collective_id),
        cost_estimate=cost(60),
        name="close_team",
    )(*values, mixed, grads, early)
    mixed = out[amount].transpose(1, 0, 2).reshape(height, width)
    return mixed, out[:amount], out[amount + 1 :]


def ffn_kernel(
    u_ref,
    dy_ref,
    gate_ref,
    up_ref,
    down_ref,
    y_ref,
    du_ref,
    early_ref,
    late_ref,
    y_sum,
    du_sum,
    u_t,
    dy_t,
):
    step = pl.program_id(0)
    early = step < pl.num_programs(0) // 2
    total, width = u_ref.shape
    block = gate_ref.shape[1]
    tile = down_ref.shape[2]

    @pl.when(step == 0)
    def _():
        y_sum[...] = jnp.zeros_like(y_sum)
        du_sum[...] = jnp.zeros_like(du_sum)
        for start in range(0, width, tile):
            u_t[start : start + tile, :] = u_ref[:, start : start + tile].T
            dy_t[start : start + tile, :] = dy_ref[:, start : start + tile].T

    gate = dot(u_ref[...], gate_ref[...])
    upward = dot(u_ref[...], up_ref[...])
    shards_in = down_ref.shape[0]
    grad_hidden = 0.0
    for k in range(shards_in):
        grad_hidden = grad_hidden + contract_cols(
            dy_ref[:, k * tile : (k + 1) * tile], down_ref[k]
        )
    sigma = jax.nn.sigmoid(gate)
    swish = gate * sigma
    hidden = (swish * upward).astype(jnp.bfloat16)
    grad_gate = (grad_hidden * upward * (sigma + swish * (1.0 - sigma))).astype(jnp.bfloat16)
    grad_up = (grad_hidden * swish).astype(jnp.bfloat16)
    for k in range(shards_in):
        span = slice(k * tile, (k + 1) * tile)
        y_sum[:, span] += dot(hidden, down_ref[k])
        du_sum[:, span] += contract_cols(grad_gate, gate_ref[span, :]) + contract_cols(
            grad_up, up_ref[span, :]
        )

    def weights_back(grad_ref):
        for start in range(0, width, tile):
            span = slice(start, start + tile)
            grad_ref[span, :block] = dot(u_t[span, :], grad_gate).astype(jnp.bfloat16)
            grad_ref[span, block : 2 * block] = dot(u_t[span, :], grad_up).astype(jnp.bfloat16)
            grad_ref[span, 2 * block :] = dot(dy_t[span, :], hidden).astype(jnp.bfloat16)

    @pl.when(early)
    def _():
        weights_back(early_ref)

    @pl.when(jnp.logical_not(early))
    def _():
        weights_back(late_ref)

    @pl.when(step == pl.num_programs(0) - 1)
    def _():
        y_ref[...] = y_sum[...].astype(jnp.bfloat16)
        du_ref[...] = du_sum[...].astype(jnp.bfloat16)


def ffn(u, dy, weights):
    total, width = u.shape
    shards_in = lax.axis_size("shard")
    depth = width // shards_in
    units = weights.shape[1] // 3
    blocks = BLOCKS
    block = units // blocks
    half = blocks // 2
    whole = pl.BlockSpec((total, width), lambda j: (0, 0), pipeline_mode=pl.Buffered(1))
    low = functools.partial(jax.ShapeDtypeStruct, dtype=jnp.bfloat16)
    return pl.pallas_call(
        ffn_kernel,
        grid=(blocks,),
        in_specs=[
            whole,
            whole,
            pl.BlockSpec((width, block), lambda j: (0, j)),
            pl.BlockSpec((width, block), lambda j: (0, blocks + j)),
            pl.BlockSpec(
                (shards_in, block, depth),
                lambda j: (0, j % (depth // block), 2 * units // depth + j // (depth // block)),
            ),
        ],
        out_specs=[
            whole,
            whole,
            pl.BlockSpec((width, 3 * block), lambda j: (0, jnp.minimum(j, half - 1))),
            pl.BlockSpec((width, 3 * block), lambda j: (0, jnp.maximum(j - half, 0))),
        ],
        out_shape=[low((total, width))] * 2 + [low((width, 3 * units // 2))] * 2,
        scratch_shapes=[
            pltpu.VMEM((total, width), jnp.float32),
            pltpu.VMEM((total, width), jnp.float32),
            pltpu.VMEM((width, total), jnp.bfloat16),
            pltpu.VMEM((width, total), jnp.bfloat16),
        ],
        compiler_params=pltpu.CompilerParams(
            dimension_semantics=("arbitrary",), vmem_limit_bytes=60 << 20
        ),
        cost_estimate=cost(30),
        name="ffn",
    )(u, dy, weights, weights, weights.reshape(shards_in, depth, 3 * units))


def pack_kernel(sent, value, out):
    out[0] = value[...]


def pack_runs(value, sent, part):
    total, rows_in, width = value.shape
    return pl.pallas_call(
        pack_kernel,
        grid_spec=pltpu.PrefetchScalarGridSpec(
            num_scalar_prefetch=1,
            grid=(sent.shape[0],),
            in_specs=[
                pl.BlockSpec((total, part, width), lambda c, first: (0, first[c], 0)),
            ],
            out_specs=pl.BlockSpec((1, total, part, width), lambda c, first: (c, 0, 0, 0)),
        ),
        out_shape=jax.ShapeDtypeStruct((sent.shape[0], total, part, width), value.dtype),
        compiler_params=pltpu.CompilerParams(dimension_semantics=("arbitrary",)),
        cost_estimate=cost(2),
        name="pack_runs",
    )(sent, value)


def head_probs(query, key, placing, placed):
    scores = contract_cols(query, key) * HD ** (-0.5)
    allowed = (placed >= placing[:, 0:1]) & (placed <= placing[:, 1:2])
    scores = jnp.where(allowed, scores, FLOOR_SCORE)
    probs = jnp.exp(scores - jnp.max(scores, -1, keepdims=True))
    return probs / jnp.sum(probs, -1, keepdims=True)


def turn(value, turns, back):
    swung = pltpu.roll(value, HD // 2, 1) * turns[1]
    return value * turns[0] - swung if back else value * turns[0] + swung


def attend_kernel(
    u_ref, qkv_ref, out_ref, turns, placing, placed, y_ref, q_ref, k_ref, v_ref, o_ref
):
    count = q_ref.shape[1]
    u = u_ref[...]
    for first in range(0, count, HD):
        head = slice(first, first + HD)

        def lin(which):
            start = which * count + first
            return dot(u, qkv_ref[:, start : start + HD])

        query = turn(lin(0), turns, False).astype(jnp.bfloat16)
        key = turn(lin(1), turns, False).astype(jnp.bfloat16)
        value = lin(2).astype(jnp.bfloat16)
        q_ref[:, head] = query
        k_ref[:, head] = key
        v_ref[:, head] = value
        probs = head_probs(query, key, placing[...], placed[...])
        o_ref[:, head] = dot(probs.astype(jnp.bfloat16), value).astype(jnp.bfloat16)
    width = y_ref.shape[1]
    for start in range(0, width, 512):
        y_ref[:, start : start + 512] = dot(o_ref[...], out_ref[:, start : start + 512])


def attend(u, qkv, out_w, turns, placing, placed):
    total, count = u.shape[0], out_w.shape[0]
    low = jax.ShapeDtypeStruct((total, count), jnp.bfloat16)
    return pl.pallas_call(
        attend_kernel,
        out_shape=[jax.ShapeDtypeStruct((total, out_w.shape[1]), jnp.float32)] + [low] * 4,
        in_specs=[INSIDE] * 6,
        out_specs=[INSIDE] * 5,
        compiler_params=pltpu.CompilerParams(vmem_limit_bytes=56 << 20),
        cost_estimate=cost(12),
        name="attend",
    )(u, qkv, out_w, turns, placing, placed)


def attend_back_kernel(
    dy_ref,
    u_ref,
    qkv_ref,
    out_ref,
    q_ref,
    k_ref,
    v_ref,
    o_ref,
    turns,
    placing,
    placed,
    du_ref,
    grad_ref,
    lin,
):
    count = q_ref.shape[1]
    width = du_ref.shape[1]
    scale = HD ** (-0.5)
    low = jnp.bfloat16
    for first in range(0, count, HD):
        head = slice(first, first + HD)
        query, key, value = q_ref[:, head], k_ref[:, head], v_ref[:, head]
        grad_out = contract_cols(dy_ref[...], out_ref[head, :]).astype(low)
        probs = head_probs(query, key, placing[...], placed[...])
        grad_probs = contract_cols(grad_out, value)
        delta = jnp.sum(probs * grad_probs, -1, keepdims=True)
        grad_scores = (probs * (grad_probs - delta)).astype(low)
        grad_query = turn(dot(grad_scores, key) * scale, turns, True)
        grad_key = turn(contract_rows(grad_scores, query) * scale, turns, True)
        grad_value = contract_rows(probs.astype(low), grad_out)
        for which, grad in enumerate((grad_query, grad_key, grad_value)):
            start = which * count + first
            lin[:, start : start + HD] = grad.astype(low)
    tile = min(512, width)
    edge = lin.shape[1]
    for start in range(0, width, tile):
        span = slice(start, start + tile)
        du_ref[:, span] = contract_cols(lin[...], qkv_ref[span, :]).astype(low)
        grad_ref[span, :edge] = dot(u_ref[:, span].T, lin[...]).astype(low)
        grad_ref[span, edge:] = dot(dy_ref[:, span].T, o_ref[...]).astype(low)


def attend_back(dy, u, qkv, out_w, q, k, v, o, turns, placing, placed):
    total, width = u.shape
    count = q.shape[1]
    return pl.pallas_call(
        attend_back_kernel,
        out_shape=[
            jax.ShapeDtypeStruct((total, width), jnp.bfloat16),
            jax.ShapeDtypeStruct((width, 4 * count), jnp.bfloat16),
        ],
        in_specs=[INSIDE] * 11,
        out_specs=[INSIDE] * 2,
        scratch_shapes=[pltpu.VMEM((total, 3 * count), jnp.bfloat16)],
        compiler_params=pltpu.CompilerParams(vmem_limit_bytes=56 << 20),
        cost_estimate=cost(20),
        name="attend_back",
    )(dy, u, qkv, out_w, q, k, v, o, turns, placing, placed)


EXACT = functools.partial(
    lax.dot_general, precision=PRECISE, preferred_element_type=jnp.float32
)


def columns_of(pieces):
    rows_in = pieces[0].shape[0]
    lane = lax.broadcasted_iota(jnp.int32, (rows_in, 8), 1)
    out = jnp.zeros((rows_in, 8), jnp.float32)
    for k, piece in enumerate(pieces):
        out = jnp.where(lane == k, piece, out)
    return out


def tables_of(current, weight, static, table_ref, active_ref):
    branch_in = 0.0
    tables = []
    for i, stream in enumerate(current):
        normed, scaled = norm_rows(stream)
        active = jnp.tanh(EXACT(normed, weight, (((1,), (1,)), ((), ()))))
        table = active + static[i : i + 1, :]
        table_ref[i] = table
        active_ref[i] = active
        tables.append(table)
        branch_in = branch_in + table[:, 0:1] * stream
    return tables, branch_in


def norm_plain(value):
    centred = value - jnp.mean(value, -1, keepdims=True)
    scaled = lax.rsqrt(jnp.mean(centred * centred, -1, keepdims=True) + EPSILON)
    return (centred * scaled, scaled)


def mix_first(current, weight, static):
    normed, _ = norm_plain(current)
    active = jnp.tanh(jnp.einsum("tsd,dk->tsk", normed, weight, precision=PRECISE))
    table = active + static
    total = current.shape[1]
    branch_in = sum(table[:, i, 0][:, None] * current[:, i] for i in range(total))
    normed, scaled = norm_plain(branch_in)

    def by_stream(value):
        return jnp.pad(value.transpose(1, 0, 2), ((0, 0), (0, 0), (0, 8 - value.shape[2])))

    scaled = jnp.pad(scaled, ((0, 0), (0, 7)))
    return normed.astype(jnp.bfloat16), normed, scaled, by_stream(table), by_stream(active)


def mix_second_kernel(
    source,
    streams,
    branch_out,
    table_one,
    arrived,
    weight,
    static,
    middle_ref,
    low_ref,
    grad_low_ref,
    normed_ref,
    scaled_ref,
    table_ref,
    active_ref,
    top_ref,
):
    total = streams.shape[0]
    y = branch_out[...]
    first = [table_one[i] for i in range(total)]
    current = [streams[i].astype(jnp.float32) for i in range(total)]
    middle = []
    for j in range(total):
        mixed = first[j][:, total + 1 : total + 2] * y
        for i in range(total):
            mixed = mixed + first[i][:, 1 + j : 2 + j] * current[i]
        middle.append(mixed)
        middle_ref[j] = mixed
    tables, branch_in = tables_of(middle, weight[...], static[...], table_ref, active_ref)
    normed, scaled = norm_rows(branch_in)
    normed_ref[...] = normed
    low_ref[...] = normed.astype(jnp.bfloat16)
    scaled_ref[...] = columns_of([scaled])
    grad = 0.0
    for j in range(total):
        top = arrived[0, j]
        top_ref[j] = top
        grad = grad + tables[j][:, total + 1 : total + 2] * top.astype(jnp.float32)
    grad_low_ref[...] = grad.astype(jnp.bfloat16)


def connection_back(
    current, grad_top, branch_out, grad_in, normed_in, scaled_in, tables, actives, weight, sums
):
    total = len(current)
    weight_sum, static_sum = sums
    dx = scaled_in * (grad_in - mean_of(grad_in) - normed_in * mean_of(grad_in * normed_in))
    result = []
    for i, stream in enumerate(current):
        pieces = [jnp.sum(dx * stream, -1, keepdims=True)]
        pieces += [jnp.sum(stream * top, -1, keepdims=True) for top in grad_top]
        pieces.append(jnp.sum(grad_top[i] * branch_out, -1, keepdims=True))
        grad_table = columns_of(pieces)
        static_sum[i : i + 1, :] += jnp.sum(grad_table, 0, keepdims=True)
        grad_inner = grad_table * (1.0 - actives[i] * actives[i])
        normed, scaled = norm_rows(stream)
        weight_sum[...] += EXACT(grad_inner, normed, (((0,), (0,)), ((), ())))
        grad_normed = EXACT(grad_inner, weight, (((1,), (0,)), ((), ())))
        grad = tables[i][:, 0:1] * dx + norm_back(normed, scaled, grad_normed)
        for j in range(total):
            grad = grad + tables[i][:, 1 + j : 2 + j] * grad_top[j]
        result.append(grad)
    return result


def start_sums(sums):
    @pl.when(pl.program_id(0) == 0)
    def _():
        for ref in sums:
            ref[...] = jnp.zeros_like(ref)


def back_second_kernel(
    middle,
    top,
    branch_out,
    grad_in,
    normed_in,
    scaled_in,
    table,
    active,
    table_one,
    weight,
    final_ref,
    grad_ref,
    grad_low_ref,
    *sums,
):
    start_sums(sums)
    total = middle.shape[0]
    current = [middle[i] for i in range(total)]
    grad_top = [top[i].astype(jnp.float32) for i in range(total)]
    tables = [table[i] for i in range(total)]
    y = branch_out[...]
    for j in range(total):
        mixed = tables[j][:, total + 1 : total + 2] * y
        for i in range(total):
            mixed = mixed + tables[i][:, 1 + j : 2 + j] * current[i]
        final_ref[j] = mixed.astype(jnp.bfloat16)
    grads = connection_back(
        current,
        grad_top,
        y,
        grad_in[...],
        normed_in[...],
        scaled_in[:, 0:1],
        tables,
        [active[i] for i in range(total)],
        weight[...],
        sums,
    )
    low = 0.0
    for j in range(total):
        grad_ref[j] = grads[j]
        low = low + table_one[j][:, total + 1 : total + 2] * grads[j]
    grad_low_ref[...] = low.astype(jnp.bfloat16)


def back_first_kernel(
    streams,
    top,
    branch_out,
    grad_in,
    normed_in,
    scaled_in,
    table,
    active,
    weight,
    grad_ref,
    *sums,
):
    start_sums(sums)
    total = streams.shape[0]
    grads = connection_back(
        [streams[i].astype(jnp.float32) for i in range(total)],
        [top[i] for i in range(total)],
        branch_out[...],
        grad_in[...],
        normed_in[...],
        scaled_in[:, 0:1],
        [table[i] for i in range(total)],
        [active[i] for i in range(total)],
        weight[...],
        sums,
    )
    for j in range(total):
        grad_ref[j] = grads[j].astype(jnp.bfloat16)


def by_token(tile, shape, kind=jnp.float32):
    block = (*shape[:-2], tile, shape[-1])
    lead = (0,) * (len(shape) - 2)
    spec = pl.BlockSpec(block, lambda step, *_: (*lead, step, 0))
    return spec, jax.ShapeDtypeStruct(shape, kind)


def fixed(shape, kind=jnp.float32):
    spec = pl.BlockSpec(shape, lambda step, *_: (0,) * len(shape))
    return spec, jax.ShapeDtypeStruct(shape, kind)


def token_call(kernel, name, tile, ins, outs, prefetch=(), special=None):
    specs, values = [], []
    for value, tiled in ins:
        if tiled == "run":
            specs.append(special)
        else:
            specs.append(by_token(tile, value.shape)[0] if tiled else fixed(value.shape)[0])
        values.append(value)
    tokens = outs[0][1].shape[-2]
    return pl.pallas_call(
        kernel,
        grid_spec=pltpu.PrefetchScalarGridSpec(
            num_scalar_prefetch=len(prefetch),
            grid=(tokens // tile,),
            in_specs=specs,
            out_specs=[o[0] for o in outs],
        ),
        out_shape=[o[1] for o in outs],
        compiler_params=pltpu.CompilerParams(
            dimension_semantics=("arbitrary",), vmem_limit_bytes=48 << 20
        ),
        cost_estimate=cost(5),
        name=name,
    )(*prefetch, *values)


def shards(
    streams,
    lengths,
    destination,
    w_query,
    w_key,
    w_value,
    w_output,
    w_gate,
    w_up,
    w_down,
    mix_weight,
    mix_static,
    cotangent,
):
    rows_here, stream_total, width = streams.shape
    owners = lax.axis_size("ctx")
    cores = lax.axis_size("tensor")
    here = lax.axis_index("ctx")
    core = lax.axis_index("tensor")
    run_rows = rows_here // owners
    part = run_rows // cores
    mine = rows_here // cores
    group_rows = rows_here * owners
    head_cols = w_query.shape[1] // owners
    heads = head_cols // HD
    units = w_gate.shape[1] // owners
    scale = HD ** (-0.5)

    def columns(weight, count):
        return lax.dynamic_slice_in_dim(weight, here * count, count, 1)

    def rows(weight, count):
        return lax.dynamic_slice_in_dim(weight, here * count, count, 0)

    order = jnp.arange(group_rows, dtype=jnp.int32)
    within = order % mine
    placed = (
        order // rows_here * rows_here
        + within // part * run_rows
        + order % rows_here // mine * part
        + within % part
    )
    spans = lengths[0]
    count = jnp.arange(spans.shape[0], dtype=jnp.int32)
    starts = jnp.sum(jnp.where(count[None, :] < count[:, None], spans[None, :], 0), 1)
    begin = jnp.max(jnp.where(starts[None, :] <= placed[:, None], starts[None, :], 0), axis=1)
    cosine, sine = angles(placed - begin, HD)
    turns = jnp.stack(
        [jnp.concatenate([cosine, cosine], -1), jnp.concatenate([-sine, sine], -1)]
    ).reshape(2, group_rows, HD)
    placing = jnp.stack([begin, placed], 1)
    placed = placed[None]

    local_dest = destination - lax.axis_index("shard") * group_rows
    heads_of_runs = local_dest.reshape(owners, run_rows)[:, 0]
    came_from = heads_of_runs // rows_here
    note = jnp.broadcast_to(jnp.pad(heads_of_runs, (0, 128 - owners)), (8, 128))

    turned_weight = jnp.pad(mix_weight.transpose(0, 2, 1), ((0, 0), (0, 2), (0, 0)))
    static = jnp.pad(mix_static, ((0, 0), (0, 0), (0, 2)))
    split = streams.reshape(owners, cores, part, stream_total, width)
    current = lax.dynamic_index_in_dim(split, core, 1, keepdims=False)
    current = current.reshape(mine, stream_total, width)
    attn_low, attn_normed, attn_scaled, table_one, active_one = mix_first(
        current.astype(jnp.float32), mix_weight[0], mix_static[0]
    )
    current = current.transpose(1, 0, 2)
    low = jnp.bfloat16
    tile = min(16, part)
    small = by_token(tile, (stream_total, mine, 8))
    attn_input, qkv, out_w, packed, notes = open_team(
        0, attn_low, (w_query, w_key, w_value, w_output, w_gate, w_up, w_down), note
    )
    ffn_weights = lax.all_gather(packed, "shard", axis=0, tiled=True)
    every = notes[:, 0, :owners]
    sent = jnp.sum(jnp.where(every // rows_here == here, every % rows_here, 0), 1) // part + core
    packed = pack_runs(cotangent.transpose(1, 0, 2), sent, part)
    arrived = lax.all_to_all(packed, "ctx", split_axis=0, concat_axis=0, tiled=True)
    attn_part, queries, keys, values, attended = attend(
        attn_input, qkv, out_w, turns, placing, placed
    )
    [attn_out] = team_sum(1, attn_part)

    (
        middle,
        ffn_low,
        grad_ffn_low,
        ffn_normed,
        ffn_scaled,
        table_two,
        active_two,
        grad_top,
    ) = token_call(
        mix_second_kernel,
        "mix_second",
        tile,
        [
            (current, True),
            (attn_out, True),
            (table_one, True),
            (arrived, "run"),
            (turned_weight[1], False),
            (static[1], False),
        ],
        [
            by_token(tile, (stream_total, mine, width)),
            by_token(tile, (mine, width), low),
            by_token(tile, (mine, width), low),
            by_token(tile, (mine, width)),
            by_token(tile, (mine, 8)),
            small,
            small,
            by_token(tile, (stream_total, mine, width), low),
        ],
        (came_from,),
        pl.BlockSpec(
            (1, stream_total, tile, width),
            lambda step, source: (source[step * tile // part], 0, step % (part // tile), 0),
        ),
    )
    ffn_input, grad_ffn_out = team_gather(2, ffn_low, grad_ffn_low)
    ffn_part, ffn_input_part, *ffn_grads = ffn(ffn_input, grad_ffn_out, ffn_weights)

    def shard_sum(partial):
        return lax.psum_scatter(partial, "shard", scatter_dimension=0, tiled=True)

    early_sum, late_sum = [shard_sum(grads) for grads in ffn_grads]
    ffn_out, grad_ffn_input = team_sum(3, ffn_part, ffn_input_part)
    sums = [fixed((8, width)), fixed((stream_total, 8))]
    final, grad_middle, grad_attn_low, weight_two, static_two = token_call(
        back_second_kernel,
        "back_second",
        tile,
        [
            (middle, True),
            (grad_top, True),
            (ffn_out, True),
            (grad_ffn_input, True),
            (ffn_normed, True),
            (ffn_scaled, True),
            (table_two, True),
            (active_two, True),
            (table_one, True),
            (turned_weight[1], False),
        ],
        [
            by_token(tile, (stream_total, mine, width), low),
            by_token(tile, (stream_total, mine, width)),
            by_token(tile, (mine, width), low),
            *sums,
        ],
    )
    [grad_attn_out] = team_gather(4, grad_attn_low)

    attn_input_part, attn_grads = attend_back(
        grad_attn_out, attn_input, qkv, out_w, queries, keys, values, attended, turns, placing, placed
    )
    attn_sum = shard_sum(attn_grads)
    [grad_attn_input], [early_rows] = team_sum_and_rows(5, early_sum, attn_input_part)
    grad_current, weight_one, static_one = token_call(
        back_first_kernel,
        "back_first",
        tile,
        [
            (current, True),
            (grad_middle, True),
            (attn_out, True),
            (grad_attn_input, True),
            (attn_normed, True),
            (attn_scaled, True),
            (table_one, True),
            (active_one, True),
            (turned_weight[0], False),
        ],
        [by_token(tile, (stream_total, mine, width), low), *sums],
    )
    statics = jnp.stack([static_one, static_two]).reshape(1, -1)
    mixed = jnp.concatenate(
        [
            jnp.stack([weight_one, weight_two], 1).reshape(16, width),
            jnp.pad(statics, ((0, 7), (0, width - statics.size))),
        ],
        0,
    )

    def runs(value):
        return value.transpose(1, 0, 2).reshape(owners, part, stream_total, width)

    mixed, (streams_out, grad_streams), (grad_gate, grad_up, grad_down) = close_team(
        7, early_rows, late_sum, mixed, runs(final), runs(grad_current)
    )
    mixed, attn_sum = lax.optimization_barrier((mixed, attn_sum))
    grad_query, grad_key, grad_value, grad_output = team_rows(8, attn_sum, 4, head_cols)
    columns_in = mix_weight.shape[2]
    grad_mix_weight = mixed[: 2 * columns_in].reshape(columns_in, 2, width).transpose(1, 2, 0)
    grad_mix_static = mixed[16, : statics.size].reshape(2, stream_total, 8)[:, :, :columns_in]

    return (
        streams_out.reshape(rows_here, stream_total, width),
        grad_streams.reshape(rows_here, stream_total, width),
        grad_query,
        grad_key,
        grad_value,
        grad_output,
        grad_gate,
        grad_up,
        grad_down,
        grad_mix_weight,
        grad_mix_static,
    )


def solution(mesh):
    return jax.shard_map(
        shards,
        mesh=mesh,
        in_specs=(
            P(("shard", "ctx"), None, None),
            P("shard", None),
            P(("shard", "ctx")),
            P("shard", "tensor"),
            P("shard", "tensor"),
            P("shard", "tensor"),
            P("tensor", "shard"),
            P("shard", "tensor"),
            P("shard", "tensor"),
            P("tensor", "shard"),
            P(),
            P(),
            P(("shard", "ctx"), None, None),
        ),
        out_specs=(
            P(("shard", "ctx"), None, None),
            P(("shard", "ctx"), None, None),
            P(("shard", "ctx"), "tensor"),
            P(("shard", "ctx"), "tensor"),
            P(("shard", "ctx"), "tensor"),
            P("tensor", ("shard", "ctx")),
            P(("shard", "ctx"), "tensor"),
            P(("shard", "ctx"), "tensor"),
            P("tensor", ("shard", "ctx")),
            P(),
            P(),
        ),
        check_vma=False,
    )
```

time: 579 us -> 494 us (0.85)
  Pallas kernels: 259 us -> 397 us
  matrix products: 86.1 us -> 2.42 us
  waiting for transfers between devices: 62.7 us -> 0.8 us
  other arithmetic: 47.6 us -> 7.58 us
  between operations: 32.1 us -> 14.6 us
  starting transfers between devices: 24.2 us -> 7.67 us
    pallas_call x4 -> x11, Pallas kernels: 140 us -> 253 us  [the longest x3 139 us: team_sum_and_rows(): pl.pallas_call(functools.partial(scatter_kernel, amount, bool(more), owne...]
    dot_general x23 -> x1, matrix products: 84.8 us -> 2.42 us  [mix_first(): jnp.einsum('tsd,dk->tsk', normed, weight, precision=PRECISE)]
    reduce_scatter x3, waiting for transfers between devices: 44.5 us -> 0.06 us  [shard_sum(): return lax.psum_scatter(partial, 'shard', scatter_dimension=0, tiled=True)]
    pallas_call x1, Pallas kernels: 25.5 us -> 48.9 us  [close_team(): pl.pallas_call(functools.partial(close_kernel, amount, shards_in, owners,...]
    all_to_all x3 -> x0, starting transfers between devices: 18.2 us -> none  [to_owner_rows(): lax.all_to_all(summed, 'ctx', split_axis=0, concat_axis=0, tiled=True)]
    unnamed x365 -> x102, local copies, waits for them, and re-layouts: 31.5 us -> 49.2 us
    all_to_all x3 -> x0, waiting for transfers between devices: 17.6 us -> none  [to_owner_rows(): lax.all_to_all(summed, 'ctx', split_axis=0, concat_axis=0, tiled=True)]
    convert_element_type x10 -> x2, other arithmetic: 9.94 us -> 0.37 us  [the longest x1 0.24 us: shards(): current.astype(jnp.float32)]
  transfers between devices with their start and end apart: 9 -> 5, of which waited for: 2 -> 0; matrix products, arithmetic and copies ran while one was open for 19% -> 3% of each run, Pallas kernels for 39% -> 61%
where the time goes in v3:
time: 494 us; the launch traced here: 487 us
  Pallas kernels  397 us (80%)
  local copies, waits for them, and re-layouts  56.8 us (11%)
  between operations  14.6 us (3%)
  starting transfers between devices  7.67 us (2%)
  other arithmetic  7.58 us (2%)
    pallas_call x3, Pallas kernels, team_sum_and_rows(): pl.pallas_call(functools.partial(scatter_kernel, amount, bool(more), owne...  139 us
    pallas_call x2, Pallas kernels, team_gather(): pl.pallas_call(functools.partial(gather_kernel, amount, owners, cores), o...  55.5 us
    unnamed x102, local copies, waits for them, and re-layouts  49.2 us
    pallas_call x1, Pallas kernels, close_team(): pl.pallas_call(functools.partial(close_kernel, amount, shards_in, owners,...  48.9 us
    pallas_call x1, Pallas kernels, open_team(): pl.pallas_call(functools.partial(open_kernel, shards_in, owners, cores),...  39.2 us
    pallas_call x1, Pallas kernels, ffn(): pl.pallas_call(ffn_kernel, grid=(blocks,), in_specs=[whole, whole, pl.Blo...  33.9 us
    pallas_call x1, Pallas kernels, team_rows(): pl.pallas_call(functools.partial(swap_kernel_alone, owners, block, amount...  26.1 us
    pallas_call x3, Pallas kernels, token_call(): pl.pallas_call(kernel, grid_spec=pltpu.PrefetchScalarGridSpec(num_scalar_...  24.7 us
  transfers between devices with their start and end apart: 5, of which 0 were waited for; matrix products, arithmetic and copies ran while one was open for 3% of the time, Pallas kernels for 61%

profile of v3, /device:TPU:8, one launch (start us, length us, event | category | flops | bytes accessed | tf_op | source)
XLA Modules:
  0.0 486.9 jit_solution(6931362419333559090)
XLA Ops:
  7.2 1.5 copy-done
  13.1 2.4 broadcast_add_fusion.1
  20.8 39.2 %open_team.1 = (bf16[4,2,64,2048]{3,2,1,0:T(8,128)(2,1)}, bf16[2048,768]{1,0:T(8,128)(2,1)}, bf16[256,2048]{1,0:T(8,128)(2,1)S(1)}, bf16[512,3072]{1,0:T(8,128)(2,1)}, s32[4,8,128]{2,1,0:T(8,128)S(1)}) custom-call(bf16[64,2048]{1,0:T(8,128)(2,1)S(1)} %get-tuple-element.115.refs_0_, bf16[512,1024]{1,0:T(8,128)(2,1)S(1)} %copy-done.15, ...), custom_call_target="tpu_custom_call" | custom-call | bytes 120000000 | tf_op jit(solution)/shard_map/open_team/pallas_call | solution.py:308
  61.0 4.1 copy.82
  65.8 4.2 pack_runs.1
  69.9 7.3 %all-to-all-start = ((bf16[4,4,16,2048]{3,2,1,0:T(8,128)(2,1)}), bf16[4,4,16,2048]{3,2,1,0:T(8,128)(2,1)S(1)}, u32[]{:S(2)}, u32[]{:S(2)}) async-start(bf16[4,4,16,2048]{3,2,1,0:T(8,128)(2,1)} %pack_runs.1), calls=%async_computation | async-start | bytes 2097152 | tf_op jit(solution)/shard_map/all_to_all | solution.py:1234
  81.3 10.8 %attend.1 = (f32[512,2048]{1,0:T(8,128)}, bf16[512,256]{1,0:T(8,128)(2,1)}, bf16[512,256]{1,0:T(8,128)(2,1)}, bf16[512,256]{1,0:T(8,128)(2,1)}, bf16[512,256]{1,0:T(8,128)(2,1)}) custom-call(bf16[512,2048]{1,0:T(8,128)(2,1)} %bitcast.120, bf16[2048,768]{1,0:T(8,128)(2,1)} %get-tuple-element.62.qkv_ref, bf16[256,2048]{1,0:T(8,128)(2,1)} %copy-done.4, ...), custom_call_target="tpu_custom_call" | custom-call | bytes 36000000 | tf_op jit(solution)/shard_map/attend/pallas_call | solution.py:848
  92.0 2.2 copy-done.3
  94.2 45.0 %team_sum.3.branch_out = f32[64,2048]{1,0:T(8,128)S(1)} custom-call(f32[4,2,64,2048]{3,2,1,0:T(8,128)S(1)} %bitcast.102), custom_call_target="tpu_custom_call" | custom-call | bytes 60000000 | tf_op jit(solution)/shard_map/team_sum/pallas_call | solution.py:437
  139.4 7.4 %mix_second.1 = (f32[4,64,2048]{2,1,0:T(8,128)}, bf16[64,2048]{1,0:T(8,128)(2,1)S(1)}, bf16[64,2048]{1,0:T(8,128)(2,1)S(1)}, f32[64,2048]{1,0:T(8,128)S(1)}, f32...) custom-call(s32[4]{0:T(128)S(1)} %and_select_fusion.13.source, ...), custom_call_target="tpu_custom_call" | custom-call | bytes 15000000 | tf_op jit(solution)/shard_map/mix_second/pallas_call | solution.py:1139
  149.8 35.0 %team_gather.2 = (bf16[4,2,64,2048]{3,2,1,0:T(8,128)(2,1)S(1)}, bf16[4,2,64,2048]{3,2,1,0:T(8,128)(2,1)S(1)}) custom-call(bf16[64,2048]{1,0:T(8,128)(2,1)S(1)} %get-tuple-element.68.refs_0_, bf16[64,2048]{1,0:T(8,128)(2,1)S(1)} %get-tuple-element.69.refs_1_), custom_call_target="tpu_custom_call" | custom-call | bytes 120000000 | tf_op jit(solution)/shard_map/team_gather/pallas_call | solution.py:186
  187.4 33.9 %ffn.1 = (bf16[512,2048]{1,0:T(8,128)(2,1)}, bf16[512,2048]{1,0:T(8,128)(2,1)}, bf16[2048,1536]{1,0:T(8,128)(2,1)}, bf16[2048,1536]{1,0:T(8,128)(2,1)}) custom-call(bf16[512,2048]{1,0:T(8,128)(2,1)} %bitcast.105, bf16[512,2048]{1,0:T(8,128)(2,1)} %bitcast.106, bf16[2048,3072]{1,0:T(8,128)(2,1)} %all-gather.2.cloned.1.call-done.gate_ref.up_ref, ...), custom_call_target="tpu_custom_call" | custom-call | bytes 90000000 | tf_op jit(solution)/shard_map/ffn/pallas_call | solution.py:750
  222.1 1.6 copy-done.9
  223.7 1.6 copy-done.10
  225.3 41.8 %team_sum.4 = (f32[64,2048]{1,0:T(8,128)S(1)}, f32[64,2048]{1,0:T(8,128)S(1)}) custom-call(bf16[4,2,64,2048]{3,2,1,0:T(8,128)(2,1)S(1)} %bitcast.108, bf16[4,2,64,2048]{3,2,1,0:T(8,128)(2,1)S(1)} %bitcast.109), custom_call_target="tpu_custom_call" | custom-call | bytes 120000000 | tf_op jit(solution)/shard_map/team_sum/pallas_call | solution.py:437
  267.2 9.7 %back_second.1 = (bf16[4,64,2048]{2,1,0:T(8,128)(2,1)S(1)}, f32[4,64,2048]{2,1,0:T(8,128)}, bf16[64,2048]{1,0:T(8,128)(2,1)S(1)}, f32[8,2048]{1,0:T(8,128)S(1)}, f32[4,8]{1,0:T(4,128)S(1)}) custom-call(f32[4,64,2048]{2,1,0:T(8,128)} %get-tuple-element.66.middle, bf16[4,64,2048]{2,1,0:T(8,128)(2,1)S(1)} %copy-done.20, ...), custom_call_target="tpu_custom_call" | custom-call | bytes 15000000 | tf_op jit(solution)/shard_map/back_second/pallas_call | solution.py:1139
  277.8 20.5 %team_gather.3 = bf16[4,2,64,2048]{3,2,1,0:T(8,128)(2,1)S(1)} custom-call(bf16[64,2048]{1,0:T(8,128)(2,1)S(1)} %get-tuple-element.83.refs_0_), custom_call_target="tpu_custom_call" | custom-call | bytes 60000000 | tf_op jit(solution)/shard_map/team_gather/pallas_call | solution.py:186
  299.7 14.9 %attend_back.1 = (bf16[512,2048]{1,0:T(8,128)(2,1)}, bf16[2048,1024]{1,0:T(8,128)(2,1)}) custom-call(bf16[512,2048]{1,0:T(8,128)(2,1)} %bitcast.101, bf16[512,2048]{1,0:T(8,128)(2,1)} %bitcast.121, bf16[2048,768]{1,0:T(8,128)(2,1)} %get-tuple-element.62.qkv_ref, bf16[256,2048]{1,0:T(8,128)(2,1)} %copy-done.4, bf16[512,256]{1,0:T(8,128)(2,1)} %get-tuple-element.84.q_ref, ...), custom_call_target="tpu_custom_call" | custom-call | bytes 60000000 | tf_op jit(solution)/shard_map/attend_back/pallas_call | solution.py:905
  315.6 2.0 copy.67
  317.7 1.6 copy-done.7
  319.3 1.4 copy-done.11
  320.7 52.0 %team_sum.5 = (f32[64,2048]{1,0:T(8,128)S(1)}, bf16[4,128,1536]{2,1,0:T(8,128)(2,1)S(1)}) custom-call(bf16[4,2,64,2048]{3,2,1,0:T(8,128)(2,1)S(1)} %bitcast.107, bf16[512,1536]{1,0:T(8,128)(2,1)S(1)} %copy-done.11), custom_call_target="tpu_custom_call" | custom-call | bytes 60000000 | tf_op jit(solution)/shard_map/team_sum/pallas_call | solution.py:437
  373.9 7.7 %back_first.1 = (bf16[4,64,2048]{2,1,0:T(8,128)(2,1)S(1)}, f32[8,2048]{1,0:T(8,128)S(1)}, f32[4,8]{1,0:T(4,128)S(1)}) custom-call(bf16[4,64,2048]{2,1,0:T(8,128)(2,1)S(1)} %bitcast.100, f32[4,64,2048]{2,1,0:T(8,128)S(1)} %copy-done.8, f32[64,2048]{1,0:T(8,128)S(1)} %team_sum.3.branch_out, f32[64,2048]{1,0:T(8,128)S(1)} %get-tuple-element.90.grad_in, ...), custom_call_target="tpu_custom_call" | custom-call | bytes 15000000 | tf_op jit(solution)/shard_map/back_first/pallas_call | solution.py:1139
  382.9 2.0 copy.70
  385.0 1.4 copy-done.12
  386.4 1.4 copy-done.14
  387.8 48.9 %close_team.1 = (bf16[4,2,16,4,2048]{4,3,2,1,0:T(4,128)(2,1)}, bf16[4,2,16,4,2048]{4,3,2,1,0:T(4,128)(2,1)}, f32[8,24,256]{2,1,0:T(8,128)S(1)}, f32[128,4096]{1,...) custom-call(bf16[4,16,4,2048]{3,2,1,0:T(4,128)(2,1)S(1)} %bitcast.103, bf16[4,16,4,2048]{3,2,1,0:T(4,128)(2,1)S(1)} %bitcast.104, ...), custom_call_target="tpu_custom_call" | custom-call | bytes 180000000 | tf_op jit(solution)/shard_map/close_team/pallas_call | solution.py:636
  438.1 26.1 %team_rows.1 = (f32[128,1024]{1,0:T(8,128)S(1)}, f32[128,1024]{1,0:T(8,128)S(1)}, f32[128,1024]{1,0:T(8,128)S(1)}, f32[1024,128]{1,0:T(8,128)S(1)}) custom-call(bf16[512,1024]{1,0:T(8,128)(2,1)S(1)} %copy-done.21), custom_call_target="tpu_custom_call" | custom-call | bytes 60000000 | tf_op jit(solution)/shard_map/team_rows/pallas_call | solution.py:530
  465.6 4.1 copy.93
  469.6 1.3 copy.94
  474.1 1.3 copy.99
  476.5 1.3 copy.100
  (154 shorter events, 36.6 us)
Async XLA Ops:
  7.2 1.6 copy-start
  7.2 180.2 %all-gather.2.cloned.1.call-start = ((), (), s32[]{:S(2)}) async-start(), calls=%async_computation.4 | async-start | bytes 15728640 | tf_op jit(solution)/shard_map/all_gather | solution.py:1230
  11.0 2.0 copy-start.40
  11.0 2.0 copy-start.41
  13.1 2.8 copy-start.38
  65.8 11.8 %copy-start.44 = (s32[1,4]{1,0:T(1,128)S(1)}, s32[1,4]{1,0:T(1,128)}, u32[]{:S(2)}) copy-start(s32[1,4]{1,0:T(1,128)} %param.15) | copy-start | bytes 52
  65.8 13.5 %copy-start.42 = (f32[64]{0:T(128)S(1)}, f32[64]{0:T(128)}, u32[]{:S(2)}) copy-start(f32[64]{0:T(128)} %constant.173) | copy-start | bytes 772
  69.9 69.4 %all-to-all-start = ((bf16[4,4,16,2048]{3,2,1,0:T(8,128)(2,1)}), bf16[4,4,16,2048]{3,2,1,0:T(8,128)(2,1)S(1)}, u32[]{:S(2)}, u32[]{:S(2)}) async-start(bf16[4,4,16,2048]{3,2,1,0:T(8,128)(2,1)} %pack_runs.1), calls=%async_computation | async-start | bytes 2097152 | tf_op jit(solution)/shard_map/all_to_all | solution.py:1234
  77.3 240.4 %reduce-scatter.4.cloned.1.call-start = ((), (), s32[]{:S(2)}) async-start(), calls=%async_computation.5 | async-start | bytes 7864320 | tf_op jit(solution)/shard_map/reduce_scatter | solution.py:1281
  92.0 2.2 copy-start.3
  94.2 45.0 %copy-start.36 = (f32[64,4,6]{2,0,1:T(8,128)S(1)}, f32[64,4,6]{2,0,1:T(8,128)}, u32[]{:S(2)}) copy-start(f32[64,4,6]{2,0,1:T(8,128)} %get-tuple-element.129) | copy-start | bytes 18436
  94.2 45.1 %copy-start.39 = (f32[2,2048,6]{1,2,0:T(8,128)S(1)}, f32[2,2048,6]{1,2,0:T(8,128)}, u32[]{:S(2)}) copy-start(f32[2,2048,6]{1,2,0:T(8,128)} %copy-done.38) | copy-start | bytes 294916
  221.3 163.6 %reduce-scatter.6.cloned.1.call-start = ((), (), s32[]{:S(2)}) async-start(), calls=%async_computation.6 | async-start | bytes 7864320 | tf_op jit(solution)/shard_map/reduce_scatter | solution.py:1281
  222.1 214.7 %reduce-scatter.8.cloned.1.call-start = ((), (), s32[]{:S(2)}) async-start(), calls=%async_computation.7 | async-start | bytes 5242880 | tf_op jit(solution)/shard_map/reduce_scatter | solution.py:1281
  222.1 1.6 copy-start.9
  223.7 1.6 copy-start.10
  225.3 41.9 %copy-start.20 = (bf16[4,64,2048]{2,1,0:T(8,128)(2,1)S(1)}, bf16[4,64,2048]{2,1,0:T(8,128)(2,1)}, u32[]{:S(2)}) copy-start(bf16[4,64,2048]{2,1,0:T(8,128)(2,1)} %copy-done.19) | copy-start | bytes 3145732
  225.3 41.9 %copy-start.25 = (f32[64,2048]{1,0:T(8,128)S(1)}, f32[64,2048]{1,0:T(8,128)}, u32[]{:S(2)}) copy-start(f32[64,2048]{1,0:T(8,128)} %copy-done.24) | copy-start | bytes 1572868
  225.3 41.9 %copy-start.27 = (f32[4,64,8]{2,1,0:T(8,128)S(1)}, f32[4,64,8]{2,1,0:T(8,128)}, u32[]{:S(2)}) copy-start(f32[4,64,8]{2,1,0:T(8,128)} %copy-done.26) | copy-start | bytes 24580
  225.3 41.9 %copy-start.29 = (f32[4,64,8]{2,1,0:T(8,128)S(1)}, f32[4,64,8]{2,1,0:T(8,128)}, u32[]{:S(2)}) copy-start(f32[4,64,8]{2,1,0:T(8,128)} %copy-done.28) | copy-start | bytes 24580
  277.8 36.8 %copy-start.30 = (f32[8,2048]{1,0:T(8,128)}, f32[8,2048]{1,0:T(8,128)S(1)}, u32[]{:S(2)}) copy-start(f32[8,2048]{1,0:T(8,128)S(1)} %get-tuple-element.93) | copy-start | bytes 196612
  317.6 1.6 copy-start.7
  319.3 1.4 copy-start.11
  320.7 53.2 %copy-start.8 = (f32[4,64,2048]{2,1,0:T(8,128)S(1)}, f32[4,64,2048]{2,1,0:T(8,128)}, u32[]{:S(2)}) copy-start(f32[4,64,2048]{2,1,0:T(8,128)} %get-tuple-element.82.top) | copy-start | bytes 6291460
  373.9 8.7 %copy-start.31 = (f32[8,2048]{1,0:T(8,128)S(1)}, f32[8,2048]{1,0:T(8,128)}, u32[]{:S(2)}) copy-start(f32[8,2048]{1,0:T(8,128)} %copy-done.30) | copy-start | bytes 196612
  385.0 1.4 copy-start.12
  386.4 1.4 copy-start.14
  465.6 4.1 copy-start.35
  471.0 3.2 copy-start.34
  474.1 2.3 copy-start.33
  476.5 2.3 copy-start.32
  476.5 3.7 copy-start.1
  (18 other events, 18.9 us)
Sparse Core Ops, SparseCore 0:
  61.1 124.4 all-gather.1
  221.5 71.4 reduce-scatter.3
  296.0 70.2 reduce-scatter.5
  369.0 53.7 reduce-scatter.7

commit v4 on v3

--- a/solution.py
+++ b/solution.py
@@ -172,7 +172,7 @@
 
 def params(collective_id):
     return pltpu.CompilerParams(
-        collective_id=collective_id, has_side_effects=True, vmem_limit_bytes=48 << 20
+        collective_id=collective_id, has_side_effects=True, vmem_limit_bytes=60 << 20
     )
 
 
@@ -186,7 +186,7 @@
     outs = pl.pallas_call(
         functools.partial(gather_kernel, amount, owners, cores),
         out_shape=[jax.ShapeDtypeStruct((owners, cores, *v.shape), v.dtype) for v in values],
-        in_specs=[ANY] * amount,
+        in_specs=[INSIDE] * amount,
         out_specs=[ANY] * amount,
         scratch_shapes=gather_sems(amount, owners),
         compiler_params=params(collective_id),
@@ -314,7 +314,7 @@
             jax.ShapeDtypeStruct((depth, 3 * units), value.dtype),
             jax.ShapeDtypeStruct((owners, *note.shape), note.dtype),
         ],
-        in_specs=[ANY] + [FAR] * 7 + [INSIDE],
+        in_specs=[INSIDE] + [FAR] * 7 + [INSIDE],
         out_specs=[ANY] * 3 + [FAR] + [INSIDE],
         scratch_shapes=[
             pltpu.SemaphoreType.DMA((4,)),
@@ -344,11 +344,12 @@
     outs, refs = refs[:amount], refs[amount:]
     if swapped:
         rows, refs = refs[0], refs[1:]
-    pairs, halves, from_left, from_right = [
-        refs[k * amount : (k + 1) * amount] for k in range(4)
+    pairs, halves, from_left, from_right, own = [
+        refs[k * amount : (k + 1) * amount] for k in range(5)
     ]
-    total, sent_pair, came_pair, sent, came_left, came_right = refs[4 * amount : 4 * amount + 6]
-    swap = refs[4 * amount + 6 :]
+    refs = refs[5 * amount :]
+    total, sent_pair, came_pair, sent, came_left, came_right, load = refs[:7]
+    swap = refs[7:]
     here, core, pair, right, left = ring(owners, cores)
     if swapped:
         greet(around("ctx", owners) + around("tensor", cores))
@@ -357,6 +358,9 @@
     order = [k // 2 if k % 2 else owners - 1 - k // 2 for k in range(owners)]
     for i in range(amount):
         for block in order:
+            pltpu.make_async_copy(
+                parts[i].at[block, core], own[i].at[block], load.at[i, block]
+            ).start()
             send(
                 parts[i].at[block, pair],
                 pairs[i].at[block],
@@ -370,9 +374,8 @@
 
     def add_up(i, block, more, arrived, came):
         landed(pairs[i].at[block], came_pair.at[i, block])
-        total[...] = parts[i][block, core].astype(jnp.float32) + pairs[i][block].astype(
-            jnp.float32
-        )
+        landed(own[i].at[block], load.at[i, block])
+        total[...] = own[i][block].astype(jnp.float32) + pairs[i][block].astype(jnp.float32)
 
         @pl.when(more)
         def _():
@@ -413,7 +416,7 @@
 
         outs[i][...] = total[...]
     if swapped:
-        swap_rest(summed, rows, *swap, owners, (), 0)
+        swap_rest(summed, rows, *swap, owners)
     for i in range(amount):
         for block in range(owners):
             landed(pairs[i].at[block], sent_pair.at[i, block])
@@ -438,11 +441,11 @@
         functools.partial(scatter_kernel, amount, bool(more), owners, cores),
         out_shape=[jax.ShapeDtypeStruct((mine, width), jnp.float32)] * amount
         + [jax.ShapeDtypeStruct(held_shape(m, owners), m.dtype) for m in more],
-        in_specs=[INSIDE] * amount + [FAR] * len(more),
+        in_specs=[ANY] * amount + [FAR] * len(more),
         out_specs=[INSIDE] * amount + [FAR] * len(more),
-        scratch_shapes=blocks * 4
+        scratch_shapes=blocks * 5
         + [pltpu.VMEM((mine, width), jnp.float32)]
-        + [pltpu.SemaphoreType.DMA((amount, owners)) for _ in range(5)]
+        + [pltpu.SemaphoreType.DMA((amount, owners)) for _ in range(6)]
         + [sem for m in more for sem in swap_sems(owners)],
         compiler_params=params(collective_id),
         cost_estimate=cost(20 * amount),
@@ -464,21 +467,65 @@
     pltpu.make_async_copy(rows(here), held.at[here], local).start()
 
 
-def put_rows(held, source, outs, block, half, halves):
+def put_rows(rows, outs, block, half, halves):
     amount = len(outs)
-    units = held.shape[2] // amount
+    units = rows.shape[1] // amount
     for j in range(units // block):
-        start = pl.multiple_of((source * halves + half) * units + j * block, block)
+        start = half * units + j * block
         for i, out in enumerate(outs):
             first = (j * amount + i) * block
-            piece = held[source, :, first : first + block].astype(jnp.float32)
+            piece = rows[:, first : first + block].astype(jnp.float32)
             if i < amount - 1:
-                out[:, pl.ds(start, block)] = piece
+                out[:, start : start + block] = piece
             else:
-                out[pl.ds(start, block), :] = piece.T
-
-
-def swap_rest(summed, held, local, sent, came, owners, outs, block, half=0, halves=1):
+                out[start : start + block, :] = piece.T
+
+
+def place_kernel(block, where, own_a, far_a, own_b, far_b, early, late, attn, *outs):
+    core = where[0]
+    for own, far, out in ((own_a, far_a, outs[0]), (own_b, far_b, outs[1])):
+        out[0, core] = own[0]
+        out[0, out.shape[1] - 1 - core] = far[0]
+    put_rows(early[0], outs[2:5], block, 0, 2)
+    put_rows(late[0], outs[2:5], block, 1, 2)
+    put_rows(attn[0], outs[5:], outs[5].shape[1], 0, 1)
+
+
+def place_all(streams, early, late, attn):
+    owners, cores = lax.axis_size("ctx"), lax.axis_size("tensor")
+    run = streams[0].shape
+    block = late.shape[2] // (3 * BLOCKS // 2)
+
+    def lead(shape):
+        return pl.BlockSpec((1, *shape[1:]), lambda c, _: (c,) + (0,) * (len(shape) - 1))
+
+    both = (run[0], cores, *run[1:])
+    specs, shapes = [lead(both)] * 2, [jax.ShapeDtypeStruct(both, streams[0].dtype)] * 2
+    for amount, units in ((3, 2 * late.shape[2] // 3), (4, attn.shape[2] // 4)):
+        count = late.shape[1]
+        specs += [pl.BlockSpec((count, units), lambda c, _: (0, c))] * (amount - 1)
+        specs.append(pl.BlockSpec((units, count), lambda c, _: (c, 0)))
+        wide = jax.ShapeDtypeStruct((count, owners * units), jnp.float32)
+        shapes += [wide] * (amount - 1)
+        shapes.append(jax.ShapeDtypeStruct((owners * units, count), jnp.float32))
+    return pl.pallas_call(
+        functools.partial(place_kernel, block),
+        grid_spec=pltpu.PrefetchScalarGridSpec(
+            num_scalar_prefetch=1,
+            grid=(owners,),
+            in_specs=[lead(v.shape) for v in (*streams, early, late, attn)],
+            out_specs=specs,
+        ),
+        out_shape=shapes,
+        compiler_params=pltpu.CompilerParams(
+            dimension_semantics=("arbitrary",), vmem_limit_bytes=60 << 20
+        ),
+        cost_estimate=cost(7),
+        name="place_all",
+    )(lax.axis_index("tensor")[None].astype(jnp.int32), *streams, early, late, attn)
+
+
+def swap_rest(summed, held, local, sent, came, owners):
     here = lax.axis_index("ctx")
     count = summed.shape[0] // owners
     own = summed.at[pl.ds(pl.multiple_of(here * count, count), count), :]
@@ -488,8 +535,6 @@
             pltpu.make_async_copy(own, held.at[here], local).wait()
         else:
             landed(held.at[source], came.at[source])
-        if outs:
-            put_rows(held, source, outs, block, half, halves)
     for step in range(1, owners):
         other = lax.rem(here + step, owners)
         landed(held.at[other], sent.at[other])
@@ -507,33 +552,25 @@
     ]
 
 
-def swap_outs(summed, owners, amount, halves=1):
-    count, units = summed.shape[0] // owners, summed.shape[1] // amount * halves
-    shapes = [(count, owners * units)] * (amount - 1) + [(owners * units, count)]
-    return [jax.ShapeDtypeStruct(shape, jnp.float32) for shape in shapes]
-
-
 def around(axis, size):
     index = lax.axis_index(axis)
     return [{axis: lax.rem(index + step, size)} for step in range(1, size)]
 
 
-def swap_kernel_alone(owners, block, amount, *refs):
-    summed, outs, scratch = refs[0], refs[1 : 1 + amount], refs[1 + amount :]
+def swap_kernel_alone(owners, summed, held, *sems):
     greet(around("ctx", owners))
-    swap_first(summed, *scratch, owners)
-    swap_rest(summed, *scratch, owners, outs, block)
-
-
-def team_rows(collective_id, summed, amount, block):
+    swap_first(summed, held, *sems, owners)
+    swap_rest(summed, held, *sems, owners)
+
+
+def team_rows(collective_id, summed):
     owners = lax.axis_size("ctx")
     return pl.pallas_call(
-        functools.partial(swap_kernel_alone, owners, block, amount),
-        out_shape=swap_outs(summed, owners, amount),
-        in_specs=[ANY],
-        out_specs=[INSIDE] * amount,
-        scratch_shapes=[pltpu.VMEM(held_shape(summed, owners), summed.dtype)]
-        + swap_sems(owners),
+        functools.partial(swap_kernel_alone, owners),
+        out_shape=jax.ShapeDtypeStruct(held_shape(summed, owners), summed.dtype),
+        in_specs=[INSIDE],
+        out_specs=ANY,
+        scratch_shapes=swap_sems(owners),
         compiler_params=params(collective_id),
         cost_estimate=cost(20),
         name="team_rows",
@@ -541,13 +578,13 @@
 
 
 def close_kernel(amount, shards_in, owners, cores, *refs):
-    values, mixed, grads, early = refs[:amount], refs[amount], refs[amount + 1], refs[amount + 2]
-    refs = refs[amount + 3 :]
-    outs, summed, grad_outs = refs[:amount], refs[amount], refs[amount + 1 : amount + 4]
-    refs = refs[amount + 4 :]
-    pairs, half, quarters, blocks, local, sent, came = refs[:7]
-    sent_c, came_c, sent_s, came_s, sent_b, came_b = refs[7:13]
-    swap = refs[13:]
+    values, mixed, grads = refs[:amount], refs[amount], refs[amount + 1]
+    refs = refs[amount + 2 :]
+    outs, mix_out, late = refs[:amount], refs[amount], refs[amount + 1]
+    summed, refs = refs[amount + 2], refs[amount + 3 :]
+    pairs, half, quarters, blocks, sent, came = refs[:6]
+    sent_c, came_c, sent_s, came_s, sent_b, came_b = refs[6:12]
+    swap = refs[12:]
     here, core, pair, right, left = ring(owners, cores)
     index = lax.axis_index("shard")
     near = [lax.rem(here + step, owners) for step in range(1, owners)]
@@ -563,9 +600,7 @@
         {"tensor": pair},
     )
     for i in range(amount):
-        target = outs[i].at[:, core]
-        send(values[i], target, sent.at[i], came.at[i], {"tensor": pair})
-        pltpu.make_async_copy(values[i], target, local.at[i]).start()
+        send(values[i], outs[i], sent.at[i], came.at[i], {"tensor": pair})
     landed(pairs, came.at[amount])
     half[...] = mixed[:, pl.ds(pl.multiple_of(core * wide, wide), wide)] + pairs[...]
     for other in near:
@@ -576,6 +611,7 @@
             came_c.at[here],
             {"ctx": other},
         )
+    swap_first(grads, late, *swap, owners)
     total = half[:, pl.ds(pl.multiple_of(here * thin, thin), thin)]
     for other in near:
         landed(quarters.at[other], came_c.at[other])
@@ -585,7 +621,6 @@
         send(
             blocks.at[index], blocks.at[index], sent_s.at[other], came_s.at[index], {"shard": other}
         )
-    swap_first(grads, *swap, owners)
     for other in others:
         landed(blocks.at[other], came_s.at[other])
     total = blocks[0]
@@ -611,24 +646,26 @@
     for owner in range(owners):
         landed(place(owner, pair), came_b.at[owner, pair])
         landed(place(owner, core), sent_b.at[owner])
+    for owner in range(owners):
+        for half_of in range(cores):
+            found = summed[half_of * owners + owner]
+            start = (half_of * owners + owner) * thin
+            for row in range(mix_out.shape[0] * mix_out.shape[1]):
+                k, h = row // mix_out.shape[1], row % mix_out.shape[1]
+                mix_out[k, h : h + 1, start : start + thin] = found[row : row + 1, :]
     for other in near:
         landed(place(other, core), sent_b.at[owners + other])
         landed(quarters.at[other], sent_c.at[other])
     for other in others:
         landed(blocks.at[other], sent_s.at[other])
     landed(pairs, sent.at[amount])
-    block = grads.shape[1] // (3 * BLOCKS // 2)
-    for source in range(owners):
-        put_rows(early, source, grad_outs, block, 0, 2)
-    swap_rest(grads, *swap, owners, grad_outs, block, 1, 2)
+    swap_rest(grads, late, *swap, owners)
     for i in range(amount):
-        target = outs[i].at[:, core]
-        landed(outs[i].at[:, pair], came.at[i])
-        landed(target, sent.at[i])
-        pltpu.make_async_copy(values[i], target, local.at[i]).wait()
-
-
-def close_team(collective_id, early, grads, mixed, *values):
+        landed(outs[i], came.at[i])
+        landed(values[i], sent.at[i])
+
+
+def close_team(collective_id, grads, mixed, *values):
     shards_in, owners, cores = [lax.axis_size(a) for a in ("shard", "ctx", "tensor")]
     amount = len(values)
     height, width = mixed.shape
@@ -636,18 +673,18 @@
     out = pl.pallas_call(
         functools.partial(close_kernel, amount, shards_in, owners, cores),
         out_shape=[
-            jax.ShapeDtypeStruct((v.shape[0], cores, *v.shape[1:]), v.dtype) for v in values
+            jax.ShapeDtypeStruct(v.shape, v.dtype) for v in values
         ]
-        + [jax.ShapeDtypeStruct((cores * owners, height, thin), jnp.float32)]
-        + swap_outs(grads, owners, 3, 2),
-        in_specs=[ANY] * amount + [INSIDE, FAR, INSIDE],
-        out_specs=[ANY] * amount + [INSIDE] * 4,
+        + [jax.ShapeDtypeStruct((height // 2, 2, width), jnp.float32)]
+        + [jax.ShapeDtypeStruct(held_shape(grads, owners), grads.dtype)],
+        in_specs=[INSIDE] * (amount + 2),
+        out_specs=[ANY] * amount + [INSIDE, ANY],
         scratch_shapes=[
+            pltpu.VMEM((cores * owners, height, thin), jnp.float32),
             pltpu.VMEM((height, width // cores), jnp.float32),
             pltpu.VMEM((height, width // cores), jnp.float32),
             pltpu.VMEM((owners, height, thin), jnp.float32),
             pltpu.VMEM((shards_in, height, thin), jnp.float32),
-            pltpu.SemaphoreType.DMA((amount,)),
             pltpu.SemaphoreType.DMA((amount + 1,)),
             pltpu.SemaphoreType.DMA((amount + 1,)),
             pltpu.SemaphoreType.DMA((owners,)),
@@ -657,14 +694,12 @@
             pltpu.SemaphoreType.DMA((2 * owners,)),
             pltpu.SemaphoreType.DMA((owners, cores)),
         ]
-        + [pltpu.VMEM(held_shape(grads, owners), grads.dtype)]
         + swap_sems(owners),
         compiler_params=params(collective_id),
         cost_estimate=cost(60),
         name="close_team",
-    )(*values, mixed, grads, early)
-    mixed = out[amount].transpose(1, 0, 2).reshape(height, width)
-    return mixed, out[:amount], out[amount + 1 :]
+    )(*values, mixed, grads)
+    return out[amount], out[:amount], out[amount + 1]
 
 
 def ffn_kernel(
@@ -782,18 +817,19 @@
 
 
 def pack_kernel(sent, value, out):
-    out[0] = value[...]
+    for i in range(value.shape[1]):
+        out[0, i] = value[:, i, :]
 
 
 def pack_runs(value, sent, part):
-    total, rows_in, width = value.shape
+    rows_in, total, width = value.shape
     return pl.pallas_call(
         pack_kernel,
         grid_spec=pltpu.PrefetchScalarGridSpec(
             num_scalar_prefetch=1,
             grid=(sent.shape[0],),
             in_specs=[
-                pl.BlockSpec((total, part, width), lambda c, first: (0, first[c], 0)),
+                pl.BlockSpec((part, total, width), lambda c, first: (first[c], 0, 0)),
             ],
             out_specs=pl.BlockSpec((1, total, part, width), lambda c, first: (c, 0, 0, 0)),
         ),
@@ -850,7 +886,7 @@
         out_shape=[jax.ShapeDtypeStruct((total, out_w.shape[1]), jnp.float32)] + [low] * 4,
         in_specs=[INSIDE] * 6,
         out_specs=[INSIDE] * 5,
-        compiler_params=pltpu.CompilerParams(vmem_limit_bytes=56 << 20),
+        compiler_params=pltpu.CompilerParams(vmem_limit_bytes=60 << 20),
         cost_estimate=cost(12),
         name="attend",
     )(u, qkv, out_w, turns, placing, placed)
@@ -911,7 +947,7 @@
         in_specs=[INSIDE] * 11,
         out_specs=[INSIDE] * 2,
         scratch_shapes=[pltpu.VMEM((total, 3 * count), jnp.bfloat16)],
-        compiler_params=pltpu.CompilerParams(vmem_limit_bytes=56 << 20),
+        compiler_params=pltpu.CompilerParams(vmem_limit_bytes=60 << 20),
         cost_estimate=cost(20),
         name="attend_back",
     )(dy, u, qkv, out_w, q, k, v, o, turns, placing, placed)
@@ -1146,7 +1182,7 @@
         ),
         out_shape=[o[1] for o in outs],
         compiler_params=pltpu.CompilerParams(
-            dimension_semantics=("arbitrary",), vmem_limit_bytes=48 << 20
+            dimension_semantics=("arbitrary",), vmem_limit_bytes=60 << 20
         ),
         cost_estimate=cost(5),
         name=name,
@@ -1230,7 +1266,7 @@
     ffn_weights = lax.all_gather(packed, "shard", axis=0, tiled=True)
     every = notes[:, 0, :owners]
     sent = jnp.sum(jnp.where(every // rows_here == here, every % rows_here, 0), 1) // part + core
-    packed = pack_runs(cotangent.transpose(1, 0, 2), sent, part)
+    packed = pack_runs(cotangent, sent, part)
     arrived = lax.all_to_all(packed, "ctx", split_axis=0, concat_axis=0, tiled=True)
     attn_part, queries, keys, values, attended = attend(
         attn_input, qkv, out_w, turns, placing, placed
@@ -1342,14 +1378,27 @@
     def runs(value):
         return value.transpose(1, 0, 2).reshape(owners, part, stream_total, width)
 
-    mixed, (streams_out, grad_streams), (grad_gate, grad_up, grad_down) = close_team(
-        7, early_rows, late_sum, mixed, runs(final), runs(grad_current)
+    own_final, own_grad = runs(final), runs(grad_current)
+    mixed, (far_final, far_grad), late_rows = close_team(
+        7, late_sum, mixed, own_final, own_grad
     )
     mixed, attn_sum = lax.optimization_barrier((mixed, attn_sum))
-    grad_query, grad_key, grad_value, grad_output = team_rows(8, attn_sum, 4, head_cols)
+    (
+        streams_out,
+        grad_streams,
+        grad_gate,
+        grad_up,
+        grad_down,
+        grad_query,
+        grad_key,
+        grad_value,
+        grad_output,
+    ) = place_all(
+        (own_final, far_final, own_grad, far_grad), early_rows, late_rows, team_rows(8, attn_sum)
+    )
     columns_in = mix_weight.shape[2]
-    grad_mix_weight = mixed[: 2 * columns_in].reshape(columns_in, 2, width).transpose(1, 2, 0)
-    grad_mix_static = mixed[16, : statics.size].reshape(2, stream_total, 8)[:, :, :columns_in]
+    grad_mix_weight = mixed[:columns_in].transpose(1, 2, 0)
+    grad_mix_static = mixed[8, 0, : statics.size].reshape(2, stream_total, 8)[:, :, :columns_in]
 
     return (
         streams_out.reshape(rows_here, stream_total, width),

time: 494 us -> 477 us (0.966)
  local copies, waits for them, and re-layouts: 56.8 us -> 17.5 us
  Pallas kernels: 397 us -> 416 us
    unnamed x102 -> x26, local copies, waits for them, and re-layouts: 49.2 us -> 3.23 us
    pallas_call x1 -> x2, Pallas kernels: 26.1 us -> 35.2 us  [the longest x1 27.2 us: team_rows(): pl.pallas_call(functools.partial(swap_kernel_alone, owners), out_shape=ja...]
  transfers between devices with their start and end apart: 5 -> 5, of which waited for: 0 -> 1; matrix products, arithmetic and copies ran while one was open for 3% -> 3% of each run, Pallas kernels for 61% -> 65%
where the time goes in v4:
time: 477 us; the launch traced here: 470 us
  Pallas kernels  416 us (87%)
  local copies, waits for them, and re-layouts  17.5 us (4%)
  between operations  14.4 us (3%)
  other arithmetic  11.2 us (2%)
  starting transfers between devices  7.67 us (2%)
    pallas_call x3, Pallas kernels, team_sum_and_rows(): pl.pallas_call(functools.partial(scatter_kernel, amount, bool(more), owne...  144 us
    pallas_call x2, Pallas kernels, team_gather(): pl.pallas_call(functools.partial(gather_kernel, amount, owners, cores), o...  58 us
    pallas_call x1, Pallas kernels, close_team(): pl.pallas_call(functools.partial(close_kernel, amount, shards_in, owners,...  46 us
    pallas_call x1, Pallas kernels, open_team(): pl.pallas_call(functools.partial(open_kernel, shards_in, owners, cores),...  40.6 us
    pallas_call x1, Pallas kernels, ffn(): pl.pallas_call(ffn_kernel, grid=(blocks,), in_specs=[whole, whole, pl.Blo...  33.9 us
    pallas_call x3, Pallas kernels, token_call(): pl.pallas_call(kernel, grid_spec=pltpu.PrefetchScalarGridSpec(num_scalar_...  28.2 us
    pallas_call x1, Pallas kernels, team_rows(): pl.pallas_call(functools.partial(swap_kernel_alone, owners), out_shape=ja...  27.2 us
    pallas_call x1, Pallas kernels, attend_back(): pl.pallas_call(attend_back_kernel, out_shape=[jax.ShapeDtypeStruct((total...  14.2 us
  transfers between devices with their start and end apart: 5, of which 1 were waited for; matrix products, arithmetic and copies ran while one was open for 3% of the time, Pallas kernels for 65%

profile of v4, /device:TPU:8, one launch (start us, length us, event | category | flops | bytes accessed | tf_op | source)
XLA Modules:
  0.0 470.3 jit_solution(16650587646434021196)
XLA Ops:
  7.2 1.5 copy-done
  9.2 1.1 convert_reduce_fusion
  11.0 1.2 fusion.2
  12.2 0.7 fusion
  13.1 1.8 broadcast_add_fusion.1
  15.8 1.0 fusion.50
  17.6 40.6 %open_team.1 = (bf16[4,2,64,2048]{3,2,1,0:T(8,128)(2,1)}, bf16[2048,768]{1,0:T(8,128)(2,1)}, bf16[256,2048]{1,0:T(8,128)(2,1)}, bf16[512,3072]{1,0:T(8,128)(2,1)}, s32[4,8,128]{2,1,0:T(8,128)}) custom-call(bf16[64,2048]{1,0:T(8,128)(2,1)} %get-tuple-element.121.refs_0_, bf16[512,1024]{1,0:T(8,128)(2,1)} %refs_1_.1, bf16[512,1024]{1,0:T(8,128)(2,1)} %refs_2_.1, ...), custom_call_target="tpu_custom_call" | custom-call | bytes 120000000 | tf_op jit(solution)/shard_map/open_team/pallas_call | solution.py:308
  59.6 5.1 %pack_runs.1 = bf16[4,4,16,2048]{3,2,1,0:T(8,128)(2,1)} custom-call(s32[4]{0:T(128)} %fusion.48.sent, bf16[128,4,2048]{2,1,0:T(4,128)(2,1)} %value.1), custom_call_target="tpu_custom_call" | custom-call | bytes 6000000 | tf_op jit(solution)/shard_map/pack_runs/pallas_call | solution.py:826
  64.8 7.3 %all-to-all-start = ((bf16[4,4,16,2048]{3,2,1,0:T(8,128)(2,1)}), bf16[4,4,16,2048]{3,2,1,0:T(8,128)(2,1)S(1)}, u32[]{:S(2)}, u32[]{:S(2)}) async-start(bf16[4,4,16,2048]{3,2,1,0:T(8,128)(2,1)} %pack_runs.1), calls=%async_computation | async-start | bytes 2097152 | tf_op jit(solution)/shard_map/all_to_all | solution.py:1270
  72.6 0.9 copy.59.placing
  74.1 1.0 multiply_cosine_fusion
  75.3 0.8 maximum_bitcast_fusion.turns
  76.1 10.8 %attend.1 = (f32[512,2048]{1,0:T(8,128)}, bf16[512,256]{1,0:T(8,128)(2,1)}, bf16[512,256]{1,0:T(8,128)(2,1)}, bf16[512,256]{1,0:T(8,128)(2,1)}, bf16[512,256]{1,0:T(8,128)(2,1)}) custom-call(bf16[512,2048]{1,0:T(8,128)(2,1)} %bitcast.104, bf16[2048,768]{1,0:T(8,128)(2,1)} %get-tuple-element.65.qkv_ref, bf16[256,2048]{1,0:T(8,128)(2,1)} %get-tuple-element.66.out_ref, ...), custom_call_target="tpu_custom_call" | custom-call | bytes 36000000 | tf_op jit(solution)/shard_map/attend/pallas_call | solution.py:884
  86.9 46.3 %team_sum.3.branch_out = f32[64,2048]{1,0:T(8,128)} custom-call(f32[4,2,64,2048]{3,2,1,0:T(8,128)} %bitcast.106), custom_call_target="tpu_custom_call" | custom-call | bytes 60000000 | tf_op jit(solution)/shard_map/team_sum/pallas_call | solution.py:440
  135.7 1.0 copy-done.3
  136.6 8.9 %mix_second.1 = (f32[4,64,2048]{2,1,0:T(8,128)}, bf16[64,2048]{1,0:T(8,128)(2,1)}, bf16[64,2048]{1,0:T(8,128)(2,1)}, f32[64,2048]{1,0:T(8,128)}, f32[64,8]{1,0:T...) custom-call(s32[4]{0:T(128)} %and_select_fusion.13.source, ...), custom_call_target="tpu_custom_call" | custom-call | bytes 15000000 | tf_op jit(solution)/shard_map/mix_second/pallas_call | solution.py:1175
  145.5 36.1 %team_gather.2 = (bf16[4,2,64,2048]{3,2,1,0:T(8,128)(2,1)}, bf16[4,2,64,2048]{3,2,1,0:T(8,128)(2,1)}) custom-call(bf16[64,2048]{1,0:T(8,128)(2,1)} %get-tuple-element.71.refs_0_, bf16[64,2048]{1,0:T(8,128)(2,1)} %get-tuple-element.72.refs_1_), custom_call_target="tpu_custom_call" | custom-call | bytes 120000000 | tf_op jit(solution)/shard_map/team_gather/pallas_call | solution.py:186
  181.6 1.3 all-gather.2.cloned.1.call-done.gate_ref.up_ref
  182.9 33.9 %ffn.1 = (bf16[512,2048]{1,0:T(8,128)(2,1)}, bf16[512,2048]{1,0:T(8,128)(2,1)}, bf16[2048,1536]{1,0:T(8,128)(2,1)}, bf16[2048,1536]{1,0:T(8,128)(2,1)}) custom-call(bf16[512,2048]{1,0:T(8,128)(2,1)} %bitcast.107, bf16[512,2048]{1,0:T(8,128)(2,1)} %bitcast.108, bf16[2048,3072]{1,0:T(8,128)(2,1)} %all-gather.2.cloned.1.call-done.gate_ref.up_ref, ...), custom_call_target="tpu_custom_call" | custom-call | bytes 90000000 | tf_op jit(solution)/shard_map/ffn/pallas_call | solution.py:785
  217.6 42.4 %team_sum.4 = (f32[64,2048]{1,0:T(8,128)}, f32[64,2048]{1,0:T(8,128)}) custom-call(bf16[4,2,64,2048]{3,2,1,0:T(8,128)(2,1)} %bitcast.110, bf16[4,2,64,2048]{3,2,1,0:T(8,128)(2,1)} %bitcast.111), custom_call_target="tpu_custom_call" | custom-call | bytes 120000000 | tf_op jit(solution)/shard_map/team_sum/pallas_call | solution.py:440
  260.0 9.9 %back_second.1 = (bf16[4,64,2048]{2,1,0:T(8,128)(2,1)}, f32[4,64,2048]{2,1,0:T(8,128)}, bf16[64,2048]{1,0:T(8,128)(2,1)}, f32[8,2048]{1,0:T(8,128)}, f32[4,8]{1,0:T(4,128)}) custom-call(f32[4,64,2048]{2,1,0:T(8,128)} %get-tuple-element.69.middle, bf16[4,64,2048]{2,1,0:T(8,128)(2,1)} %get-tuple-element.70.top, f32[64,2048]{1,0:T(8,128)} %get-tuple-element.78.branch_out, ...), custom_call_target="tpu_custom_call" | custom-call | bytes 15000000 | tf_op jit(solution)/shard_map/back_second/pallas_call | solution.py:1175
  269.9 21.9 %team_gather.3 = bf16[4,2,64,2048]{3,2,1,0:T(8,128)(2,1)} custom-call(bf16[64,2048]{1,0:T(8,128)(2,1)} %get-tuple-element.86.refs_0_), custom_call_target="tpu_custom_call" | custom-call | bytes 60000000 | tf_op jit(solution)/shard_map/team_gather/pallas_call | solution.py:186
  291.8 14.2 %attend_back.1 = (bf16[512,2048]{1,0:T(8,128)(2,1)}, bf16[2048,1024]{1,0:T(8,128)(2,1)}) custom-call(bf16[512,2048]{1,0:T(8,128)(2,1)} %bitcast.103, bf16[512,2048]{1,0:T(8,128)(2,1)} %bitcast.105, bf16[2048,768]{1,0:T(8,128)(2,1)} %get-tuple-element.65.qkv_ref, bf16[256,2048]{1,0:T(8,128)(2,1)} %get-tuple-element.66.out_ref, ...), custom_call_target="tpu_custom_call" | custom-call | bytes 60000000 | tf_op jit(solution)/shard_map/attend_back/pallas_call | solution.py:941
  307.4 1.8 copy.61
  309.2 55.1 %team_sum.5 = (f32[64,2048]{1,0:T(8,128)}, bf16[4,128,1536]{2,1,0:T(8,128)(2,1)}) custom-call(bf16[4,2,64,2048]{3,2,1,0:T(8,128)(2,1)} %bitcast.109, bf16[512,1536]{1,0:T(8,128)(2,1)} %reduce-scatter.4.cloned.1.call-done.refs_1_), custom_call_target="tpu_custom_call" | custom-call | bytes 60000000 | tf_op jit(solution)/shard_map/team_sum/pallas_call | solution.py:440
  364.3 9.5 %back_first.1 = (bf16[4,64,2048]{2,1,0:T(8,128)(2,1)}, f32[8,2048]{1,0:T(8,128)}, f32[4,8]{1,0:T(4,128)}) custom-call(bf16[4,64,2048]{2,1,0:T(8,128)(2,1)} %bitcast.97, f32[4,64,2048]{2,1,0:T(8,128)} %get-tuple-element.85.top, f32[64,2048]{1,0:T(8,128)} %team_sum.3.branch_out, f32[64,2048]{1,0:T(8,128)} %get-tuple-element.93.grad_in, ...), custom_call_target="tpu_custom_call" | custom-call | bytes 15000000 | tf_op jit(solution)/shard_map/back_first/pallas_call | solution.py:1175
  373.8 0.9 pad_maximum_fusion
  375.6 3.0 copy.64
  379.3 46.0 %close_team.1 = (bf16[4,16,4,2048]{3,2,1,0:T(4,128)(2,1)}, bf16[4,16,4,2048]{3,2,1,0:T(4,128)(2,1)}, f32[12,2,2048]{2,1,0:T(2,128)}, bf16[4,128,1536]{2,1,0:T(8,128)(2,1)}) custom-call(bf16[4,16,4,2048]{3,2,1,0:T(4,128)(2,1)} %bitcast.98, bf16[4,16,4,2048]{3,2,1,0:T(4,128)(2,1)} %bitcast.100, f32[24,2048]{1,0:T(8,128)} %select_maximum_fusion.refs_2_, ...), custom_call_target="tpu_custom_call" | custom-call | bytes 180000000 | tf_op jit(solution)/shard_map/close_team/pallas_call | solution.py:673
  425.3 1.5 slice_bitcast_fusion.4
  427.6 27.2 %team_rows.1.attn = bf16[4,128,1024]{2,1,0:T(8,128)(2,1)} custom-call(bf16[512,1024]{1,0:T(8,128)(2,1)} %reduce-scatter.8.cloned.1.call-done.summed), custom_call_target="tpu_custom_call" | custom-call | bytes 60000000 | tf_op jit(solution)/shard_map/team_rows/pallas_call | solution.py:568
  455.4 8.0 %place_all.1 = (bf16[4,2,16,4,2048]{4,3,2,1,0:T(4,128)(2,1)}, bf16[4,2,16,4,2048]{4,3,2,1,0:T(4,128)(2,1)}, f32[128,4096]{1,0:T(8,128)}, f32[128,4096]{1,0:T(8,1...) custom-call(s32[1]{0:T(128)} %bitcast.where, ...), custom_call_target="tpu_custom_call" | custom-call | bytes 21000000 | tf_op jit(solution)/shard_map/place_all/pallas_call | solution.py:511
  (77 shorter events, 13.4 us)
Async XLA Ops:
  7.2 1.6 copy-start
  7.2 175.7 %all-gather.2.cloned.1.call-start = ((), (), s32[]{:S(2)}) async-start(), calls=%async_computation.4 | async-start | bytes 15728640 | tf_op jit(solution)/shard_map/all_gather | solution.py:1266
  11.0 4.0 copy-start.2
  11.0 2.0 copy-start.5
  11.0 2.0 copy-start.7
  15.2 1.6 copy-start.10
  59.6 12.7 %copy-start.11 = (s32[1,4]{1,0:T(1,128)S(1)}, s32[1,4]{1,0:T(1,128)}, u32[]{:S(2)}) copy-start(s32[1,4]{1,0:T(1,128)} %param.15) | copy-start | bytes 52
  59.6 14.4 %copy-start.9 = (f32[64]{0:T(128)S(1)}, f32[64]{0:T(128)}, u32[]{:S(2)}) copy-start(f32[64]{0:T(128)} %constant.173) | copy-start | bytes 772
  64.8 70.9 %all-to-all-start = ((bf16[4,4,16,2048]{3,2,1,0:T(8,128)(2,1)}), bf16[4,4,16,2048]{3,2,1,0:T(8,128)(2,1)S(1)}, u32[]{:S(2)}, u32[]{:S(2)}) async-start(bf16[4,4,16,2048]{3,2,1,0:T(8,128)(2,1)} %pack_runs.1), calls=%async_computation | async-start | bytes 2097152 | tf_op jit(solution)/shard_map/all_to_all | solution.py:1270
  72.1 237.1 %reduce-scatter.4.cloned.1.call-start = ((), (), s32[]{:S(2)}) async-start(), calls=%async_computation.5 | async-start | bytes 7864320 | tf_op jit(solution)/shard_map/reduce_scatter | solution.py:1317
  135.7 1.0 copy-start.3
  216.8 162.5 %reduce-scatter.6.cloned.1.call-start = ((), (), s32[]{:S(2)}) async-start(), calls=%async_computation.6 | async-start | bytes 7864320 | tf_op jit(solution)/shard_map/reduce_scatter | solution.py:1317
  217.6 207.7 %reduce-scatter.8.cloned.1.call-start = ((), (), s32[]{:S(2)}) async-start(), calls=%async_computation.7 | async-start | bytes 5242880 | tf_op jit(solution)/shard_map/reduce_scatter | solution.py:1317
  306.0 1.4 copy-start.4
  364.3 9.5 %copy-start.6 = (f32[8,2048]{1,0:T(8,128)S(1)}, f32[8,2048]{1,0:T(8,128)}, u32[]{:S(2)}) copy-start(f32[8,2048]{1,0:T(8,128)} %get-tuple-element.96) | copy-start | bytes 196612
  364.3 10.6 %copy-start.8 = (f32[4,8]{1,0:T(4,128)S(1)}, f32[4,8]{1,0:T(4,128)}, u32[]{:S(2)}) copy-start(f32[4,8]{1,0:T(4,128)} %get-tuple-element.98) | copy-start | bytes 388
  455.4 8.0 %copy-start.1 = (bf16[128,4,2048]{2,1,0:T(4,128)(2,1)S(1)}, bf16[128,4,2048]{2,1,0:T(4,128)(2,1)}, u32[]{:S(2)}) copy-start(bf16[128,4,2048]{2,1,0:T(4,128)(2,1)} %param.14) | copy-start | bytes 6291460
Sparse Core Ops, SparseCore 0:
  58.4 124.4 all-gather.1
  217.0 70.7 reduce-scatter.3
  290.8 70.2 reduce-scatter.5
  363.9 54.2 reduce-scatter.7

commit v5 on v4

--- a/solution.py
+++ b/solution.py
@@ -337,24 +337,18 @@
     return out.reshape(-1, value.shape[1]), qkv, out_w, packed, notes
 
 
-def scatter_kernel(amount, swapped, owners, cores, *refs):
-    parts, refs = refs[:amount], refs[amount:]
-    if swapped:
-        summed, refs = refs[0], refs[1:]
-    outs, refs = refs[:amount], refs[amount:]
-    if swapped:
-        rows, refs = refs[0], refs[1:]
+def scatter_kernel(amount, owners, cores, *refs):
+    parts, outs, refs = refs[:amount], refs[amount : 2 * amount], refs[2 * amount :]
+    greet(line_partners(owners, cores))
+    scatter(amount, owners, cores, parts, outs, refs)
+
+
+def scatter(amount, owners, cores, parts, outs, refs):
     pairs, halves, from_left, from_right, own = [
         refs[k * amount : (k + 1) * amount] for k in range(5)
     ]
-    refs = refs[5 * amount :]
-    total, sent_pair, came_pair, sent, came_left, came_right, load = refs[:7]
-    swap = refs[7:]
+    total, sent_pair, came_pair, sent, came_left, came_right, load = refs[5 * amount :]
     here, core, pair, right, left = ring(owners, cores)
-    if swapped:
-        greet(around("ctx", owners) + around("tensor", cores))
-    else:
-        greet(line_partners(owners, cores))
     order = [k // 2 if k % 2 else owners - 1 - k // 2 for k in range(owners)]
     for i in range(amount):
         for block in order:
@@ -369,9 +363,6 @@
                 {"tensor": pair},
             )
 
-    if swapped:
-        swap_first(summed, rows, *swap, owners)
-
     def add_up(i, block, more, arrived, came):
         landed(pairs[i].at[block], came_pair.at[i, block])
         landed(own[i].at[block], load.at[i, block])
@@ -415,8 +406,6 @@
             total[...] += from_right[i][here].astype(jnp.float32)
 
         outs[i][...] = total[...]
-    if swapped:
-        swap_rest(summed, rows, *swap, owners)
     for i in range(amount):
         for block in range(owners):
             landed(pairs[i].at[block], sent_pair.at[i, block])
@@ -426,32 +415,27 @@
                 landed(halves[i].at[block], sent.at[i, block])
 
 
+def scatter_scratch(amount, owners, block, kind):
+    held = [pltpu.VMEM((owners, *block), kind)] * amount
+    sems = [pltpu.SemaphoreType.DMA((amount, owners)) for _ in range(6)]
+    return held * 5 + [pltpu.VMEM(block, jnp.float32)] + sems
+
+
 def team_sum(collective_id, *values):
-    return team_sum_and_rows(collective_id, None, *values)[0]
-
-
-def team_sum_and_rows(collective_id, summed, *values):
     owners, cores = lax.axis_size("ctx"), lax.axis_size("tensor")
     amount = len(values)
     width = values[0].shape[1]
     mine = values[0].shape[0] // (owners * cores)
-    blocks = [pltpu.VMEM((owners, mine, width), v.dtype) for v in values]
-    more = [] if summed is None else [summed]
-    out = pl.pallas_call(
-        functools.partial(scatter_kernel, amount, bool(more), owners, cores),
-        out_shape=[jax.ShapeDtypeStruct((mine, width), jnp.float32)] * amount
-        + [jax.ShapeDtypeStruct(held_shape(m, owners), m.dtype) for m in more],
-        in_specs=[ANY] * amount + [FAR] * len(more),
-        out_specs=[INSIDE] * amount + [FAR] * len(more),
-        scratch_shapes=blocks * 5
-        + [pltpu.VMEM((mine, width), jnp.float32)]
-        + [pltpu.SemaphoreType.DMA((amount, owners)) for _ in range(6)]
-        + [sem for m in more for sem in swap_sems(owners)],
+    return pl.pallas_call(
+        functools.partial(scatter_kernel, amount, owners, cores),
+        out_shape=[jax.ShapeDtypeStruct((mine, width), jnp.float32)] * amount,
+        in_specs=[ANY] * amount,
+        out_specs=[INSIDE] * amount,
+        scratch_shapes=scatter_scratch(amount, owners, (mine, width), values[0].dtype),
         compiler_params=params(collective_id),
         cost_estimate=cost(20 * amount),
         name="team_sum",
-    )(*[v.reshape(owners, cores, mine, width) for v in values], *more)
-    return out[:amount], out[amount:]
+    )(*[v.reshape(owners, cores, mine, width) for v in values])
 
 
 def swap_first(summed, held, local, sent, came, owners):
@@ -893,6 +877,8 @@
 
 
 def attend_back_kernel(
+    owners,
+    cores,
     dy_ref,
     u_ref,
     qkv_ref,
@@ -904,12 +890,19 @@
     turns,
     placing,
     placed,
+    summed,
+    grad_ref,
+    sum_ref,
+    rows,
+    lin,
     du_ref,
-    grad_ref,
-    lin,
+    *refs,
 ):
+    greet(around("ctx", owners) + around("tensor", cores))
+    swap, refs = refs[:3], refs[3:]
+    swap_first(summed, rows, *swap, owners)
     count = q_ref.shape[1]
-    width = du_ref.shape[1]
+    width = dy_ref.shape[1]
     scale = HD ** (-0.5)
     low = jnp.bfloat16
     for first in range(0, count, HD):
@@ -930,27 +923,40 @@
     edge = lin.shape[1]
     for start in range(0, width, tile):
         span = slice(start, start + tile)
-        du_ref[:, span] = contract_cols(lin[...], qkv_ref[span, :]).astype(low)
+        du_part = contract_cols(lin[...], qkv_ref[span, :]).astype(low)
+        du_ref[:, :, :, span] = du_part.reshape(*du_ref.shape[:3], tile)
+    for start in range(0, width, tile):
+        span = slice(start, start + tile)
         grad_ref[span, :edge] = dot(u_ref[:, span].T, lin[...]).astype(low)
         grad_ref[span, edge:] = dot(dy_ref[:, span].T, o_ref[...]).astype(low)
-
-
-def attend_back(dy, u, qkv, out_w, q, k, v, o, turns, placing, placed):
+    scatter(1, owners, cores, [du_ref], [sum_ref], refs)
+    swap_rest(summed, rows, *swap, owners)
+
+
+def attend_back(collective_id, dy, u, qkv, out_w, q, k, v, o, turns, placing, placed, summed):
+    owners, cores = lax.axis_size("ctx"), lax.axis_size("tensor")
     total, width = u.shape
     count = q.shape[1]
+    mine = total // (owners * cores)
     return pl.pallas_call(
-        attend_back_kernel,
+        functools.partial(attend_back_kernel, owners, cores),
         out_shape=[
-            jax.ShapeDtypeStruct((total, width), jnp.bfloat16),
             jax.ShapeDtypeStruct((width, 4 * count), jnp.bfloat16),
+            jax.ShapeDtypeStruct((mine, width), jnp.float32),
+            jax.ShapeDtypeStruct(held_shape(summed, owners), summed.dtype),
         ],
-        in_specs=[INSIDE] * 11,
-        out_specs=[INSIDE] * 2,
-        scratch_shapes=[pltpu.VMEM((total, 3 * count), jnp.bfloat16)],
-        compiler_params=pltpu.CompilerParams(vmem_limit_bytes=60 << 20),
-        cost_estimate=cost(20),
+        in_specs=[INSIDE] * 11 + [ANY],
+        out_specs=[INSIDE] * 2 + [ANY],
+        scratch_shapes=[
+            pltpu.VMEM((total, 3 * count), jnp.bfloat16),
+            pltpu.VMEM((owners, cores, mine, width), jnp.bfloat16),
+        ]
+        + swap_sems(owners)
+        + scatter_scratch(1, owners, (mine, width), jnp.bfloat16),
+        compiler_params=params(collective_id),
+        cost_estimate=cost(50),
         name="attend_back",
-    )(dy, u, qkv, out_w, q, k, v, o, turns, placing, placed)
+    )(dy, u, qkv, out_w, q, k, v, o, turns, placing, placed, summed)
 
 
 EXACT = functools.partial(
@@ -1100,7 +1106,7 @@
         mixed = tables[j][:, total + 1 : total + 2] * y
         for i in range(total):
             mixed = mixed + tables[i][:, 1 + j : 2 + j] * current[i]
-        final_ref[j] = mixed.astype(jnp.bfloat16)
+        final_ref[0, :, j, :] = mixed.astype(jnp.bfloat16)
     grads = connection_back(
         current,
         grad_top,
@@ -1148,7 +1154,7 @@
         sums,
     )
     for j in range(total):
-        grad_ref[j] = grads[j].astype(jnp.bfloat16)
+        grad_ref[0, :, j, :] = grads[j].astype(jnp.bfloat16)
 
 
 def by_token(tile, shape, kind=jnp.float32):
@@ -1171,7 +1177,7 @@
         else:
             specs.append(by_token(tile, value.shape)[0] if tiled else fixed(value.shape)[0])
         values.append(value)
-    tokens = outs[0][1].shape[-2]
+    tokens = ins[0][0].shape[-2]
     return pl.pallas_call(
         kernel,
         grid_spec=pltpu.PrefetchScalarGridSpec(
@@ -1319,6 +1325,13 @@
     early_sum, late_sum = [shard_sum(grads) for grads in ffn_grads]
     ffn_out, grad_ffn_input = team_sum(3, ffn_part, ffn_input_part)
     sums = [fixed((8, width)), fixed((stream_total, 8))]
+    runs = (
+        pl.BlockSpec(
+            (1, tile, stream_total, width),
+            lambda step, *_: (step * tile // part, step % (part // tile), 0, 0),
+        ),
+        jax.ShapeDtypeStruct((owners, part, stream_total, width), low),
+    )
     final, grad_middle, grad_attn_low, weight_two, static_two = token_call(
         back_second_kernel,
         "back_second",
@@ -1336,7 +1349,7 @@
             (turned_weight[1], False),
         ],
         [
-            by_token(tile, (stream_total, mine, width), low),
+            runs,
             by_token(tile, (stream_total, mine, width)),
             by_token(tile, (mine, width), low),
             *sums,
@@ -1344,11 +1357,23 @@
     )
     [grad_attn_out] = team_gather(4, grad_attn_low)
 
-    attn_input_part, attn_grads = attend_back(
-        grad_attn_out, attn_input, qkv, out_w, queries, keys, values, attended, turns, placing, placed
+    attn_grads, grad_attn_input, early_rows = attend_back(
+        5,
+        grad_attn_out,
+        attn_input,
+        qkv,
+        out_w,
+        queries,
+        keys,
+        values,
+        attended,
+        turns,
+        placing,
+        placed,
+        early_sum,
     )
     attn_sum = shard_sum(attn_grads)
-    [grad_attn_input], [early_rows] = team_sum_and_rows(5, early_sum, attn_input_part)
+
     grad_current, weight_one, static_one = token_call(
         back_first_kernel,
         "back_first",
@@ -1364,7 +1389,7 @@
             (active_one, True),
             (turned_weight[0], False),
         ],
-        [by_token(tile, (stream_total, mine, width), low), *sums],
+        [runs, *sums],
     )
     statics = jnp.stack([static_one, static_two]).reshape(1, -1)
     mixed = jnp.concatenate(
@@ -1375,12 +1400,8 @@
         0,
     )
 
-    def runs(value):
-        return value.transpose(1, 0, 2).reshape(owners, part, stream_total, width)
-
-    own_final, own_grad = runs(final), runs(grad_current)
     mixed, (far_final, far_grad), late_rows = close_team(
-        7, late_sum, mixed, own_final, own_grad
+        7, late_sum, mixed, final, grad_current
     )
     mixed, attn_sum = lax.optimization_barrier((mixed, attn_sum))
     (
@@ -1394,7 +1415,7 @@
         grad_value,
         grad_output,
     ) = place_all(
-        (own_final, far_final, own_grad, far_grad), early_rows, late_rows, team_rows(8, attn_sum)
+        (final, far_final, grad_current, far_grad), early_rows, late_rows, team_rows(8, attn_sum)
     )
     columns_in = mix_weight.shape[2]
     grad_mix_weight = mixed[:columns_in].transpose(1, 2, 0)

time: 477 us -> 469 us (0.983)
  Pallas kernels: 416 us -> 408 us
  local copies, waits for them, and re-layouts: 17.5 us -> 12.7 us
  waiting for transfers between devices: 2.04 us -> 6.82 us
    pallas_call x4 -> x3, Pallas kernels: 158 us -> 149 us  [the longest x2 88.3 us: team_sum(): pl.pallas_call(functools.partial(scatter_kernel, amount, owners, cores),...]
    transpose x2 -> x0, local copies, waits for them, and re-layouts: 4.8 us -> none  [runs(): return value.transpose(1, 0, 2).reshape(owners, part, stream_total, width)]
  transfers between devices with their start and end apart: 5 -> 5, of which waited for: 1 -> 2; matrix products, arithmetic and copies ran while one was open for 3% -> 2% of each run, Pallas kernels for 65% -> 64%
where the time goes in v5:
time: 469 us; the launch traced here: 463 us
  Pallas kernels  408 us (87%)
  between operations  14.6 us (3%)
  local copies, waits for them, and re-layouts  12.7 us (3%)
  other arithmetic  11.2 us (2%)
  starting transfers between devices  7.63 us (2%)
  waiting for transfers between devices  6.82 us (1%)
    pallas_call x2, Pallas kernels, team_sum(): pl.pallas_call(functools.partial(scatter_kernel, amount, owners, cores),...  88.3 us
    pallas_call x1, Pallas kernels, attend_back(): pl.pallas_call(functools.partial(attend_back_kernel, owners, cores), out_...  60.5 us
    pallas_call x2, Pallas kernels, team_gather(): pl.pallas_call(functools.partial(gather_kernel, amount, owners, cores), o...  58 us
    pallas_call x1, Pallas kernels, close_team(): pl.pallas_call(functools.partial(close_kernel, amount, shards_in, owners,...  46.3 us
    pallas_call x1, Pallas kernels, open_team(): pl.pallas_call(functools.partial(open_kernel, shards_in, owners, cores),...  40.6 us
    pallas_call x1, Pallas kernels, ffn(): pl.pallas_call(ffn_kernel, grid=(blocks,), in_specs=[whole, whole, pl.Blo...  33.9 us
    pallas_call x3, Pallas kernels, token_call(): pl.pallas_call(kernel, grid_spec=pltpu.PrefetchScalarGridSpec(num_scalar_...  29.1 us
    pallas_call x1, Pallas kernels, team_rows(): pl.pallas_call(functools.partial(swap_kernel_alone, owners), out_shape=ja...  27.3 us
  transfers between devices with their start and end apart: 5, of which 2 were waited for; matrix products, arithmetic and copies ran while one was open for 2% of the time, Pallas kernels for 64%

profile of v5, /device:TPU:8, one launch (start us, length us, event | category | flops | bytes accessed | tf_op | source)
XLA Modules:
  0.0 462.7 jit_solution(2682988841170996004)
XLA Ops:
  7.2 1.5 copy-done
  9.2 1.1 convert_reduce_fusion
  11.0 1.2 fusion.2
  12.2 0.7 fusion
  13.1 1.8 broadcast_add_fusion.1
  15.8 1.0 fusion.50
  17.6 40.6 %open_team.1 = (bf16[4,2,64,2048]{3,2,1,0:T(8,128)(2,1)}, bf16[2048,768]{1,0:T(8,128)(2,1)}, bf16[256,2048]{1,0:T(8,128)(2,1)}, bf16[512,3072]{1,0:T(8,128)(2,1)}, s32[4,8,128]{2,1,0:T(8,128)}) custom-call(bf16[64,2048]{1,0:T(8,128)(2,1)} %get-tuple-element.119.refs_0_, bf16[512,1024]{1,0:T(8,128)(2,1)} %refs_1_.1, bf16[512,1024]{1,0:T(8,128)(2,1)} %refs_2_.1, ...), custom_call_target="tpu_custom_call" | custom-call | bytes 120000000 | tf_op jit(solution)/shard_map/open_team/pallas_call | solution.py:308
  58.3 0.7 slice.66
  59.6 5.1 %pack_runs.1 = bf16[4,4,16,2048]{3,2,1,0:T(8,128)(2,1)} custom-call(s32[4]{0:T(128)} %fusion.48.sent, bf16[128,4,2048]{2,1,0:T(4,128)(2,1)} %value.1), custom_call_target="tpu_custom_call" | custom-call | bytes 6000000 | tf_op jit(solution)/shard_map/pack_runs/pallas_call | solution.py:810
  64.8 7.3 %all-to-all-start = ((bf16[4,4,16,2048]{3,2,1,0:T(8,128)(2,1)}), bf16[4,4,16,2048]{3,2,1,0:T(8,128)(2,1)S(1)}, u32[]{:S(2)}, u32[]{:S(2)}) async-start(bf16[4,4,16,2048]{3,2,1,0:T(8,128)(2,1)} %pack_runs.1), calls=%async_computation | async-start | bytes 2097152 | tf_op jit(solution)/shard_map/all_to_all | solution.py:1276
  72.6 0.9 copy.53.placing
  74.0 1.0 multiply_cosine_fusion
  75.2 0.8 maximum_bitcast_fusion.turns
  76.1 10.8 %attend.1 = (f32[512,2048]{1,0:T(8,128)}, bf16[512,256]{1,0:T(8,128)(2,1)}, bf16[512,256]{1,0:T(8,128)(2,1)}, bf16[512,256]{1,0:T(8,128)(2,1)}, bf16[512,256]{1,0:T(8,128)(2,1)}) custom-call(bf16[512,2048]{1,0:T(8,128)(2,1)} %bitcast.94, bf16[2048,768]{1,0:T(8,128)(2,1)} %get-tuple-element.64.qkv_ref, bf16[256,2048]{1,0:T(8,128)(2,1)} %get-tuple-element.65.out_ref, ...), custom_call_target="tpu_custom_call" | custom-call | bytes 36000000 | tf_op jit(solution)/shard_map/attend/pallas_call | solution.py:868
  86.8 46.1 %team_sum.2.branch_out = f32[64,2048]{1,0:T(8,128)} custom-call(f32[4,2,64,2048]{3,2,1,0:T(8,128)} %bitcast.97), custom_call_target="tpu_custom_call" | custom-call | bytes 60000000 | tf_op jit(solution)/shard_map/team_sum/pallas_call | solution.py:429
  135.4 1.0 copy-done.3
  136.4 8.9 %mix_second.1 = (f32[4,64,2048]{2,1,0:T(8,128)}, bf16[64,2048]{1,0:T(8,128)(2,1)}, bf16[64,2048]{1,0:T(8,128)(2,1)}, f32[64,2048]{1,0:T(8,128)}, f32[64,8]{1,0:T...) custom-call(s32[4]{0:T(128)} %and_select_fusion.13.source, ...), custom_call_target="tpu_custom_call" | custom-call | bytes 15000000 | tf_op jit(solution)/shard_map/mix_second/pallas_call | solution.py:1181
  145.3 36.1 %team_gather.2 = (bf16[4,2,64,2048]{3,2,1,0:T(8,128)(2,1)}, bf16[4,2,64,2048]{3,2,1,0:T(8,128)(2,1)}) custom-call(bf16[64,2048]{1,0:T(8,128)(2,1)} %get-tuple-element.70.refs_0_, bf16[64,2048]{1,0:T(8,128)(2,1)} %get-tuple-element.71.refs_1_), custom_call_target="tpu_custom_call" | custom-call | bytes 120000000 | tf_op jit(solution)/shard_map/team_gather/pallas_call | solution.py:186
  181.4 1.5 all-gather.2.cloned.1.call-done.gate_ref.up_ref
  182.9 33.9 %ffn.1 = (bf16[512,2048]{1,0:T(8,128)(2,1)}, bf16[512,2048]{1,0:T(8,128)(2,1)}, bf16[2048,1536]{1,0:T(8,128)(2,1)}, bf16[2048,1536]{1,0:T(8,128)(2,1)}) custom-call(bf16[512,2048]{1,0:T(8,128)(2,1)} %bitcast.98, bf16[512,2048]{1,0:T(8,128)(2,1)} %bitcast.99, bf16[2048,3072]{1,0:T(8,128)(2,1)} %all-gather.2.cloned.1.call-done.gate_ref.up_ref, ...), custom_call_target="tpu_custom_call" | custom-call | bytes 90000000 | tf_op jit(solution)/shard_map/ffn/pallas_call | solution.py:769
  217.6 42.2 %team_sum.3 = (f32[64,2048]{1,0:T(8,128)}, f32[64,2048]{1,0:T(8,128)}) custom-call(bf16[4,2,64,2048]{3,2,1,0:T(8,128)(2,1)} %bitcast.100, bf16[4,2,64,2048]{3,2,1,0:T(8,128)(2,1)} %bitcast.101), custom_call_target="tpu_custom_call" | custom-call | bytes 120000000 | tf_op jit(solution)/shard_map/team_sum/pallas_call | solution.py:429
  259.8 10.5 %back_second.1 = (bf16[4,16,4,2048]{3,2,1,0:T(4,128)(2,1)}, f32[4,64,2048]{2,1,0:T(8,128)}, bf16[64,2048]{1,0:T(8,128)(2,1)}, f32[8,2048]{1,0:T(8,128)}, f32[4,8]{1,0:T(4,128)}) custom-call(f32[4,64,2048]{2,1,0:T(8,128)} %get-tuple-element.68.middle, bf16[4,64,2048]{2,1,0:T(8,128)(2,1)} %get-tuple-element.69.top, f32[64,2048]{1,0:T(8,128)} %get-tuple-element.77.branch_out, ...), custom_call_target="tpu_custom_call" | custom-call | bytes 15000000 | tf_op jit(solution)/shard_map/back_second/pallas_call | solution.py:1181
  270.3 21.9 %team_gather.3 = bf16[4,2,64,2048]{3,2,1,0:T(8,128)(2,1)} custom-call(bf16[64,2048]{1,0:T(8,128)(2,1)} %get-tuple-element.85.refs_0_), custom_call_target="tpu_custom_call" | custom-call | bytes 60000000 | tf_op jit(solution)/shard_map/team_gather/pallas_call | solution.py:186
  292.2 60.5 %attend_back.1 = (bf16[2048,1024]{1,0:T(8,128)(2,1)}, f32[64,2048]{1,0:T(8,128)}, bf16[4,128,1536]{2,1,0:T(8,128)(2,1)}) custom-call(bf16[512,2048]{1,0:T(8,128)(2,1)} %bitcast.93, bf16[512,2048]{1,0:T(8,128)(2,1)} %bitcast.95, bf16[2048,768]{1,0:T(8,128)(2,1)} %get-tuple-element.64.qkv_ref, bf16[256,2048]{1,0:T(8,128)(2,1)} %get-tuple-element.65.out_ref, ...), custom_call_target="tpu_custom_call" | custom-call | bytes 150000000 | tf_op jit(solution)/shard_map/attend_back/pallas_call | solution.py:941
  354.2 9.8 %back_first.1 = (bf16[4,16,4,2048]{3,2,1,0:T(4,128)(2,1)}, f32[8,2048]{1,0:T(8,128)}, f32[4,8]{1,0:T(4,128)}) custom-call(bf16[4,64,2048]{2,1,0:T(8,128)(2,1)} %bitcast.92, f32[4,64,2048]{2,1,0:T(8,128)} %get-tuple-element.84.top, f32[64,2048]{1,0:T(8,128)} %team_sum.2.branch_out, f32[64,2048]{1,0:T(8,128)} %get-tuple-element.91.grad_in, ...), custom_call_target="tpu_custom_call" | custom-call | bytes 15000000 | tf_op jit(solution)/shard_map/back_first/pallas_call | solution.py:1181
  363.9 0.9 pad_maximum_fusion
  365.8 0.7 select_maximum_fusion.refs_2_
  366.5 46.3 %close_team.1 = (bf16[4,16,4,2048]{3,2,1,0:T(4,128)(2,1)}, bf16[4,16,4,2048]{3,2,1,0:T(4,128)(2,1)}, f32[12,2,2048]{2,1,0:T(2,128)}, bf16[4,128,1536]{2,1,0:T(8,128)(2,1)}) custom-call(bf16[4,16,4,2048]{3,2,1,0:T(4,128)(2,1)} %get-tuple-element.83.refs_0_.own_a, bf16[4,16,4,2048]{3,2,1,0:T(4,128)(2,1)} %get-tuple-element.92.refs_1_.own_b, ...), custom_call_target="tpu_custom_call" | custom-call | bytes 180000000 | tf_op jit(solution)/shard_map/close_team/pallas_call | solution.py:657
  412.8 4.6 reduce-scatter.8.cloned.1.call-done.summed
  417.4 1.5 slice_bitcast_fusion.4
  419.6 27.3 %team_rows.1.attn = bf16[4,128,1024]{2,1,0:T(8,128)(2,1)} custom-call(bf16[512,1024]{1,0:T(8,128)(2,1)} %reduce-scatter.8.cloned.1.call-done.summed), custom_call_target="tpu_custom_call" | custom-call | bytes 60000000 | tf_op jit(solution)/shard_map/team_rows/pallas_call | solution.py:552
  447.6 8.0 %place_all.1 = (bf16[4,2,16,4,2048]{4,3,2,1,0:T(4,128)(2,1)}, bf16[4,2,16,4,2048]{4,3,2,1,0:T(4,128)(2,1)}, f32[128,4096]{1,0:T(8,128)}, f32[128,4096]{1,0:T(8,1...) custom-call(s32[1]{0:T(128)} %bitcast.where, ...), custom_call_target="tpu_custom_call" | custom-call | bytes 21000000 | tf_op jit(solution)/shard_map/place_all/pallas_call | solution.py:495
  (72 shorter events, 11.9 us)
Async XLA Ops:
  7.2 1.6 copy-start
  7.2 175.7 %all-gather.2.cloned.1.call-start = ((), (), s32[]{:S(2)}) async-start(), calls=%async_computation.4 | async-start | bytes 15728640 | tf_op jit(solution)/shard_map/all_gather | solution.py:1272
  11.0 4.0 copy-start.2
  11.0 2.0 copy-start.4
  11.0 2.0 copy-start.6
  15.3 1.6 copy-start.9
  59.6 12.7 %copy-start.10 = (s32[1,4]{1,0:T(1,128)S(1)}, s32[1,4]{1,0:T(1,128)}, u32[]{:S(2)}) copy-start(s32[1,4]{1,0:T(1,128)} %param.15) | copy-start | bytes 52
  59.6 14.4 %copy-start.8 = (f32[64]{0:T(128)S(1)}, f32[64]{0:T(128)}, u32[]{:S(2)}) copy-start(f32[64]{0:T(128)} %constant.173) | copy-start | bytes 772
  64.8 70.7 %all-to-all-start = ((bf16[4,4,16,2048]{3,2,1,0:T(8,128)(2,1)}), bf16[4,4,16,2048]{3,2,1,0:T(8,128)(2,1)S(1)}, u32[]{:S(2)}, u32[]{:S(2)}) async-start(bf16[4,4,16,2048]{3,2,1,0:T(8,128)(2,1)} %pack_runs.1), calls=%async_computation | async-start | bytes 2097152 | tf_op jit(solution)/shard_map/all_to_all | solution.py:1276
  72.1 220.1 %reduce-scatter.4.cloned.1.call-start = ((), (), s32[]{:S(2)}) async-start(), calls=%async_computation.5 | async-start | bytes 7864320 | tf_op jit(solution)/shard_map/reduce_scatter | solution.py:1323
  135.4 1.0 copy-start.3
  216.8 149.7 %reduce-scatter.6.cloned.1.call-start = ((), (), s32[]{:S(2)}) async-start(), calls=%async_computation.6 | async-start | bytes 7864320 | tf_op jit(solution)/shard_map/reduce_scatter | solution.py:1323
  217.5 199.8 %reduce-scatter.8.cloned.1.call-start = ((), (), s32[]{:S(2)}) async-start(), calls=%async_computation.7 | async-start | bytes 5242880 | tf_op jit(solution)/shard_map/reduce_scatter | solution.py:1323
  354.2 9.8 %copy-start.5 = (f32[8,2048]{1,0:T(8,128)S(1)}, f32[8,2048]{1,0:T(8,128)}, u32[]{:S(2)}) copy-start(f32[8,2048]{1,0:T(8,128)} %get-tuple-element.94) | copy-start | bytes 196612
  354.2 10.8 %copy-start.7 = (f32[4,8]{1,0:T(4,128)S(1)}, f32[4,8]{1,0:T(4,128)}, u32[]{:S(2)}) copy-start(f32[4,8]{1,0:T(4,128)} %get-tuple-element.96) | copy-start | bytes 388
  447.6 8.0 %copy-start.1 = (bf16[128,4,2048]{2,1,0:T(4,128)(2,1)S(1)}, bf16[128,4,2048]{2,1,0:T(4,128)(2,1)}, u32[]{:S(2)}) copy-start(bf16[128,4,2048]{2,1,0:T(4,128)(2,1)} %param.14) | copy-start | bytes 6291460
Sparse Core Ops, SparseCore 0:
  58.4 124.4 all-gather.1
  216.9 70.5 reduce-scatter.3
  290.6 70.1 reduce-scatter.5
  363.6 53.7 reduce-scatter.7

commit v6 on v5

--- a/solution.py
+++ b/solution.py
@@ -465,17 +465,45 @@
                 out[start : start + block, :] = piece.T
 
 
-def place_kernel(block, where, own_a, far_a, own_b, far_b, early, late, attn, *outs):
+def place_attn_kernel(attn, *outs):
+    put_rows(attn[0], outs, outs[0].shape[1], 0, 1)
+
+
+def place_kernel(block, where, own_a, far_a, own_b, far_b, early, late, *outs):
     core = where[0]
     for own, far, out in ((own_a, far_a, outs[0]), (own_b, far_b, outs[1])):
         out[0, core] = own[0]
         out[0, out.shape[1] - 1 - core] = far[0]
-    put_rows(early[0], outs[2:5], block, 0, 2)
-    put_rows(late[0], outs[2:5], block, 1, 2)
-    put_rows(attn[0], outs[5:], outs[5].shape[1], 0, 1)
-
-
-def place_all(streams, early, late, attn):
+    put_rows(early[0], outs[2:], block, 0, 2)
+    put_rows(late[0], outs[2:], block, 1, 2)
+
+
+def placed_rows(owners, count, units, amount):
+    specs = [pl.BlockSpec((count, units), lambda c, *_: (0, c))] * (amount - 1)
+    specs.append(pl.BlockSpec((units, count), lambda c, *_: (c, 0)))
+    shapes = [jax.ShapeDtypeStruct((count, owners * units), jnp.float32)] * (amount - 1)
+    shapes.append(jax.ShapeDtypeStruct((owners * units, count), jnp.float32))
+    return specs, shapes
+
+
+def place_attn(attn):
+    owners, count, wide = attn.shape
+    specs, shapes = placed_rows(owners, count, wide // 4, 4)
+    return pl.pallas_call(
+        place_attn_kernel,
+        grid=(owners,),
+        in_specs=[pl.BlockSpec((1, count, wide), lambda c: (c, 0, 0))],
+        out_specs=specs,
+        out_shape=shapes,
+        compiler_params=pltpu.CompilerParams(
+            dimension_semantics=("arbitrary",), vmem_limit_bytes=60 << 20
+        ),
+        cost_estimate=cost(2),
+        name="place_attn",
+    )(attn)
+
+
+def place_all(streams, early, late):
     owners, cores = lax.axis_size("ctx"), lax.axis_size("tensor")
     run = streams[0].shape
     block = late.shape[2] // (3 * BLOCKS // 2)
@@ -485,19 +513,14 @@
 
     both = (run[0], cores, *run[1:])
     specs, shapes = [lead(both)] * 2, [jax.ShapeDtypeStruct(both, streams[0].dtype)] * 2
-    for amount, units in ((3, 2 * late.shape[2] // 3), (4, attn.shape[2] // 4)):
-        count = late.shape[1]
-        specs += [pl.BlockSpec((count, units), lambda c, _: (0, c))] * (amount - 1)
-        specs.append(pl.BlockSpec((units, count), lambda c, _: (c, 0)))
-        wide = jax.ShapeDtypeStruct((count, owners * units), jnp.float32)
-        shapes += [wide] * (amount - 1)
-        shapes.append(jax.ShapeDtypeStruct((owners * units, count), jnp.float32))
+    more, wide = placed_rows(owners, late.shape[1], 2 * late.shape[2] // 3, 3)
+    specs, shapes = specs + more, shapes + wide
     return pl.pallas_call(
         functools.partial(place_kernel, block),
         grid_spec=pltpu.PrefetchScalarGridSpec(
             num_scalar_prefetch=1,
             grid=(owners,),
-            in_specs=[lead(v.shape) for v in (*streams, early, late, attn)],
+            in_specs=[lead(v.shape) for v in (*streams, early, late)],
             out_specs=specs,
         ),
         out_shape=shapes,
@@ -506,7 +529,7 @@
         ),
         cost_estimate=cost(7),
         name="place_all",
-    )(lax.axis_index("tensor")[None].astype(jnp.int32), *streams, early, late, attn)
+    )(lax.axis_index("tensor")[None].astype(jnp.int32), *streams, early, late)
 
 
 def swap_rest(summed, held, local, sent, came, owners):
@@ -1403,20 +1426,11 @@
     mixed, (far_final, far_grad), late_rows = close_team(
         7, late_sum, mixed, final, grad_current
     )
-    mixed, attn_sum = lax.optimization_barrier((mixed, attn_sum))
-    (
-        streams_out,
-        grad_streams,
-        grad_gate,
-        grad_up,
-        grad_down,
-        grad_query,
-        grad_key,
-        grad_value,
-        grad_output,
-    ) = place_all(
-        (final, far_final, grad_current, far_grad), early_rows, late_rows, team_rows(8, attn_sum)
-    )
+    streams_out, grad_streams, grad_gate, grad_up, grad_down = place_all(
+        (final, far_final, grad_current, far_grad), early_rows, late_rows
+    )
+    mixed, attn_sum, grad_gate = lax.optimization_barrier((mixed, attn_sum, grad_gate))
+    grad_query, grad_key, grad_value, grad_output = place_attn(team_rows(8, attn_sum))
     columns_in = mix_weight.shape[2]
     grad_mix_weight = mixed[:columns_in].transpose(1, 2, 0)
     grad_mix_static = mixed[8, 0, : statics.size].reshape(2, stream_total, 8)[:, :, :columns_in]

time: 469 us -> 466 us (level)
  transfers between devices with their start and end apart: 5 -> 5, of which waited for: 2 -> 1; matrix products, arithmetic and copies ran while one was open for 2% -> 3% of each run, Pallas kernels for 64% -> 67%
where the time goes in v6:
time: 466 us; the launch traced here: 459 us
  Pallas kernels  411 us (88%)
  between operations  14.6 us (3%)
  other arithmetic  11.2 us (2%)
  local copies, waits for them, and re-layouts  11.1 us (2%)
  starting transfers between devices  7.63 us (2%)
    pallas_call x2, Pallas kernels, team_sum(): pl.pallas_call(functools.partial(scatter_kernel, amount, owners, cores),...  88.3 us
    pallas_call x1, Pallas kernels, attend_back(): pl.pallas_call(functools.partial(attend_back_kernel, owners, cores), out_...  60.5 us
    pallas_call x2, Pallas kernels, team_gather(): pl.pallas_call(functools.partial(gather_kernel, amount, owners, cores), o...  58 us
    pallas_call x1, Pallas kernels, close_team(): pl.pallas_call(functools.partial(close_kernel, amount, shards_in, owners,...  46.3 us
    pallas_call x1, Pallas kernels, open_team(): pl.pallas_call(functools.partial(open_kernel, shards_in, owners, cores),...  40.6 us
    pallas_call x1, Pallas kernels, ffn(): pl.pallas_call(ffn_kernel, grid=(blocks,), in_specs=[whole, whole, pl.Blo...  33.9 us
    pallas_call x3, Pallas kernels, token_call(): pl.pallas_call(kernel, grid_spec=pltpu.PrefetchScalarGridSpec(num_scalar_...  29.1 us
    pallas_call x1, Pallas kernels, team_rows(): pl.pallas_call(functools.partial(swap_kernel_alone, owners), out_shape=ja...  26.7 us
  transfers between devices with their start and end apart: 5, of which 1 were waited for; matrix products, arithmetic and copies ran while one was open for 3% of the time, Pallas kernels for 67%

profile of v6, /device:TPU:8, one launch (start us, length us, event | category | flops | bytes accessed | tf_op | source)
XLA Modules:
  0.0 459.2 jit_solution(17350322536745756972)
XLA Ops:
  7.2 1.5 copy-done
  9.2 1.1 convert_reduce_fusion
  11.0 1.2 fusion.2
  12.2 0.7 fusion
  13.1 1.8 broadcast_add_fusion.1
  15.8 1.0 fusion.50
  17.6 40.6 %open_team.1 = (bf16[4,2,64,2048]{3,2,1,0:T(8,128)(2,1)}, bf16[2048,768]{1,0:T(8,128)(2,1)}, bf16[256,2048]{1,0:T(8,128)(2,1)}, bf16[512,3072]{1,0:T(8,128)(2,1)}, s32[4,8,128]{2,1,0:T(8,128)}) custom-call(bf16[64,2048]{1,0:T(8,128)(2,1)} %get-tuple-element.121.refs_0_, bf16[512,1024]{1,0:T(8,128)(2,1)} %refs_1_.1, bf16[512,1024]{1,0:T(8,128)(2,1)} %refs_2_.1, ...), custom_call_target="tpu_custom_call" | custom-call | bytes 120000000 | tf_op jit(solution)/shard_map/open_team/pallas_call | solution.py:308
  58.3 0.7 slice.66
  59.6 5.1 %pack_runs.1 = bf16[4,4,16,2048]{3,2,1,0:T(8,128)(2,1)} custom-call(s32[4]{0:T(128)} %fusion.48.sent, bf16[128,4,2048]{2,1,0:T(4,128)(2,1)} %value.1), custom_call_target="tpu_custom_call" | custom-call | bytes 6000000 | tf_op jit(solution)/shard_map/pack_runs/pallas_call | solution.py:833
  64.8 7.3 %all-to-all-start = ((bf16[4,4,16,2048]{3,2,1,0:T(8,128)(2,1)}), bf16[4,4,16,2048]{3,2,1,0:T(8,128)(2,1)S(1)}, u32[]{:S(2)}, u32[]{:S(2)}) async-start(bf16[4,4,16,2048]{3,2,1,0:T(8,128)(2,1)} %pack_runs.1), calls=%async_computation | async-start | bytes 2097152 | tf_op jit(solution)/shard_map/all_to_all | solution.py:1299
  72.6 0.9 copy.53.placing
  74.0 1.0 multiply_cosine_fusion
  75.2 0.8 maximum_bitcast_fusion.turns
  76.1 10.8 %attend.1 = (f32[512,2048]{1,0:T(8,128)}, bf16[512,256]{1,0:T(8,128)(2,1)}, bf16[512,256]{1,0:T(8,128)(2,1)}, bf16[512,256]{1,0:T(8,128)(2,1)}, bf16[512,256]{1,0:T(8,128)(2,1)}) custom-call(bf16[512,2048]{1,0:T(8,128)(2,1)} %bitcast.94, bf16[2048,768]{1,0:T(8,128)(2,1)} %get-tuple-element.65.qkv_ref, bf16[256,2048]{1,0:T(8,128)(2,1)} %get-tuple-element.66.out_ref, ...), custom_call_target="tpu_custom_call" | custom-call | bytes 36000000 | tf_op jit(solution)/shard_map/attend/pallas_call | solution.py:891
  86.8 46.1 %team_sum.2.branch_out = f32[64,2048]{1,0:T(8,128)} custom-call(f32[4,2,64,2048]{3,2,1,0:T(8,128)} %bitcast.97), custom_call_target="tpu_custom_call" | custom-call | bytes 60000000 | tf_op jit(solution)/shard_map/team_sum/pallas_call | solution.py:429
  135.4 1.0 copy-done.3
  136.4 8.9 %mix_second.1 = (f32[4,64,2048]{2,1,0:T(8,128)}, bf16[64,2048]{1,0:T(8,128)(2,1)}, bf16[64,2048]{1,0:T(8,128)(2,1)}, f32[64,2048]{1,0:T(8,128)}, f32[64,8]{1,0:T...) custom-call(s32[4]{0:T(128)} %and_select_fusion.13.source, ...), custom_call_target="tpu_custom_call" | custom-call | bytes 15000000 | tf_op jit(solution)/shard_map/mix_second/pallas_call | solution.py:1204
  145.3 36.1 %team_gather.2 = (bf16[4,2,64,2048]{3,2,1,0:T(8,128)(2,1)}, bf16[4,2,64,2048]{3,2,1,0:T(8,128)(2,1)}) custom-call(bf16[64,2048]{1,0:T(8,128)(2,1)} %get-tuple-element.71.refs_0_, bf16[64,2048]{1,0:T(8,128)(2,1)} %get-tuple-element.72.refs_1_), custom_call_target="tpu_custom_call" | custom-call | bytes 120000000 | tf_op jit(solution)/shard_map/team_gather/pallas_call | solution.py:186
  181.4 1.5 all-gather.2.cloned.1.call-done.gate_ref.up_ref
  182.9 33.9 %ffn.1 = (bf16[512,2048]{1,0:T(8,128)(2,1)}, bf16[512,2048]{1,0:T(8,128)(2,1)}, bf16[2048,1536]{1,0:T(8,128)(2,1)}, bf16[2048,1536]{1,0:T(8,128)(2,1)}) custom-call(bf16[512,2048]{1,0:T(8,128)(2,1)} %bitcast.98, bf16[512,2048]{1,0:T(8,128)(2,1)} %bitcast.99, bf16[2048,3072]{1,0:T(8,128)(2,1)} %all-gather.2.cloned.1.call-done.gate_ref.up_ref, ...), custom_call_target="tpu_custom_call" | custom-call | bytes 90000000 | tf_op jit(solution)/shard_map/ffn/pallas_call | solution.py:792
  217.6 42.2 %team_sum.3 = (f32[64,2048]{1,0:T(8,128)}, f32[64,2048]{1,0:T(8,128)}) custom-call(bf16[4,2,64,2048]{3,2,1,0:T(8,128)(2,1)} %bitcast.100, bf16[4,2,64,2048]{3,2,1,0:T(8,128)(2,1)} %bitcast.101), custom_call_target="tpu_custom_call" | custom-call | bytes 120000000 | tf_op jit(solution)/shard_map/team_sum/pallas_call | solution.py:429
  259.8 10.5 %back_second.1 = (bf16[4,16,4,2048]{3,2,1,0:T(4,128)(2,1)}, f32[4,64,2048]{2,1,0:T(8,128)}, bf16[64,2048]{1,0:T(8,128)(2,1)}, f32[8,2048]{1,0:T(8,128)}, f32[4,8]{1,0:T(4,128)}) custom-call(f32[4,64,2048]{2,1,0:T(8,128)} %get-tuple-element.69.middle, bf16[4,64,2048]{2,1,0:T(8,128)(2,1)} %get-tuple-element.70.top, f32[64,2048]{1,0:T(8,128)} %get-tuple-element.78.branch_out, ...), custom_call_target="tpu_custom_call" | custom-call | bytes 15000000 | tf_op jit(solution)/shard_map/back_second/pallas_call | solution.py:1204
  270.3 21.9 %team_gather.3 = bf16[4,2,64,2048]{3,2,1,0:T(8,128)(2,1)} custom-call(bf16[64,2048]{1,0:T(8,128)(2,1)} %get-tuple-element.86.refs_0_), custom_call_target="tpu_custom_call" | custom-call | bytes 60000000 | tf_op jit(solution)/shard_map/team_gather/pallas_call | solution.py:186
  292.2 60.5 %attend_back.1 = (bf16[2048,1024]{1,0:T(8,128)(2,1)}, f32[64,2048]{1,0:T(8,128)}, bf16[4,128,1536]{2,1,0:T(8,128)(2,1)}) custom-call(bf16[512,2048]{1,0:T(8,128)(2,1)} %bitcast.93, bf16[512,2048]{1,0:T(8,128)(2,1)} %bitcast.95, bf16[2048,768]{1,0:T(8,128)(2,1)} %get-tuple-element.65.qkv_ref, bf16[256,2048]{1,0:T(8,128)(2,1)} %get-tuple-element.66.out_ref, ...), custom_call_target="tpu_custom_call" | custom-call | bytes 150000000 | tf_op jit(solution)/shard_map/attend_back/pallas_call | solution.py:964
  354.2 9.8 %back_first.1 = (bf16[4,16,4,2048]{3,2,1,0:T(4,128)(2,1)}, f32[8,2048]{1,0:T(8,128)}, f32[4,8]{1,0:T(4,128)}) custom-call(bf16[4,64,2048]{2,1,0:T(8,128)(2,1)} %bitcast.92, f32[4,64,2048]{2,1,0:T(8,128)} %get-tuple-element.85.top, f32[64,2048]{1,0:T(8,128)} %team_sum.2.branch_out, f32[64,2048]{1,0:T(8,128)} %get-tuple-element.92.grad_in, ...), custom_call_target="tpu_custom_call" | custom-call | bytes 15000000 | tf_op jit(solution)/shard_map/back_first/pallas_call | solution.py:1204
  363.9 0.9 pad_maximum_fusion
  365.0 0.7 pad_maximum_fusion.1
  365.8 0.7 select_maximum_fusion.refs_2_
  366.5 46.3 %close_team.1 = (bf16[4,16,4,2048]{3,2,1,0:T(4,128)(2,1)}, bf16[4,16,4,2048]{3,2,1,0:T(4,128)(2,1)}, f32[12,2,2048]{2,1,0:T(2,128)}, bf16[4,128,1536]{2,1,0:T(8,128)(2,1)}) custom-call(bf16[4,16,4,2048]{3,2,1,0:T(4,128)(2,1)} %get-tuple-element.84.refs_0_.own_a, bf16[4,16,4,2048]{3,2,1,0:T(4,128)(2,1)} %get-tuple-element.93.refs_1_.own_b, ...), custom_call_target="tpu_custom_call" | custom-call | bytes 180000000 | tf_op jit(solution)/shard_map/close_team/pallas_call | solution.py:680
  412.8 7.6 %place_all.1 = (bf16[4,2,16,4,2048]{4,3,2,1,0:T(4,128)(2,1)}, bf16[4,2,16,4,2048]{4,3,2,1,0:T(4,128)(2,1)}, f32[128,4096]{1,0:T(8,128)}, f32[128,4096]{1,0:T(8,128)}, f32[4096,128]{1,0:T(8,128)}) custom-call(s32[1]{0:T(128)} %bitcast.where, bf16[4,16,4,2048]{3,2,1,0:T(4,128)(2,1)} %get-tuple-element.84.refs_0_.own_a, ...), custom_call_target="tpu_custom_call" | custom-call | bytes 21000000 | tf_op jit(solution)/shard_map/place_all/pallas_call | solution.py:518
  421.1 26.7 %team_rows.1.attn = bf16[4,128,1024]{2,1,0:T(8,128)(2,1)} custom-call(bf16[512,1024]{1,0:T(8,128)(2,1)} %reduce-scatter.8.cloned.1.call-done.summed), custom_call_target="tpu_custom_call" | custom-call | bytes 60000000 | tf_op jit(solution)/shard_map/team_rows/pallas_call | solution.py:575
  447.9 3.6 place_attn.1
  (75 shorter events, 11.2 us)
Async XLA Ops:
  7.2 1.6 copy-start
  7.2 175.7 %all-gather.2.cloned.1.call-start = ((), (), s32[]{:S(2)}) async-start(), calls=%async_computation.4 | async-start | bytes 15728640 | tf_op jit(solution)/shard_map/all_gather | solution.py:1295
  11.0 4.0 copy-start.2
  11.0 2.0 copy-start.4
  11.0 2.0 copy-start.7
  15.3 1.6 copy-start.10
  59.6 12.7 %copy-start.11 = (s32[1,4]{1,0:T(1,128)S(1)}, s32[1,4]{1,0:T(1,128)}, u32[]{:S(2)}) copy-start(s32[1,4]{1,0:T(1,128)} %param.15) | copy-start | bytes 52
  59.6 14.4 %copy-start.9 = (f32[64]{0:T(128)S(1)}, f32[64]{0:T(128)}, u32[]{:S(2)}) copy-start(f32[64]{0:T(128)} %constant.173) | copy-start | bytes 772
  64.8 70.7 %all-to-all-start = ((bf16[4,4,16,2048]{3,2,1,0:T(8,128)(2,1)}), bf16[4,4,16,2048]{3,2,1,0:T(8,128)(2,1)S(1)}, u32[]{:S(2)}, u32[]{:S(2)}) async-start(bf16[4,4,16,2048]{3,2,1,0:T(8,128)(2,1)} %pack_runs.1), calls=%async_computation | async-start | bytes 2097152 | tf_op jit(solution)/shard_map/all_to_all | solution.py:1299
  72.1 220.1 %reduce-scatter.4.cloned.1.call-start = ((), (), s32[]{:S(2)}) async-start(), calls=%async_computation.5 | async-start | bytes 7864320 | tf_op jit(solution)/shard_map/reduce_scatter | solution.py:1346
  135.4 1.0 copy-start.3
  216.8 149.7 %reduce-scatter.6.cloned.1.call-start = ((), (), s32[]{:S(2)}) async-start(), calls=%async_computation.6 | async-start | bytes 7864320 | tf_op jit(solution)/shard_map/reduce_scatter | solution.py:1346
  217.5 202.9 %reduce-scatter.8.cloned.1.call-start = ((), (), s32[]{:S(2)}) async-start(), calls=%async_computation.7 | async-start | bytes 5242880 | tf_op jit(solution)/shard_map/reduce_scatter | solution.py:1346
  354.2 9.8 %copy-start.5 = (f32[8,2048]{1,0:T(8,128)S(1)}, f32[8,2048]{1,0:T(8,128)}, u32[]{:S(2)}) copy-start(f32[8,2048]{1,0:T(8,128)} %get-tuple-element.95) | copy-start | bytes 196612
  354.2 10.8 %copy-start.8 = (f32[4,8]{1,0:T(4,128)S(1)}, f32[4,8]{1,0:T(4,128)}, u32[]{:S(2)}) copy-start(f32[4,8]{1,0:T(4,128)} %get-tuple-element.97) | copy-start | bytes 388
  412.8 7.7 %copy-start.6 = (f32[12,2,2048]{2,1,0:T(2,128)S(1)}, f32[12,2,2048]{2,1,0:T(2,128)}, u32[]{:S(2)}) copy-start(f32[12,2,2048]{2,1,0:T(2,128)} %get-tuple-element.116) | copy-start | bytes 589828
  412.8 39.3 %copy-start.1 = (bf16[128,4,2048]{2,1,0:T(4,128)(2,1)S(1)}, bf16[128,4,2048]{2,1,0:T(4,128)(2,1)}, u32[]{:S(2)}) copy-start(bf16[128,4,2048]{2,1,0:T(4,128)(2,1)} %param.14) | copy-start | bytes 6291460
Sparse Core Ops, SparseCore 0:
  58.4 124.4 all-gather.1
  216.9 70.5 reduce-scatter.3
  290.6 70.1 reduce-scatter.5
  363.6 53.7 reduce-scatter.7

commit v7 on v6

--- a/solution.py
+++ b/solution.py
@@ -861,7 +861,7 @@
 
 
 def attend_kernel(
-    u_ref, qkv_ref, out_ref, turns, placing, placed, y_ref, q_ref, k_ref, v_ref, o_ref
+    u_ref, qkv_ref, out_ref, turns, placing, placed, y_low, y_high, q_ref, k_ref, v_ref, o_ref
 ):
     count = q_ref.shape[1]
     u = u_ref[...]
@@ -880,9 +880,13 @@
         v_ref[:, head] = value
         probs = head_probs(query, key, placing[...], placed[...])
         o_ref[:, head] = dot(probs.astype(jnp.bfloat16), value).astype(jnp.bfloat16)
-    width = y_ref.shape[1]
-    for start in range(0, width, 512):
-        y_ref[:, start : start + 512] = dot(o_ref[...], out_ref[:, start : start + 512])
+    half = y_low.shape[1]
+    for start in range(0, half, 512):
+        y_low[:, start : start + 512] = dot(o_ref[...], out_ref[:, start : start + 512])
+    for start in range(0, half, 512):
+        y_high[:, start : start + 512] = dot(
+            o_ref[...], out_ref[:, half + start : half + start + 512]
+        )
 
 
 def attend(u, qkv, out_w, turns, placing, placed):
@@ -890,9 +894,9 @@
     low = jax.ShapeDtypeStruct((total, count), jnp.bfloat16)
     return pl.pallas_call(
         attend_kernel,
-        out_shape=[jax.ShapeDtypeStruct((total, out_w.shape[1]), jnp.float32)] + [low] * 4,
+        out_shape=[jax.ShapeDtypeStruct((total, out_w.shape[1] // 2), jnp.float32)] * 2 + [low] * 4,
         in_specs=[INSIDE] * 6,
-        out_specs=[INSIDE] * 5,
+        out_specs=[INSIDE] * 6,
         compiler_params=pltpu.CompilerParams(vmem_limit_bytes=60 << 20),
         cost_estimate=cost(12),
         name="attend",
@@ -1297,10 +1301,10 @@
     sent = jnp.sum(jnp.where(every // rows_here == here, every % rows_here, 0), 1) // part + core
     packed = pack_runs(cotangent, sent, part)
     arrived = lax.all_to_all(packed, "ctx", split_axis=0, concat_axis=0, tiled=True)
-    attn_part, queries, keys, values, attended = attend(
+    *attn_parts, queries, keys, values, attended = attend(
         attn_input, qkv, out_w, turns, placing, placed
     )
-    [attn_out] = team_sum(1, attn_part)
+    attn_out = jnp.concatenate(team_sum(1, *attn_parts), 1)
 
     (
         middle,

time: 466 us -> 466 us (level)
  Pallas kernels: 411 us -> 406 us
    pallas_call x2, Pallas kernels: 88.3 us -> 83.3 us  [team_sum(): pl.pallas_call(functools.partial(scatter_kernel, amount, owners, cores),...]
  transfers between devices with their start and end apart: 5 -> 5, of which waited for: 1 -> 1; matrix products, arithmetic and copies ran while one was open for 3% -> 3% of each run, Pallas kernels for 67% -> 65%
where the time goes in v7:
time: 466 us; the launch traced here: 459 us
  Pallas kernels  406 us (87%)
  between operations  14.6 us (3%)
  local copies, waits for them, and re-layouts  13.1 us (3%)
  other arithmetic  11.2 us (2%)
  starting transfers between devices  7.63 us (2%)
  waiting for transfers between devices  4.86 us (1%)
    pallas_call x2, Pallas kernels, team_sum(): pl.pallas_call(functools.partial(scatter_kernel, amount, owners, cores),...  83.3 us
    pallas_call x1, Pallas kernels, attend_back(): pl.pallas_call(functools.partial(attend_back_kernel, owners, cores), out_...  61.1 us
    pallas_call x2, Pallas kernels, team_gather(): pl.pallas_call(functools.partial(gather_kernel, amount, owners, cores), o...  58.2 us
    pallas_call x1, Pallas kernels, close_team(): pl.pallas_call(functools.partial(close_kernel, amount, shards_in, owners,...  45.8 us
    pallas_call x1, Pallas kernels, open_team(): pl.pallas_call(functools.partial(open_kernel, shards_in, owners, cores),...  40.6 us
    pallas_call x1, Pallas kernels, ffn(): pl.pallas_call(ffn_kernel, grid=(blocks,), in_specs=[whole, whole, pl.Blo...  33.8 us
    pallas_call x3, Pallas kernels, token_call(): pl.pallas_call(kernel, grid_spec=pltpu.PrefetchScalarGridSpec(num_scalar_...  29.1 us
    pallas_call x1, Pallas kernels, team_rows(): pl.pallas_call(functools.partial(swap_kernel_alone, owners), out_shape=ja...  27.4 us
  transfers between devices with their start and end apart: 5, of which 1 were waited for; matrix products, arithmetic and copies ran while one was open for 3% of the time, Pallas kernels for 65%

profile of v7, /device:TPU:8, one launch (start us, length us, event | category | flops | bytes accessed | tf_op | source)
XLA Modules:
  0.0 459.5 jit_solution(9236814196309687495)
XLA Ops:
  7.2 1.5 copy-done
  9.2 1.1 convert_reduce_fusion
  11.0 1.2 fusion.2
  12.2 0.7 fusion
  13.1 1.8 broadcast_add_fusion.1
  15.8 1.0 fusion.50
  17.6 40.6 %open_team.1 = (bf16[4,2,64,2048]{3,2,1,0:T(8,128)(2,1)}, bf16[2048,768]{1,0:T(8,128)(2,1)}, bf16[256,2048]{1,0:T(8,128)(2,1)}, bf16[512,3072]{1,0:T(8,128)(2,1)}, s32[4,8,128]{2,1,0:T(8,128)}) custom-call(bf16[64,2048]{1,0:T(8,128)(2,1)} %get-tuple-element.127.refs_0_, bf16[512,1024]{1,0:T(8,128)(2,1)} %refs_1_.1, bf16[512,1024]{1,0:T(8,128)(2,1)} %refs_2_.1, ...), custom_call_target="tpu_custom_call" | custom-call | bytes 120000000 | tf_op jit(solution)/shard_map/open_team/pallas_call | solution.py:308
  58.3 0.7 slice.66
  59.6 5.1 %pack_runs.1 = bf16[4,4,16,2048]{3,2,1,0:T(8,128)(2,1)} custom-call(s32[4]{0:T(128)} %fusion.48.sent, bf16[128,4,2048]{2,1,0:T(4,128)(2,1)} %value.1), custom_call_target="tpu_custom_call" | custom-call | bytes 6000000 | tf_op jit(solution)/shard_map/pack_runs/pallas_call | solution.py:833
  64.8 7.3 %all-to-all-start = ((bf16[4,4,16,2048]{3,2,1,0:T(8,128)(2,1)}), bf16[4,4,16,2048]{3,2,1,0:T(8,128)(2,1)S(1)}, u32[]{:S(2)}, u32[]{:S(2)}) async-start(bf16[4,4,16,2048]{3,2,1,0:T(8,128)(2,1)} %pack_runs.1), calls=%async_computation | async-start | bytes 2097152 | tf_op jit(solution)/shard_map/all_to_all | solution.py:1303
  73.2 0.9 copy.53.placing
  74.0 1.0 multiply_cosine_fusion
  75.2 0.8 maximum_bitcast_fusion.turns
  76.1 10.6 %attend.1 = (f32[512,1024]{1,0:T(8,128)}, f32[512,1024]{1,0:T(8,128)}, bf16[512,256]{1,0:T(8,128)(2,1)}, bf16[512,256]{1,0:T(8,128)(2,1)}, bf16[512,256]{1,0:T(8,128)(2,1)}, /*index=5*/bf16[512,256]{1,0:T(8,128)(2,1)}) custom-call(bf16[512,2048]{1,0:T(8,128)(2,1)} %bitcast.95, bf16[2048,768]{1,0:T(8,128)(2,1)} %get-tuple-element.68.qkv_ref, ...), custom_call_target="tpu_custom_call" | custom-call | bytes 36000000 | tf_op jit(solution)/shard_map/attend/pallas_call | solution.py:895
  86.7 41.6 %team_sum.2 = (f32[64,1024]{1,0:T(8,128)}, f32[64,1024]{1,0:T(8,128)}) custom-call(f32[4,2,64,1024]{3,2,1,0:T(8,128)} %bitcast.102, f32[4,2,64,1024]{3,2,1,0:T(8,128)} %bitcast.103), custom_call_target="tpu_custom_call" | custom-call | bytes 120000000 | tf_op jit(solution)/shard_map/team_sum/pallas_call | solution.py:429
  129.6 1.0 constant_dynamic-update-slice_fusion.1
  130.6 1.0 constant_dynamic-update-slice_fusion.branch_out
  132.8 1.0 copy-done.3
  133.8 8.9 %mix_second.1 = (f32[4,64,2048]{2,1,0:T(8,128)}, bf16[64,2048]{1,0:T(8,128)(2,1)}, bf16[64,2048]{1,0:T(8,128)(2,1)}, f32[64,2048]{1,0:T(8,128)}, f32[64,8]{1,0:T...) custom-call(s32[4]{0:T(128)} %and_select_fusion.13.source, ...), custom_call_target="tpu_custom_call" | custom-call | bytes 15000000 | tf_op jit(solution)/shard_map/mix_second/pallas_call | solution.py:1208
  142.6 36.1 %team_gather.2 = (bf16[4,2,64,2048]{3,2,1,0:T(8,128)(2,1)}, bf16[4,2,64,2048]{3,2,1,0:T(8,128)(2,1)}) custom-call(bf16[64,2048]{1,0:T(8,128)(2,1)} %get-tuple-element.77.refs_0_, bf16[64,2048]{1,0:T(8,128)(2,1)} %get-tuple-element.78.refs_1_), custom_call_target="tpu_custom_call" | custom-call | bytes 120000000 | tf_op jit(solution)/shard_map/team_gather/pallas_call | solution.py:186
  178.8 4.1 all-gather.2.cloned.1.call-done.gate_ref.up_ref
  182.9 33.8 %ffn.1 = (bf16[512,2048]{1,0:T(8,128)(2,1)}, bf16[512,2048]{1,0:T(8,128)(2,1)}, bf16[2048,1536]{1,0:T(8,128)(2,1)}, bf16[2048,1536]{1,0:T(8,128)(2,1)}) custom-call(bf16[512,2048]{1,0:T(8,128)(2,1)} %bitcast.98, bf16[512,2048]{1,0:T(8,128)(2,1)} %bitcast.99, bf16[2048,3072]{1,0:T(8,128)(2,1)} %all-gather.2.cloned.1.call-done.gate_ref.up_ref, ...), custom_call_target="tpu_custom_call" | custom-call | bytes 90000000 | tf_op jit(solution)/shard_map/ffn/pallas_call | solution.py:792
  217.5 41.7 %team_sum.3 = (f32[64,2048]{1,0:T(8,128)}, f32[64,2048]{1,0:T(8,128)}) custom-call(bf16[4,2,64,2048]{3,2,1,0:T(8,128)(2,1)} %bitcast.100, bf16[4,2,64,2048]{3,2,1,0:T(8,128)(2,1)} %bitcast.101), custom_call_target="tpu_custom_call" | custom-call | bytes 120000000 | tf_op jit(solution)/shard_map/team_sum/pallas_call | solution.py:429
  259.2 10.5 %back_second.1 = (bf16[4,16,4,2048]{3,2,1,0:T(4,128)(2,1)}, f32[4,64,2048]{2,1,0:T(8,128)}, bf16[64,2048]{1,0:T(8,128)(2,1)}, f32[8,2048]{1,0:T(8,128)}, f32[4,8]{1,0:T(4,128)}) custom-call(f32[4,64,2048]{2,1,0:T(8,128)} %get-tuple-element.75.middle, bf16[4,64,2048]{2,1,0:T(8,128)(2,1)} %get-tuple-element.76.top, f32[64,2048]{1,0:T(8,128)} %get-tuple-element.84.branch_out, ...), custom_call_target="tpu_custom_call" | custom-call | bytes 15000000 | tf_op jit(solution)/shard_map/back_second/pallas_call | solution.py:1208
  269.7 22.0 %team_gather.3 = bf16[4,2,64,2048]{3,2,1,0:T(8,128)(2,1)} custom-call(bf16[64,2048]{1,0:T(8,128)(2,1)} %get-tuple-element.92.refs_0_), custom_call_target="tpu_custom_call" | custom-call | bytes 60000000 | tf_op jit(solution)/shard_map/team_gather/pallas_call | solution.py:186
  291.8 61.1 %attend_back.1 = (bf16[2048,1024]{1,0:T(8,128)(2,1)}, f32[64,2048]{1,0:T(8,128)}, bf16[4,128,1536]{2,1,0:T(8,128)(2,1)}) custom-call(bf16[512,2048]{1,0:T(8,128)(2,1)} %bitcast.94, bf16[512,2048]{1,0:T(8,128)(2,1)} %bitcast.96, bf16[2048,768]{1,0:T(8,128)(2,1)} %get-tuple-element.68.qkv_ref, bf16[256,2048]{1,0:T(8,128)(2,1)} %get-tuple-element.69.out_ref, ...), custom_call_target="tpu_custom_call" | custom-call | bytes 150000000 | tf_op jit(solution)/shard_map/attend_back/pallas_call | solution.py:968
  354.3 9.8 %back_first.1 = (bf16[4,16,4,2048]{3,2,1,0:T(4,128)(2,1)}, f32[8,2048]{1,0:T(8,128)}, f32[4,8]{1,0:T(4,128)}) custom-call(bf16[4,64,2048]{2,1,0:T(8,128)(2,1)} %bitcast.93, f32[4,64,2048]{2,1,0:T(8,128)} %get-tuple-element.91.top, f32[64,2048]{1,0:T(8,128)} %copy-done.4, f32[64,2048]{1,0:T(8,128)} %get-tuple-element.98.grad_in, ...), custom_call_target="tpu_custom_call" | custom-call | bytes 15000000 | tf_op jit(solution)/shard_map/back_first/pallas_call | solution.py:1208
  364.1 0.9 pad_maximum_fusion
  366.6 45.8 %close_team.1 = (bf16[4,16,4,2048]{3,2,1,0:T(4,128)(2,1)}, bf16[4,16,4,2048]{3,2,1,0:T(4,128)(2,1)}, f32[12,2,2048]{2,1,0:T(2,128)}, bf16[4,128,1536]{2,1,0:T(8,128)(2,1)}) custom-call(bf16[4,16,4,2048]{3,2,1,0:T(4,128)(2,1)} %get-tuple-element.90.refs_0_.own_a, bf16[4,16,4,2048]{3,2,1,0:T(4,128)(2,1)} %get-tuple-element.99.refs_1_.own_b, ...), custom_call_target="tpu_custom_call" | custom-call | bytes 180000000 | tf_op jit(solution)/shard_map/close_team/pallas_call | solution.py:680
  412.5 7.7 %place_all.1 = (bf16[4,2,16,4,2048]{4,3,2,1,0:T(4,128)(2,1)}, bf16[4,2,16,4,2048]{4,3,2,1,0:T(4,128)(2,1)}, f32[128,4096]{1,0:T(8,128)}, f32[128,4096]{1,0:T(8,128)}, f32[4096,128]{1,0:T(8,128)}) custom-call(s32[1]{0:T(128)} %bitcast.where, bf16[4,16,4,2048]{3,2,1,0:T(4,128)(2,1)} %get-tuple-element.90.refs_0_.own_a, ...), custom_call_target="tpu_custom_call" | custom-call | bytes 21000000 | tf_op jit(solution)/shard_map/place_all/pallas_call | solution.py:518
  420.8 27.4 %team_rows.1.attn = bf16[4,128,1024]{2,1,0:T(8,128)(2,1)} custom-call(bf16[512,1024]{1,0:T(8,128)(2,1)} %reduce-scatter.8.cloned.1.call-done.summed), custom_call_target="tpu_custom_call" | custom-call | bytes 60000000 | tf_op jit(solution)/shard_map/team_rows/pallas_call | solution.py:575
  448.2 3.6 place_attn.1
  (79 shorter events, 12.6 us)
Async XLA Ops:
  7.2 1.6 copy-start
  7.2 175.7 %all-gather.2.cloned.1.call-start = ((), (), s32[]{:S(2)}) async-start(), calls=%async_computation.4 | async-start | bytes 15728640 | tf_op jit(solution)/shard_map/all_gather | solution.py:1299
  11.0 4.0 copy-start.2
  11.0 2.0 copy-start.5
  11.0 2.0 copy-start.8
  15.3 1.6 copy-start.11
  59.6 12.7 %copy-start.12 = (s32[1,4]{1,0:T(1,128)S(1)}, s32[1,4]{1,0:T(1,128)}, u32[]{:S(2)}) copy-start(s32[1,4]{1,0:T(1,128)} %param.15) | copy-start | bytes 52
  59.6 14.4 %copy-start.10 = (f32[64]{0:T(128)S(1)}, f32[64]{0:T(128)}, u32[]{:S(2)}) copy-start(f32[64]{0:T(128)} %constant.173) | copy-start | bytes 772
  64.8 68.1 %all-to-all-start = ((bf16[4,4,16,2048]{3,2,1,0:T(8,128)(2,1)}), bf16[4,4,16,2048]{3,2,1,0:T(8,128)(2,1)S(1)}, u32[]{:S(2)}, u32[]{:S(2)}) async-start(bf16[4,4,16,2048]{3,2,1,0:T(8,128)(2,1)} %pack_runs.1), calls=%async_computation | async-start | bytes 2097152 | tf_op jit(solution)/shard_map/all_to_all | solution.py:1303
  72.1 219.7 %reduce-scatter.4.cloned.1.call-start = ((), (), s32[]{:S(2)}) async-start(), calls=%async_computation.5 | async-start | bytes 7864320 | tf_op jit(solution)/shard_map/reduce_scatter | solution.py:1350
  131.6 1.3 copy-start.4
  132.8 1.0 copy-start.3
  216.7 149.9 %reduce-scatter.6.cloned.1.call-start = ((), (), s32[]{:S(2)}) async-start(), calls=%async_computation.6 | async-start | bytes 7864320 | tf_op jit(solution)/shard_map/reduce_scatter | solution.py:1350
  217.5 202.7 %reduce-scatter.8.cloned.1.call-start = ((), (), s32[]{:S(2)}) async-start(), calls=%async_computation.7 | async-start | bytes 5242880 | tf_op jit(solution)/shard_map/reduce_scatter | solution.py:1350
  354.3 9.8 %copy-start.6 = (f32[8,2048]{1,0:T(8,128)S(1)}, f32[8,2048]{1,0:T(8,128)}, u32[]{:S(2)}) copy-start(f32[8,2048]{1,0:T(8,128)} %get-tuple-element.101) | copy-start | bytes 196612
  354.3 10.8 %copy-start.9 = (f32[4,8]{1,0:T(4,128)S(1)}, f32[4,8]{1,0:T(4,128)}, u32[]{:S(2)}) copy-start(f32[4,8]{1,0:T(4,128)} %get-tuple-element.103) | copy-start | bytes 388
  412.4 7.7 %copy-start.7 = (f32[12,2,2048]{2,1,0:T(2,128)S(1)}, f32[12,2,2048]{2,1,0:T(2,128)}, u32[]{:S(2)}) copy-start(f32[12,2,2048]{2,1,0:T(2,128)} %get-tuple-element.122) | copy-start | bytes 589828
  412.5 40.0 %copy-start.1 = (bf16[128,4,2048]{2,1,0:T(4,128)(2,1)S(1)}, bf16[128,4,2048]{2,1,0:T(4,128)(2,1)}, u32[]{:S(2)}) copy-start(bf16[128,4,2048]{2,1,0:T(4,128)(2,1)} %param.14) | copy-start | bytes 6291460
Sparse Core Ops, SparseCore 0:
  58.4 124.4 all-gather.1
  216.9 70.2 reduce-scatter.3
  290.1 70.1 reduce-scatter.5
  363.1 53.7 reduce-scatter.7
